TPU v7x, 512 devices: a whole 4x8x8 slice. The times are simulated.
512 devices in a mesh: prow: 32 (over x, y), pcol: 16 (over z, core).
Axes of the slice: x: 4, y: 8, z: 8, core: 2. Of those that a mesh axis runs over, the one named last changes fastest.
Arguments:
- matrix: bfloat16 [24576, 24576], P('prow', 'pcol'), as said below
- row_pattern: int32 [2, 96], replicated, may hold values from 0 to 1, as said below
- col_pattern: int32 [2, 96], replicated, may hold values from 0 to 1, as said below
Outputs:
- factored: bfloat16 [24576, 24576], P('prow', 'pcol')
Inputs may be any that keep to these rules, and one draw needn't show every extreme that they name: 1 where panel k's block column holds nonzeros in block row I, else 0. For each panel, at most 2 of the 3 block rows of any one index of prow are 1, and exactly 2 for some index. row_pattern[1, I] = 1 wherever row_pattern[0, I] = 1. Entries (0, 0) and (1, 3) are 1 and entry (0, 3) is 0. `col_pattern`: 1 where panel k's block row holds nonzeros in block column J, else 0. For each panel, at most 4 of the 6 block columns of any one index of pcol are 1, and exactly 4 for some index. Entries (0, 0), (0, 6) and (1, 6) are 1. `matrix`: in the two pivot blocks (r_k, c_k) every diagonal entry is positive and exceeds the sum of the magnitudes of the other entries of its row by at least one twelfth of itself.
All inputs are finite; a program needn't handle non-finite values.
Results may differ from a plain program's by a relative error of at most 0.0034.
Values may be sent and summed in bfloat16 or wider, within the bound.
No kernel may reach another device: no remote copies, remote signals or barrier semaphores. Data moves between devices by JAX's collectives and lax.ppermute only.
A program may use at most 64 MiB of HBM per device.

v0:
```python
import jax
import jax.numpy as jnp
from jax import lax
from jax.sharding import Mesh
from jax.sharding import PartitionSpec as P

BLK = 256
PROW = ("prow_0", "prow_1")


newton_steps = 8


def from_root(shard, axes, root):
    shard = jnp.where(lax.axis_index(axes) == root, shard, jnp.zeros_like(shard))
    for axis in axes:
        shard = lax.psum(shard, axis)
    return shard


def from_root_2(shard, axis, root):
    return lax.dynamic_index_in_dim(lax.all_gather(shard, axis), root, 0, keepdims=False)


def inverse_of(pivot_block):
    identity = jnp.eye(pivot_block.shape[0], dtype=jnp.float32)
    approx = identity / jnp.diagonal(pivot_block)[:, None]
    for sweep_no in range(newton_steps):
        product = jnp.dot(approx, pivot_block, precision=lax.Precision.HIGHEST)
        approx = jnp.dot(2.0 * identity - product, approx, precision=lax.Precision.HIGHEST)
    return approx


def shards(matrix, row_pattern, col_pattern):
    row_index = lax.axis_index(PROW)
    col_index = lax.axis_index("pcol")
    height, breadth = matrix.shape
    row_blocks = height // BLK
    col_blocks = breadth // BLK
    row_first = jnp.arange(height) < BLK
    col_first = jnp.arange(breadth) < BLK
    rows_here = lax.dynamic_slice_in_dim(row_pattern, row_index * row_blocks, row_blocks, 1)
    cols_here = lax.dynamic_slice_in_dim(col_pattern, col_index * col_blocks, col_blocks, 1)
    row_keep = jnp.repeat(rows_here, BLK, axis=1) > 0
    col_keep = jnp.repeat(cols_here, BLK, axis=1) > 0
    zero_value = jnp.zeros((), matrix.dtype)
    dropped = jnp.zeros((height, breadth), dtype=jnp.bool_)
    for panel_no in range(2):
        dropped = (
            dropped | (col_index == panel_no) & col_first[None, :] & ~row_keep[panel_no][:, None]
        )
        dropped = (
            dropped | (row_index == panel_no) & row_first[:, None] & ~col_keep[panel_no][None, :]
        )
    current = jnp.where(dropped, zero_value, matrix)
    identity = jnp.eye(BLK, dtype=jnp.float32)

    def send_row(source_rows, panel_no):
        return from_root(source_rows, PROW, panel_no)

    def send_lower(factor, panel_no):
        return from_root_2(factor, "pcol", panel_no)

    def prologue(source, panel_no):
        row_done = row_first & (row_index <= panel_no)
        col_done = col_first & (col_index <= panel_no)
        received = send_row(source[:BLK], panel_no)
        at_pivot = (row_index == panel_no) & (col_index == panel_no)
        inverse = inverse_of(jnp.where(at_pivot, source[:BLK, :BLK].astype(jnp.float32), identity))
        inverse = from_root_2(inverse, PROW, panel_no)
        factor = jnp.dot(
            source[:, :BLK].astype(jnp.float32), inverse, precision=lax.Precision.HIGHEST
        )
        factor = jnp.where(row_done[:, None], 0.0, factor).astype(jnp.bfloat16)
        lower_part = send_lower(factor, panel_no)
        upper_part = jnp.where(col_done[None, :], zero_value, received)
        filled = (col_index == panel_no) & ~row_done
        return (lower_part, upper_part, filled)

    def update(source, lower_rows, upper_cols, filled_rows, first_column):
        product = jnp.dot(lower_rows, upper_cols, preferred_element_type=jnp.float32)
        updated = (source.astype(jnp.float32) - product).astype(jnp.bfloat16)
        if first_column:
            updated = updated.at[:, :BLK].set(
                jnp.where(filled_rows[:, None], lower_rows, updated[:, :BLK])
            )
        return updated

    lower_part, upper_part, filled = prologue(current, 0)
    head_rows = update(current[:BLK], lower_part[:BLK], upper_part, filled[:BLK], True)
    left_cols = update(
        current[BLK:, :BLK], lower_part[BLK:], upper_part[:, :BLK], filled[BLK:], True
    )
    edge_done = jnp.concatenate(
        [head_rows, jnp.concatenate([left_cols, current[BLK:, BLK:]], axis=1)], axis=0
    )
    lower_next, upper_next, filled_next = prologue(edge_done, 1)
    interior = update(
        current[BLK:, BLK:], lower_part[BLK:], upper_part[:, BLK:], filled[BLK:], False
    )
    current = jnp.concatenate([head_rows, jnp.concatenate([left_cols, interior], axis=1)], axis=0)
    return update(current, lower_next, upper_next, filled_next, True)


def solution(mesh):
    torus = Mesh(mesh.devices.reshape(4, 8, mesh.shape["pcol"]), ("prow_0", "prow_1", "pcol"))
    placed = (P(PROW, "pcol"), P(), P())
    return jax.shard_map(
        shards, mesh=torus, in_specs=placed, out_specs=P(PROW, "pcol"), check_vma=False
    )
```

profile of v0, /device:TPU:1, one launch (start us, length us, event | category | flops | bytes accessed | tf_op | source)
XLA Modules:
  0.0 371.5 jit_solution(16891882686550617831)
XLA Ops:
  7.4 0.8 dynamic-slice_compare_fusion.1
  8.2 0.8 dynamic-slice_compare_fusion
  9.3 3.5 or_select_fusion
  12.7 0.9 broadcast_select_fusion.1
  13.8 2.3 gather_fusion
  16.2 0.4 select_subtract_fusion.15
  16.6 0.5 fusion.16
  22.3 1.1 fusion.63
  23.4 49.3 %all-reduce.5.cloned.1.call-done = bf16[256,1536]{1,0:T(8,128)(2,1)} async-done(((bf16[256,1536]{1,0:T(8,128)(2,1)}), bf16[256,1536]{1,0:T(8,128)(2,1)}) %all-reduce.5.cloned.1.call-update) | async-done | bytes 786448 | tf_op jit(solution)/shard_map/psum | solution.py:17
  72.8 62.7 %all-gather.9.cloned.1.call-done = f32[8192,256]{1,0:T(8,128)} async-done(((f32[256,256]{1,0:T(8,128)}), f32[8192,256]{1,0:T(8,128)}) %all-gather.9.cloned.1.call-update) | async-done | bytes 8388624 | tf_op jit(solution)/shard_map/all_gather | solution.py:22
  135.5 2.2 fusion.2
  138.0 0.6 compare_reduce_fusion
  138.6 33.9 %all-reduce.7.cloned.1.call-done = bf16[256,1536]{1,0:T(8,128)(2,1)} async-done(((bf16[256,1536]{1,0:T(8,128)(2,1)}), bf16[256,1536]{1,0:T(8,128)(2,1)}) %all-reduce.7.cloned.1.call-update) | async-done | bytes 786448 | tf_op jit(solution)/shard_map/psum | solution.py:17
  172.5 2.1 broadcast_select_fusion.2
  174.6 12.1 %all-gather.11.cloned.1.call-done = bf16[12288,256]{1,0:T(8,128)(2,1)} async-done(((bf16[768,256]{1,0:T(8,128)(2,1)}), bf16[12288,256]{1,0:T(8,128)(2,1)}) %all-gather.11.cloned.1.call-update) | async-done | bytes 6291472 | tf_op jit(solution)/shard_map/all_gather | solution.py:22
  186.7 1.6 fusion.1
  188.3 1.6 convert_select_fusion
  189.9 2.3 gather_fusion.1
  192.3 0.4 select_subtract_fusion.7
  192.7 0.5 fusion.17
  197.2 0.9 broadcast_select_fusion
  199.4 1.1 fusion.70
  200.6 48.7 %all-reduce.9.cloned.1.call-done = bf16[256,1536]{1,0:T(8,128)(2,1)} async-done(((bf16[256,1536]{1,0:T(8,128)(2,1)}), bf16[256,1536]{1,0:T(8,128)(2,1)}) %all-reduce.9.cloned.1.call-update) | async-done | bytes 786448 | tf_op jit(solution)/shard_map/psum | solution.py:17
  249.4 1.1 slice.165
  250.5 1.3 fusion.5
  251.9 54.5 %all-gather.13.cloned.1.call-done = f32[8192,256]{1,0:T(8,128)} async-done(((f32[256,256]{1,0:T(8,128)}), f32[8192,256]{1,0:T(8,128)}) %all-gather.13.cloned.1.call-update) | async-done | bytes 8388624 | tf_op jit(solution)/shard_map/all_gather | solution.py:22
  306.4 2.2 fusion.3
  308.7 2.7 fusion
  311.4 36.5 %all-reduce.11.cloned.1.call-done = bf16[256,1536]{1,0:T(8,128)(2,1)} async-done(((bf16[256,1536]{1,0:T(8,128)(2,1)}), bf16[256,1536]{1,0:T(8,128)(2,1)}) %all-reduce.11.cloned.1.call-update) | async-done | bytes 786448 | tf_op jit(solution)/shard_map/psum | solution.py:17
  347.9 9.5 %all-gather.15.cloned.1.call-done = bf16[12288,256]{1,0:T(8,128)(2,1)} async-done(((bf16[768,256]{1,0:T(8,128)(2,1)}), bf16[12288,256]{1,0:T(8,128)(2,1)}) %all-gather.15.cloned.1.call-update) | async-done | bytes 6291472 | tf_op jit(solution)/shard_map/all_gather | solution.py:22
  357.4 3.9 %subtract_convert_fusion = bf16[768,1536]{1,0:T(8,128)(2,1)} fusion(bf16[512,1280]{1,0:T(8,128)(2,1)} %fusion, bf16[512,256]{1,0:T(8,128)(2,1)S(1)} %fusion.5, bf16[256,1536]{1,0:T(8,128)(2,1)S(1)} %constant_dynamic-update-slice_fusion, bf16[256,1536]{1,0:T(8,128)(2,1)} %all-reduce.11.cloned.1.call-done, pred[1536]{0:T(1024)(128)(4,1)S(1)} %fusion.39, ...), kind=kOutput, calls=%fused_computation.2 | convolution fusion | flops 613810176 | bytes 5899776 | tf_op jit(solution)/shard_map/dot_general | solution.py:81
  361.3 2.8 fusion.9
  (65 shorter events, 11.3 us)
Async XLA Ops:
  7.4 65.4 %all-reduce.5.cloned.1.call-start = ((), (), s32[]{:S(2)}) async-start(), calls=%async_computation | async-start | bytes 1572864 | tf_op jit(solution)/shard_map/psum | solution.py:17
  13.7 121.8 %all-gather.9.cloned.1.call-start = ((), (), s32[]{:S(2)}) async-start(), calls=%async_computation.4 | async-start | bytes 8650752 | tf_op jit(solution)/shard_map/all_gather | solution.py:22
  23.4 149.1 %all-reduce.7.cloned.1.call-start = ((), (), s32[]{:S(2)}) async-start(), calls=%async_computation.1 | async-start | bytes 1572864 | tf_op jit(solution)/shard_map/psum | solution.py:17
  72.8 114.0 %all-gather.11.cloned.1.call-start = ((), (), s32[]{:S(2)}) async-start(), calls=%async_computation.5 | async-start | bytes 6684672 | tf_op jit(solution)/shard_map/all_gather | solution.py:22
  137.7 111.6 %all-reduce.9.cloned.1.call-start = ((), (), s32[]{:S(2)}) async-start(), calls=%async_computation.2 | async-start | bytes 1572864 | tf_op jit(solution)/shard_map/psum | solution.py:17
  198.2 108.2 %all-gather.13.cloned.1.call-start = ((), (), s32[]{:S(2)}) async-start(), calls=%async_computation.6 | async-start | bytes 8650752 | tf_op jit(solution)/shard_map/all_gather | solution.py:22
  200.5 147.4 %all-reduce.11.cloned.1.call-start = ((), (), s32[]{:S(2)}) async-start(), calls=%async_computation.3 | async-start | bytes 1572864 | tf_op jit(solution)/shard_map/psum | solution.py:17
  249.3 108.1 %all-gather.15.cloned.1.call-start = ((), (), s32[]{:S(2)}) async-start(), calls=%async_computation.7 | async-start | bytes 6684672 | tf_op jit(solution)/shard_map/all_gather | solution.py:22
Sparse Core Ops, SparseCore 0:
  13.8 58.8 all-reduce.4
  75.1 97.3 all-reduce.6
  198.3 50.9 all-reduce.8
  251.5 96.3 all-reduce.10
Sparse Core Ops, SparseCore 1:
  23.5 112.0 all-gather.8
  137.8 48.9 all-gather.10
  201.8 104.5 all-gather.12
  308.7 48.7 all-gather.14
where the time goes:
time: 372 us; the launch traced here: 371 us
  waiting for transfers between devices  307 us (83%)
  matrix products  28.1 us (8%)
  between operations  15.2 us (4%)
  other arithmetic  14.1 us (4%)
  local copies, waits for them, and re-layouts  6.21 us (2%)
    psum x4, waiting for transfers between devices, from_root(): shard = lax.psum(shard, axis)  168 us
    all_gather x4, waiting for transfers between devices, from_root_2(): lax.all_gather(shard, axis)  139 us
    dot_general x4, matrix products, update(): jnp.dot(lower_rows, upper_cols, preferred_element_type=jnp.float32)  9.54 us
    dot_general x16, matrix products, inverse_of(): jnp.dot(2.0 * identity - product, approx, precision=lax.Precision.HIGHEST)  7.67 us
  transfers between devices with their start and end apart: 8, of which 8 were waited for; matrix products, arithmetic and copies ran while one was open for 7% of the time, Pallas kernels for 0%

commit v1 on v0

v1 whole, which is shorter than its diff:
```python
import jax
import jax.numpy as jnp
from jax import lax
from jax.experimental import pallas as pl
from jax.experimental.pallas import tpu as pltpu
from jax.sharding import Mesh
from jax.sharding import PartitionSpec as P

BLK = 256
X, Y, Z = 4, 8, 8
AXES = ("prow_0", "prow_1", "pcol")
PROW = ("prow_0", "prow_1")
ROW_CAP, COL_CAP = 2, 4


def device(x, y, z, core):
    return ((x % X) * Y + y % Y) * (2 * Z) + (z % Z) * 2 + core


def plane_pairs(pairs):
    out = []
    for (xs, ys), (xt, yt) in pairs:
        for z in range(Z):
            for core in range(2):
                out.append((device(xs, ys, z, core), device(xt, yt, z, core)))
                out.append((device(xs, 1 - ys, z, core), device(xt, 1 - yt, z, core)))
    return out


def line_pairs(pairs):
    return [
        (device(x, y, s, core), device(x, y, t, core))
        for s, t in pairs
        for x in range(X)
        for y in range(Y)
        for core in range(2)
    ]


HOLDERS = [(0, 0), (2, 0), (1, 4), (3, 4)]
SPREAD_1 = [plane_pairs([((0, 0), h)]) for h in ((3, 4), (1, 4), (2, 0))]
SPREAD_2 = [
    plane_pairs([(h, (h[0] + dx, h[1] + dy)) for h in HOLDERS])
    for dx, dy in ((-1, 2), (0, 2), (1, 0))
]
UP = [
    (device(x, y, z, c), device(x, y + 1, z, c))
    for x in range(X) for y in range(Y) for z in range(Z) for c in range(2)
]
DOWN = [(t, s) for s, t in UP]
LINE_1 = [line_pairs([(0, 3)]), line_pairs([(0, 5)])]
LINE_2 = [line_pairs([(0, 1), (3, 4), (5, 6)]), line_pairs([(0, 7), (3, 2)])]
SWAP = [
    (device(x, y, z, c), device(x, y, z, 1 - c))
    for x in range(X) for y in range(Y) for z in range(Z) for c in range(2)
]


def send(value, pairs):
    return lax.ppermute(value, AXES, pairs)


def slots(flags, capacity):
    count = jnp.int32(0)
    slot_of = []
    where = [jnp.int32(0)] * capacity
    for position, flag in enumerate(flags):
        one = flag.astype(jnp.int32)
        slot_of.append(jnp.minimum(count, capacity - 1))
        where = [
            jnp.where(flag & (count == s), jnp.int32(position), w) for s, w in enumerate(where)
        ]
        count = count + one
    return slot_of, where, count


def pack_kernel(here, row_pattern, col_pattern, matrix, first_out, rest_out, panel_out, sems):
    prow, pcol = here[0], here[1]
    row_blocks, col_blocks = matrix.shape[0] // BLK, matrix.shape[1] // BLK
    k = (prow == 1).astype(jnp.int32)
    cols = [col_pattern[k, pcol * col_blocks + j] > 0 for j in range(col_blocks)]
    _, col_at, _ = slots(cols, COL_CAP)
    copies = []
    for s in range(COL_CAP):
        source = matrix.at[pl.ds(0, BLK), pl.ds(pl.multiple_of(col_at[s] * BLK, BLK), BLK)]
        target = first_out if s == 0 else rest_out.at[pl.ds((s - 1) * BLK, BLK)]
        copies.append(pltpu.make_async_copy(source, target, sems.at[s]))
    rows = [row_pattern[1, prow * row_blocks + i] > 0 for i in range(row_blocks)]
    _, row_at, count = slots(rows, ROW_CAP)
    for s in range(ROW_CAP):
        source = matrix.at[pl.ds(pl.multiple_of(row_at[s] * BLK, BLK), BLK), pl.ds(0, BLK)]
        target = panel_out.at[pl.ds(s * BLK, BLK)]
        copies.append(pltpu.make_async_copy(source, target, sems.at[COL_CAP + s]))
    for copy in copies:
        copy.start()
    for copy in copies:
        copy.wait()
    own = (pcol == 1).astype(jnp.int32)
    for s in range(ROW_CAP):
        stored = (count > s) & (row_pattern[own, prow * row_blocks + row_at[s]] > 0)

        @pl.when(jnp.logical_not(stored))
        def _(s=s):
            panel_out[pl.ds(s * BLK, BLK), :] = jnp.zeros((BLK, BLK), jnp.bfloat16)


def pack(here, row_pattern, col_pattern, matrix):
    smem = pl.BlockSpec(memory_space=pltpu.SMEM)
    vmem = pl.BlockSpec(memory_space=pltpu.VMEM)
    return pl.pallas_call(
        pack_kernel,
        in_specs=[smem, smem, smem, pl.BlockSpec(memory_space=pl.ANY)],
        out_specs=[vmem] * 3,
        out_shape=[
            jax.ShapeDtypeStruct((BLK, BLK), jnp.bfloat16),
            jax.ShapeDtypeStruct(((COL_CAP - 1) * BLK, BLK), jnp.bfloat16),
            jax.ShapeDtypeStruct((ROW_CAP * BLK, BLK), jnp.bfloat16),
        ],
        scratch_shapes=[pltpu.SemaphoreType.DMA((COL_CAP + ROW_CAP,))],
        name="pack",
    )(here, row_pattern, col_pattern, matrix)


def halves(value):
    high = value.astype(jnp.bfloat16)
    return high, (value - high.astype(jnp.float32)).astype(jnp.bfloat16)


def dot(a, b):
    return jnp.dot(a, b, preferred_element_type=jnp.float32)


def panels_kernel(
    here, row_pattern, pivot_0, upper_01, pivot_1, panel_0, panel_1, lower_0, lower_1
):
    prow = here[0]
    row_blocks = row_pattern.shape[1] // (X * Y)
    i = lax.broadcasted_iota(jnp.int32, (BLK, BLK), 0)
    j = lax.broadcasted_iota(jnp.int32, (BLK, BLK), 1)
    diagonal = i == j
    powers, sums, scales = [], [], []
    for pivot in (pivot_0, pivot_1):
        p = pivot[...].astype(jnp.float32)
        d = jnp.where(diagonal, p, 0.0)
        by_row = jnp.sum(d, axis=1, keepdims=True)
        scales.append(1.0 / jnp.sum(d, axis=0, keepdims=True))
        r = jnp.where(diagonal, 0.0, -p / by_row)
        powers.append(r)
        sums.append(jnp.where(diagonal, 1.0, r))
    for step in range(8):
        for n in range(2):
            high, low = halves(powers[n])
            if step > 0:
                sum_high, sum_low = halves(sums[n])
                sums[n] = sums[n] + (
                    dot(high, sum_high) + (dot(high, sum_low) + dot(low, sum_high))
                )
            if step < 7:
                powers[n] = dot(high, high) + (dot(high, low) + dot(low, high))
    rows = [row_pattern[1, prow * row_blocks + b] > 0 for b in range(row_blocks)]
    _, row_at, _ = slots(rows, ROW_CAP)
    for n in range(2):
        inverse = sums[n] * scales[n]
        high, low = halves(inverse)
        for s in range(ROW_CAP):
            here_rows = pl.ds(s * BLK, BLK)
            if n == 0:
                source = panel_0[here_rows, :]
                done = (prow == 0) & (row_at[s] == 0)
            else:
                source = (
                    panel_1[here_rows, :].astype(jnp.float32)
                    - dot(lower_0[here_rows, :], upper_01[...])
                ).astype(jnp.bfloat16)
                done = (prow <= 1) & (row_at[s] == 0)
            lower = dot(source, high) + dot(source, low)
            target = lower_0 if n == 0 else lower_1
            target[here_rows, :] = jnp.where(done, 0.0, lower).astype(jnp.bfloat16)


def panels(here, row_pattern, *blocks):
    smem = pl.BlockSpec(memory_space=pltpu.SMEM)
    vmem = pl.BlockSpec(memory_space=pltpu.VMEM)
    shape = jax.ShapeDtypeStruct((ROW_CAP * BLK, BLK), jnp.bfloat16)
    return pl.pallas_call(
        panels_kernel,
        in_specs=[smem, smem] + [vmem] * 5,
        out_specs=[vmem] * 2,
        out_shape=[shape, shape],
        name="panels",
    )(here, row_pattern, *blocks)


def update_kernel(
    here, row_pattern, col_pattern, source, lower_0, lower_1, first_0, rest_0, first_1, rest_1, out
):
    prow, pcol = here[0], here[1]
    i = pl.program_id(0)
    row_blocks = pl.num_programs(0)
    col_blocks = source.shape[1] // BLK
    row = prow * row_blocks + i
    slot = jnp.int32(0)
    for b in range(2):
        slot = slot + ((i > b) & (row_pattern[1, prow * row_blocks + b] > 0)).astype(jnp.int32)
    slot = jnp.minimum(slot, ROW_CAP - 1)
    stored = [row_pattern[k, row] > 0 for k in range(2)]
    first = i == 0
    done = [first & (prow == 0), first & (prow <= 1)]
    rows = pl.ds(pl.multiple_of(slot * BLK, BLK), BLK)
    lower = [lower_0[rows, :], lower_1[rows, :]]
    upper = [(first_0, rest_0), (first_1, rest_1)]
    flags = [[col_pattern[k, pcol * col_blocks + j] > 0 for j in range(col_blocks)] for k in (0, 1)]
    col_slot = [slots(f, COL_CAP)[0] for f in flags]
    for j in range(col_blocks):
        columns = pl.ds(j * BLK, BLK)
        dropped = jnp.bool_(False)
        for k in range(2):
            dropped = dropped | (first & (prow == k) & jnp.logical_not(flags[k][j]))
            if j == 0:
                dropped = dropped | ((pcol == k) & jnp.logical_not(stored[k]))
        value = jnp.where(dropped, 0.0, source[:, columns].astype(jnp.float32))
        for k in range(2):
            used = stored[k] & jnp.logical_not(done[k]) & flags[k][j]
            if j == 0:
                used = used & (pcol > k)
            s = col_slot[k][j]
            if j == 0:
                block = upper[k][0][...]
            else:
                at = pl.ds(pl.multiple_of(jnp.maximum(s - 1, 0) * BLK, BLK), BLK)
                block = jnp.where(s == 0, upper[k][0][...], upper[k][1][at, :])
            product = jnp.where(used, dot(lower[k], block), 0.0)
            value = (value - product).astype(jnp.bfloat16)
            if j == 0:
                taken = (pcol == k) & jnp.logical_not(done[k])
                kept = jnp.where(stored[k], lower[k], jnp.zeros_like(lower[k]))
                value = jnp.where(taken, kept, value)
            if k == 0:
                value = value.astype(jnp.float32)
        out[:, columns] = value


def update(here, row_pattern, col_pattern, matrix, *blocks):
    row_blocks = matrix.shape[0] // BLK
    breadth = matrix.shape[1]
    smem = pl.BlockSpec(memory_space=pltpu.SMEM)
    vmem = pl.BlockSpec(memory_space=pltpu.VMEM)
    strip = pl.BlockSpec((BLK, breadth), lambda i: (i, 0))
    return pl.pallas_call(
        update_kernel,
        grid=(row_blocks,),
        in_specs=[smem] * 3 + [strip] + [vmem] * 6,
        out_specs=strip,
        out_shape=jax.ShapeDtypeStruct(matrix.shape, matrix.dtype),
        name="update",
    )(here, row_pattern, col_pattern, matrix, *blocks)


def shards(matrix, row_pattern, col_pattern):
    prow = lax.axis_index(PROW).astype(jnp.int32)
    pcol = lax.axis_index("pcol").astype(jnp.int32)
    y = lax.axis_index("prow_1")
    here = jnp.where(jnp.arange(2) == 0, prow, pcol)
    even = y % 2 == 0
    core_0 = pcol % 2 == 0
    first, rest, panel = pack(here, row_pattern, col_pattern, matrix)
    zero = jnp.zeros((), jnp.bfloat16)

    def only(flag, value):
        return jnp.where(flag, value, zero)

    def spread(value):
        held = only(prow <= 1, value)
        for pairs in SPREAD_1:
            held = held + send(value, pairs)
        every = held
        for pairs in SPREAD_2:
            every = every + send(held, pairs)
        return every

    def along(value):
        held = only(pcol <= 1, value)
        for pairs in LINE_1:
            held = held + send(value, pairs)
        every = held
        for pairs in LINE_2:
            every = every + send(held, pairs)
        return every, send(every, SWAP)

    first_held = spread(first)
    first_came = send(first_held, UP)
    first_0 = jnp.where(even, first_held, first_came)
    first_1 = jnp.where(even, first_came, first_held)
    mine, other = along(panel)
    panel_0 = jnp.where(core_0, mine, other)
    panel_1 = jnp.where(core_0, other, mine)
    mine, other = along(jnp.concatenate([first_0, first_1], axis=0))
    pivot_0 = jnp.where(core_0, mine[:BLK], other[:BLK])
    upper_01 = jnp.where(core_0, other[:BLK], mine[:BLK])
    pivot_1 = jnp.where(core_0, other[BLK:], mine[BLK:])
    rest_held = spread(rest)
    half = rest.shape[0] // 2
    rest_came = jnp.concatenate(
        [send(rest_held[:half], UP), send(rest_held[half:], DOWN)],
        axis=0,
    )
    rest_0 = jnp.where(even, rest_held, rest_came)
    rest_1 = jnp.where(even, rest_came, rest_held)
    lower_0, lower_1 = panels(here, row_pattern, pivot_0, upper_01, pivot_1, panel_0, panel_1)
    return update(
        here, row_pattern, col_pattern, matrix,
        lower_0, lower_1, first_0, rest_0, first_1, rest_1,
    )


def solution(mesh):
    torus = Mesh(mesh.devices.reshape(X, Y, mesh.shape["pcol"]), AXES)
    placed = (P(PROW, "pcol"), P(), P())
    return jax.shard_map(
        shards, mesh=torus, in_specs=placed, out_specs=P(PROW, "pcol"), check_vma=False
    )
```

time: 372 us -> 124 us (0.33)
  the two profiles are of different devices: /device:TPU:1 before, /device:TPU:4 now
where the time goes in v1:
time: 124 us; the launch traced here: 123 us
  starting transfers between devices  56.9 us (46%)
  waiting for transfers between devices  47.3 us (38%)
  Pallas kernels  13.9 us (11%)
  other arithmetic  4.53 us (4%)
    ppermute x25, starting transfers between devices, send(): return lax.ppermute(value, AXES, pairs)  56.9 us
    ppermute x25, waiting for transfers between devices, send(): return lax.ppermute(value, AXES, pairs)  47.3 us
    pallas_call x1, Pallas kernels, panels(): pl.pallas_call(panels_kernel, in_specs=[smem, smem] + [vmem] * 5, out_spe...  5.69 us
    pallas_call x1, Pallas kernels, update(): pl.pallas_call(update_kernel, grid=(row_blocks,), in_specs=[smem] * 3 + [...  5.31 us
    pallas_call x1, Pallas kernels, pack(): pl.pallas_call(pack_kernel, in_specs=[smem, smem, smem, pl.BlockSpec(memo...  2.89 us
  transfers between devices with their start and end apart: 25, of which 8 were waited for; matrix products, arithmetic and copies ran while one was open for 3% of the time, Pallas kernels for 0%

profile of v1, /device:TPU:4, one launch (start us, length us, event | category | flops | bytes accessed | tf_op | source)
XLA Modules:
  0.0 123.2 jit_solution(5260517029872075033)
XLA Ops:
  0.5 2.9 %pack.1 = (bf16[256,256]{1,0:T(8,128)(2,1)}, bf16[768,256]{1,0:T(8,128)(2,1)}, bf16[512,256]{1,0:T(8,128)(2,1)}) custom-call(s32[2]{0:T(128)} %compare_select_fusion.here, s32[2,96]{1,0:T(2,128)} %row_pattern.5, s32[2,96]{1,0:T(2,128)} %col_pattern.3, bf16[768,1536]{1,0:T(8,128)(2,1)} %source.1), custom_call_target="tpu_custom_call" | custom-call | tf_op jit(solution)/shard_map/pack/pallas_call | solution.py:110
  3.4 1.4 %collective-permute-start.2 = (bf16[256,256]{1,0:T(8,128)(2,1)}, bf16[256,256]{1,0:T(8,128)(2,1)S(1)}, u32[]{:S(2)}, u32[]{:S(2)}) collective-permute-start(bf16[256,256]{1,0:T(8,128)(2,1)} %get-tuple-element.10), channel_id=1, source_target_pairs={{0,256},{16,272},{1,257},{17,273},{2,258},{18,274},{3,259},{19,275... | collective-permute-start | bytes 393224 | tf_op jit(solution)/shard_map/ppermute | solution.py:60
  6.2 7.7 %collective-permute-done.2 = bf16[256,256]{1,0:T(8,128)(2,1)S(1)} collective-permute-done((bf16[256,256]{1,0:T(8,128)(2,1)}, bf16[256,256]{1,0:T(8,128)(2,1)S(1)}, u32[]{:S(2)}, u32[]{:S(2)}) %collective-permute-start.2) | collective-permute-done | bytes 131104 | tf_op jit(solution)/shard_map/ppermute | solution.py:60
  13.9 1.3 %collective-permute-start.5 = (bf16[256,256]{1,0:T(8,128)(2,1)S(1)}, bf16[256,256]{1,0:T(8,128)(2,1)S(1)}, u32[]{:S(2)}, u32[]{:S(2)}) collective-permute-start(bf16[256,256]{1,0:T(8,128)(2,1)S(1)} %add_add_fusion.7), channel_id=1, source_target_pairs={{0,128},{16,144},{1,129},{17,145},{2,130},{18,146},{3,131},{19,147... | collective-permute-start | bytes 393224 | tf_op jit(solution)/shard_map/ppermute | solution.py:60
  15.2 1.3 %collective-permute-start.4 = (bf16[256,256]{1,0:T(8,128)(2,1)S(1)}, bf16[256,256]{1,0:T(8,128)(2,1)S(1)}, u32[]{:S(2)}, u32[]{:S(2)}) collective-permute-start(bf16[256,256]{1,0:T(8,128)(2,1)S(1)} %add_add_fusion.7), channel_id=1, source_target_pairs={{0,32},{16,112},{1,33},{17,113},{2,34},{18,114},{3,35},{19,115},{4... | collective-permute-start | bytes 393224 | tf_op jit(solution)/shard_map/ppermute | solution.py:60
  16.5 1.3 %collective-permute-start.3 = (bf16[256,256]{1,0:T(8,128)(2,1)S(1)}, bf16[256,256]{1,0:T(8,128)(2,1)S(1)}, u32[]{:S(2)}, u32[]{:S(2)}) collective-permute-start(bf16[256,256]{1,0:T(8,128)(2,1)S(1)} %add_add_fusion.7), channel_id=1, source_target_pairs={{0,416},{16,496},{1,417},{17,497},{2,418},{18,498},{3,419},{19,499... | collective-permute-start | bytes 393224 | tf_op jit(solution)/shard_map/ppermute | solution.py:60
  17.8 9.5 %collective-permute-start.13 = (bf16[512,256]{1,0:T(8,128)(2,1)}, bf16[512,256]{1,0:T(8,128)(2,1)S(1)}, u32[]{:S(2)}, u32[]{:S(2)}) collective-permute-start(bf16[512,256]{1,0:T(8,128)(2,1)} %get-tuple-element.11), channel_id=1, source_target_pairs={{0,10},{1,11},{16,26},{17,27},{32,42},{33,43},{48,58},{49,59},{64,... | collective-permute-start | bytes 786440 | tf_op jit(solution)/shard_map/ppermute | solution.py:60
  27.3 1.3 %collective-permute-start.12 = (bf16[512,256]{1,0:T(8,128)(2,1)}, bf16[512,256]{1,0:T(8,128)(2,1)S(1)}, u32[]{:S(2)}, u32[]{:S(2)}) collective-permute-start(bf16[512,256]{1,0:T(8,128)(2,1)} %get-tuple-element.11), channel_id=1, source_target_pairs={{0,6},{1,7},{16,22},{17,23},{32,38},{33,39},{48,54},{49,55},{64,70... | collective-permute-start | bytes 786440 | tf_op jit(solution)/shard_map/ppermute | solution.py:60
  28.7 1.3 %collective-permute-start.19 = (bf16[768,256]{1,0:T(8,128)(2,1)}, bf16[768,256]{1,0:T(8,128)(2,1)S(1)}, u32[]{:S(2)}, u32[]{:S(2)}) collective-permute-start(bf16[768,256]{1,0:T(8,128)(2,1)} %get-tuple-element.14), channel_id=1, source_target_pairs={{0,256},{16,272},{1,257},{17,273},{2,258},{18,274},{3,259},{19,275... | collective-permute-start | bytes 1179656 | tf_op jit(solution)/shard_map/ppermute | solution.py:60
  32.3 3.5 %collective-permute-start.6 = (bf16[256,256]{1,0:T(8,128)(2,1)S(1)}, bf16[256,256]{1,0:T(8,128)(2,1)S(1)}, u32[]{:S(2)}, u32[]{:S(2)}) collective-permute-start(bf16[256,256]{1,0:T(8,128)(2,1)S(1)} %add_add_fusion.6), channel_id=1, source_target_pairs={{0,16},{1,17},{2,18},{3,19},{4,20},{5,21},{6,22},{7,23},{8,24},{9,... | collective-permute-start | bytes 393224 | tf_op jit(solution)/shard_map/ppermute | solution.py:60
  35.8 1.0 add_add_fusion.3
  36.8 1.3 %collective-permute-start.15 = (bf16[512,256]{1,0:T(8,128)(2,1)S(1)}, bf16[512,256]{1,0:T(8,128)(2,1)S(1)}, u32[]{:S(2)}, u32[]{:S(2)}) collective-permute-start(bf16[512,256]{1,0:T(8,128)(2,1)S(1)} %add_add_fusion.3), channel_id=1, source_target_pairs={{0,14},{1,15},{16,30},{17,31},{32,46},{33,47},{48,62},{49,63},{64,... | collective-permute-start | bytes 786440 | tf_op jit(solution)/shard_map/ppermute | solution.py:60
  38.1 2.3 %collective-permute-done.6 = bf16[256,256]{1,0:T(8,128)(2,1)S(1)} collective-permute-done((bf16[256,256]{1,0:T(8,128)(2,1)S(1)}, bf16[256,256]{1,0:T(8,128)(2,1)S(1)}, u32[]{:S(2)}, u32[]{:S(2)}) %collective-permute-start.6) | collective-permute-done | bytes 131104 | tf_op jit(solution)/shard_map/ppermute | solution.py:60
  40.4 1.3 %collective-permute-start.14 = (bf16[512,256]{1,0:T(8,128)(2,1)S(1)}, bf16[512,256]{1,0:T(8,128)(2,1)S(1)}, u32[]{:S(2)}, u32[]{:S(2)}) collective-permute-start(bf16[512,256]{1,0:T(8,128)(2,1)S(1)} %add_add_fusion.3), channel_id=1, source_target_pairs={{0,2},{1,3},{16,18},{17,19},{32,34},{33,35},{48,50},{49,51},{64,66... | collective-permute-start | bytes 786440 | tf_op jit(solution)/shard_map/ppermute | solution.py:60
  42.0 3.2 %collective-permute-start.7 = (bf16[512,256]{1,0:T(8,128)(2,1)S(1)}, bf16[512,256]{1,0:T(8,128)(2,1)S(1)}, u32[]{:S(2)}, u32[]{:S(2)}) collective-permute-start(bf16[512,256]{1,0:T(8,128)(2,1)S(1)} %pad_maximum_fusion), channel_id=1, source_target_pairs={{0,6},{1,7},{16,22},{17,23},{32,38},{33,39},{48,54},{49,55},{64,70... | collective-permute-start | bytes 786440 | tf_op jit(solution)/shard_map/ppermute | solution.py:60
  45.2 3.1 %collective-permute-done.14 = bf16[512,256]{1,0:T(8,128)(2,1)S(1)} collective-permute-done((bf16[512,256]{1,0:T(8,128)(2,1)S(1)}, bf16[512,256]{1,0:T(8,128)(2,1)S(1)}, u32[]{:S(2)}, u32[]{:S(2)}) %collective-permute-start.14) | collective-permute-done | bytes 262176 | tf_op jit(solution)/shard_map/ppermute | solution.py:60
  48.2 4.6 %collective-permute-start.8 = (bf16[512,256]{1,0:T(8,128)(2,1)S(1)}, bf16[512,256]{1,0:T(8,128)(2,1)S(1)}, u32[]{:S(2)}, u32[]{:S(2)}) collective-permute-start(bf16[512,256]{1,0:T(8,128)(2,1)S(1)} %pad_maximum_fusion), channel_id=1, source_target_pairs={{0,10},{1,11},{16,26},{17,27},{32,42},{33,43},{48,58},{49,59},{64,... | collective-permute-start | bytes 786440 | tf_op jit(solution)/shard_map/ppermute | solution.py:60
  52.9 1.9 %collective-permute-start.16 = (bf16[512,256]{1,0:T(8,128)(2,1)S(1)}, bf16[512,256]{1,0:T(8,128)(2,1)S(1)}, u32[]{:S(2)}, u32[]{:S(2)}) collective-permute-start(bf16[512,256]{1,0:T(8,128)(2,1)S(1)} %add_add_fusion.2), channel_id=1, source_target_pairs={{0,1},{1,0},{2,3},{3,2},{4,5},{5,4},{6,7},{7,6},{8,9},{9,8},{10,11... | collective-permute-start | bytes 786440 | tf_op jit(solution)/shard_map/ppermute | solution.py:60
  54.9 5.3 %collective-permute-start.22 = (bf16[768,256]{1,0:T(8,128)(2,1)S(1)}, bf16[768,256]{1,0:T(8,128)(2,1)S(1)}, u32[]{:S(2)}, u32[]{:S(2)}) collective-permute-start(bf16[768,256]{1,0:T(8,128)(2,1)S(1)} %add_add_fusion.1), channel_id=1, source_target_pairs={{0,128},{16,144},{1,129},{17,145},{2,130},{18,146},{3,131},{19,147... | collective-permute-start | bytes 1179656 | tf_op jit(solution)/shard_map/ppermute | solution.py:60
  60.3 3.0 %collective-permute-start.21 = (bf16[768,256]{1,0:T(8,128)(2,1)S(1)}, bf16[768,256]{1,0:T(8,128)(2,1)S(1)}, u32[]{:S(2)}, u32[]{:S(2)}) collective-permute-start(bf16[768,256]{1,0:T(8,128)(2,1)S(1)} %add_add_fusion.1), channel_id=1, source_target_pairs={{0,32},{16,112},{1,33},{17,113},{2,34},{18,114},{3,35},{19,115},{4... | collective-permute-start | bytes 1179656 | tf_op jit(solution)/shard_map/ppermute | solution.py:60
  63.2 1.3 %collective-permute-start.20 = (bf16[768,256]{1,0:T(8,128)(2,1)S(1)}, bf16[768,256]{1,0:T(8,128)(2,1)S(1)}, u32[]{:S(2)}, u32[]{:S(2)}) collective-permute-start(bf16[768,256]{1,0:T(8,128)(2,1)S(1)} %add_add_fusion.1), channel_id=1, source_target_pairs={{0,416},{16,496},{1,417},{17,497},{2,418},{18,498},{3,419},{19,499... | collective-permute-start | bytes 1179656 | tf_op jit(solution)/shard_map/ppermute | solution.py:60
  64.7 1.3 %collective-permute-start.10 = (bf16[512,256]{1,0:T(8,128)(2,1)S(1)}, bf16[512,256]{1,0:T(8,128)(2,1)S(1)}, u32[]{:S(2)}, u32[]{:S(2)}) collective-permute-start(bf16[512,256]{1,0:T(8,128)(2,1)S(1)} %add_add_fusion.5), channel_id=1, source_target_pairs={{0,14},{1,15},{16,30},{17,31},{32,46},{33,47},{48,62},{49,63},{64,... | collective-permute-start | bytes 786440 | tf_op jit(solution)/shard_map/ppermute | solution.py:60
  66.0 2.4 %collective-permute-start.9 = (bf16[512,256]{1,0:T(8,128)(2,1)S(1)}, bf16[512,256]{1,0:T(8,128)(2,1)S(1)}, u32[]{:S(2)}, u32[]{:S(2)}) collective-permute-start(bf16[512,256]{1,0:T(8,128)(2,1)S(1)} %add_add_fusion.5), channel_id=1, source_target_pairs={{0,2},{1,3},{16,18},{17,19},{32,34},{33,35},{48,50},{49,51},{64,66... | collective-permute-start | bytes 786440 | tf_op jit(solution)/shard_map/ppermute | solution.py:60
  69.3 3.4 %collective-permute-done.21 = bf16[768,256]{1,0:T(8,128)(2,1)S(1)} collective-permute-done((bf16[768,256]{1,0:T(8,128)(2,1)S(1)}, bf16[768,256]{1,0:T(8,128)(2,1)S(1)}, u32[]{:S(2)}, u32[]{:S(2)}) %collective-permute-start.21) | collective-permute-done | bytes 393248 | tf_op jit(solution)/shard_map/ppermute | solution.py:60
  72.7 8.0 %collective-permute-done.20 = bf16[768,256]{1,0:T(8,128)(2,1)S(1)} collective-permute-done((bf16[768,256]{1,0:T(8,128)(2,1)S(1)}, bf16[768,256]{1,0:T(8,128)(2,1)S(1)}, u32[]{:S(2)}, u32[]{:S(2)}) %collective-permute-start.20) | collective-permute-done | bytes 393248 | tf_op jit(solution)/shard_map/ppermute | solution.py:60
  80.8 1.9 %collective-permute-start.24 = (bf16[384,256]{1,0:T(8,128)(2,1)S(1)}, bf16[384,256]{1,0:T(8,128)(2,1)S(1)}, u32[]{:S(2)}, u32[]{:S(2)}) collective-permute-start(bf16[384,256]{1,0:T(8,128)(2,1)S(1)} %get-tuple-element.22), channel_id=1, source_target_pairs={{16,0},{17,1},{18,2},{19,3},{20,4},{21,5},{22,6},{23,7},{24,8},{25... | collective-permute-start | bytes 589832 | tf_op jit(solution)/shard_map/ppermute | solution.py:60
  82.7 3.9 %collective-permute-start.23 = (bf16[384,256]{1,0:T(8,128)(2,1)S(1)}, bf16[384,256]{1,0:T(8,128)(2,1)S(1)}, u32[]{:S(2)}, u32[]{:S(2)}) collective-permute-start(bf16[384,256]{1,0:T(8,128)(2,1)S(1)} %get-tuple-element.23), channel_id=1, source_target_pairs={{0,16},{1,17},{2,18},{3,19},{4,20},{5,21},{6,22},{7,23},{8,24},{9,... | collective-permute-start | bytes 589832 | tf_op jit(solution)/shard_map/ppermute | solution.py:60
  86.7 1.9 %collective-permute-start.11 = (bf16[512,256]{1,0:T(8,128)(2,1)S(1)}, bf16[512,256]{1,0:T(8,128)(2,1)S(1)}, u32[]{:S(2)}, u32[]{:S(2)}) collective-permute-start(bf16[512,256]{1,0:T(8,128)(2,1)S(1)} %add_add_fusion.4), channel_id=1, source_target_pairs={{0,1},{1,0},{2,3},{3,2},{4,5},{5,4},{6,7},{7,6},{8,9},{9,8},{10,11... | collective-permute-start | bytes 786440 | tf_op jit(solution)/shard_map/ppermute | solution.py:60
  88.6 21.8 %collective-permute-done.23 = bf16[384,256]{1,0:T(8,128)(2,1)S(1)} collective-permute-done((bf16[384,256]{1,0:T(8,128)(2,1)S(1)}, bf16[384,256]{1,0:T(8,128)(2,1)S(1)}, u32[]{:S(2)}, u32[]{:S(2)}) %collective-permute-start.23) | collective-permute-done | bytes 196640 | tf_op jit(solution)/shard_map/ppermute | solution.py:60
  110.4 1.0 broadcast_select_fusion
  112.2 5.7 %panels.1 = (bf16[512,256]{1,0:T(8,128)(2,1)}, bf16[512,256]{1,0:T(8,128)(2,1)}) custom-call(s32[2]{0:T(128)} %compare_select_fusion.here, s32[2,96]{1,0:T(2,128)} %row_pattern.5, bf16[256,256]{1,0:T(8,128)(2,1)} %get-tuple-element.21.pivot_0, bf16[256,256]{1,0:T(8,128)(2,1)} %get-tuple-element.20.upper_01, bf16[256,256]{1,0:T(8,128)(2,1)} %get-tuple-element.19.pivot_1, ...), custom_call_target="tpu_custom_call" | custom-call | tf_op jit(solution)/shard_map/panels/pallas_call | solution.py:185
  117.9 5.3 %update.1 = bf16[768,1536]{1,0:T(8,128)(2,1)} custom-call(s32[2]{0:T(128)} %compare_select_fusion.here, s32[2,96]{1,0:T(2,128)} %row_pattern.5, s32[2,96]{1,0:T(2,128)} %col_pattern.3, bf16[768,1536]{1,0:T(8,128)(2,1)} %source.1, bf16[512,256]{1,0:T(8,128)(2,1)} %get-tuple-element.12.lower_0, bf16[512,256]{1,0:T(8,128)(2,1)} %get-tuple-element.13.lower_1, ...), custom_call_target="tpu_custom_call" | custom-call | tf_op jit(solution)/shard_map/update/pallas_call | solution.py:249
  (44 shorter events, 6.5 us)
Async XLA Ops:
  3.4 51.4 %copy-start.2 = (bf16[768,256]{1,0:T(8,128)(2,1)S(1)}, bf16[768,256]{1,0:T(8,128)(2,1)}, u32[]{:S(2)}) copy-start(bf16[768,256]{1,0:T(8,128)(2,1)} %get-tuple-element.14) | copy-start | bytes 1179652
  3.4 10.4 %collective-permute-start.2 = (bf16[256,256]{1,0:T(8,128)(2,1)}, bf16[256,256]{1,0:T(8,128)(2,1)S(1)}, u32[]{:S(2)}, u32[]{:S(2)}) collective-permute-start(bf16[256,256]{1,0:T(8,128)(2,1)} %get-tuple-element.10), channel_id=1, source_target_pairs={{0,256},{16,272},{1,257},{17,273},{2,258},{18,274},{3,259},{19,275... | collective-permute-start | bytes 393224 | tf_op jit(solution)/shard_map/ppermute | solution.py:60
  4.9 9.0 %collective-permute-start.1 = (bf16[256,256]{1,0:T(8,128)(2,1)}, bf16[256,256]{1,0:T(8,128)(2,1)S(1)}, u32[]{:S(2)}, u32[]{:S(2)}) collective-permute-start(bf16[256,256]{1,0:T(8,128)(2,1)} %get-tuple-element.10), channel_id=1, source_target_pairs={{0,192},{16,208},{1,193},{17,209},{2,194},{18,210},{3,195},{19,211... | collective-permute-start | bytes 393224 | tf_op jit(solution)/shard_map/ppermute | solution.py:60
  5.5 8.3 %collective-permute-start = (bf16[256,256]{1,0:T(8,128)(2,1)}, bf16[256,256]{1,0:T(8,128)(2,1)S(1)}, u32[]{:S(2)}, u32[]{:S(2)}) collective-permute-start(bf16[256,256]{1,0:T(8,128)(2,1)} %get-tuple-element.10), channel_id=1, source_target_pairs={{0,448},{16,464},{1,449},{17,465},{2,450},{18,466},{3,451},{19,467... | collective-permute-start | bytes 393224 | tf_op jit(solution)/shard_map/ppermute | solution.py:60
  13.9 14.7 %collective-permute-start.5 = (bf16[256,256]{1,0:T(8,128)(2,1)S(1)}, bf16[256,256]{1,0:T(8,128)(2,1)S(1)}, u32[]{:S(2)}, u32[]{:S(2)}) collective-permute-start(bf16[256,256]{1,0:T(8,128)(2,1)S(1)} %add_add_fusion.7), channel_id=1, source_target_pairs={{0,128},{16,144},{1,129},{17,145},{2,130},{18,146},{3,131},{19,147... | collective-permute-start | bytes 393224 | tf_op jit(solution)/shard_map/ppermute | solution.py:60
  15.2 14.7 %collective-permute-start.4 = (bf16[256,256]{1,0:T(8,128)(2,1)S(1)}, bf16[256,256]{1,0:T(8,128)(2,1)S(1)}, u32[]{:S(2)}, u32[]{:S(2)}) collective-permute-start(bf16[256,256]{1,0:T(8,128)(2,1)S(1)} %add_add_fusion.7), channel_id=1, source_target_pairs={{0,32},{16,112},{1,33},{17,113},{2,34},{18,114},{3,35},{19,115},{4... | collective-permute-start | bytes 393224 | tf_op jit(solution)/shard_map/ppermute | solution.py:60
  16.5 14.1 %collective-permute-start.3 = (bf16[256,256]{1,0:T(8,128)(2,1)S(1)}, bf16[256,256]{1,0:T(8,128)(2,1)S(1)}, u32[]{:S(2)}, u32[]{:S(2)}) collective-permute-start(bf16[256,256]{1,0:T(8,128)(2,1)S(1)} %add_add_fusion.7), channel_id=1, source_target_pairs={{0,416},{16,496},{1,417},{17,497},{2,418},{18,498},{3,419},{19,499... | collective-permute-start | bytes 393224 | tf_op jit(solution)/shard_map/ppermute | solution.py:60
  17.8 14.5 %collective-permute-start.13 = (bf16[512,256]{1,0:T(8,128)(2,1)}, bf16[512,256]{1,0:T(8,128)(2,1)S(1)}, u32[]{:S(2)}, u32[]{:S(2)}) collective-permute-start(bf16[512,256]{1,0:T(8,128)(2,1)} %get-tuple-element.11), channel_id=1, source_target_pairs={{0,10},{1,11},{16,26},{17,27},{32,42},{33,43},{48,58},{49,59},{64,... | collective-permute-start | bytes 786440 | tf_op jit(solution)/shard_map/ppermute | solution.py:60
  27.3 8.5 %collective-permute-start.12 = (bf16[512,256]{1,0:T(8,128)(2,1)}, bf16[512,256]{1,0:T(8,128)(2,1)S(1)}, u32[]{:S(2)}, u32[]{:S(2)}) collective-permute-start(bf16[512,256]{1,0:T(8,128)(2,1)} %get-tuple-element.11), channel_id=1, source_target_pairs={{0,6},{1,7},{16,22},{17,23},{32,38},{33,39},{48,54},{49,55},{64,70... | collective-permute-start | bytes 786440 | tf_op jit(solution)/shard_map/ppermute | solution.py:60
  28.7 24.2 %collective-permute-start.19 = (bf16[768,256]{1,0:T(8,128)(2,1)}, bf16[768,256]{1,0:T(8,128)(2,1)S(1)}, u32[]{:S(2)}, u32[]{:S(2)}) collective-permute-start(bf16[768,256]{1,0:T(8,128)(2,1)} %get-tuple-element.14), channel_id=1, source_target_pairs={{0,256},{16,272},{1,257},{17,273},{2,258},{18,274},{3,259},{19,275... | collective-permute-start | bytes 1179656 | tf_op jit(solution)/shard_map/ppermute | solution.py:60
  30.0 24.8 %collective-permute-start.18 = (bf16[768,256]{1,0:T(8,128)(2,1)}, bf16[768,256]{1,0:T(8,128)(2,1)S(1)}, u32[]{:S(2)}, u32[]{:S(2)}) collective-permute-start(bf16[768,256]{1,0:T(8,128)(2,1)} %get-tuple-element.14), channel_id=1, source_target_pairs={{0,192},{16,208},{1,193},{17,209},{2,194},{18,210},{3,195},{19,211... | collective-permute-start | bytes 1179656 | tf_op jit(solution)/shard_map/ppermute | solution.py:60
  30.7 24.1 %collective-permute-start.17 = (bf16[768,256]{1,0:T(8,128)(2,1)}, bf16[768,256]{1,0:T(8,128)(2,1)S(1)}, u32[]{:S(2)}, u32[]{:S(2)}) collective-permute-start(bf16[768,256]{1,0:T(8,128)(2,1)} %get-tuple-element.14), channel_id=1, source_target_pairs={{0,448},{16,464},{1,449},{17,465},{2,450},{18,466},{3,451},{19,467... | collective-permute-start | bytes 1179656 | tf_op jit(solution)/shard_map/ppermute | solution.py:60
  32.3 8.1 %collective-permute-start.6 = (bf16[256,256]{1,0:T(8,128)(2,1)S(1)}, bf16[256,256]{1,0:T(8,128)(2,1)S(1)}, u32[]{:S(2)}, u32[]{:S(2)}) collective-permute-start(bf16[256,256]{1,0:T(8,128)(2,1)S(1)} %add_add_fusion.6), channel_id=1, source_target_pairs={{0,16},{1,17},{2,18},{3,19},{4,20},{5,21},{6,22},{7,23},{8,24},{9,... | collective-permute-start | bytes 393224 | tf_op jit(solution)/shard_map/ppermute | solution.py:60
  36.8 5.2 %collective-permute-start.15 = (bf16[512,256]{1,0:T(8,128)(2,1)S(1)}, bf16[512,256]{1,0:T(8,128)(2,1)S(1)}, u32[]{:S(2)}, u32[]{:S(2)}) collective-permute-start(bf16[512,256]{1,0:T(8,128)(2,1)S(1)} %add_add_fusion.3), channel_id=1, source_target_pairs={{0,14},{1,15},{16,30},{17,31},{32,46},{33,47},{48,62},{49,63},{64,... | collective-permute-start | bytes 786440 | tf_op jit(solution)/shard_map/ppermute | solution.py:60
  40.4 7.9 %collective-permute-start.14 = (bf16[512,256]{1,0:T(8,128)(2,1)S(1)}, bf16[512,256]{1,0:T(8,128)(2,1)S(1)}, u32[]{:S(2)}, u32[]{:S(2)}) collective-permute-start(bf16[512,256]{1,0:T(8,128)(2,1)S(1)} %add_add_fusion.3), channel_id=1, source_target_pairs={{0,2},{1,3},{16,18},{17,19},{32,34},{33,35},{48,50},{49,51},{64,66... | collective-permute-start | bytes 786440 | tf_op jit(solution)/shard_map/ppermute | solution.py:60
  41.7 27.6 %copy-start = (bf16[256,256]{1,0:T(8,128)(2,1)}, bf16[256,256]{1,0:T(8,128)(2,1)S(1)}, u32[]{:S(2)}) copy-start(bf16[256,256]{1,0:T(8,128)(2,1)S(1)} %get-tuple-element.24.first_0) | copy-start | bytes 393220
  41.7 27.5 %copy-start.1 = (bf16[256,256]{1,0:T(8,128)(2,1)}, bf16[256,256]{1,0:T(8,128)(2,1)S(1)}, u32[]{:S(2)}) copy-start(bf16[256,256]{1,0:T(8,128)(2,1)S(1)} %get-tuple-element.25.first_1) | copy-start | bytes 393220
  42.0 21.3 %collective-permute-start.7 = (bf16[512,256]{1,0:T(8,128)(2,1)S(1)}, bf16[512,256]{1,0:T(8,128)(2,1)S(1)}, u32[]{:S(2)}, u32[]{:S(2)}) collective-permute-start(bf16[512,256]{1,0:T(8,128)(2,1)S(1)} %pad_maximum_fusion), channel_id=1, source_target_pairs={{0,6},{1,7},{16,22},{17,23},{32,38},{33,39},{48,54},{49,55},{64,70... | collective-permute-start | bytes 786440 | tf_op jit(solution)/shard_map/ppermute | solution.py:60
  48.2 16.3 %collective-permute-start.8 = (bf16[512,256]{1,0:T(8,128)(2,1)S(1)}, bf16[512,256]{1,0:T(8,128)(2,1)S(1)}, u32[]{:S(2)}, u32[]{:S(2)}) collective-permute-start(bf16[512,256]{1,0:T(8,128)(2,1)S(1)} %pad_maximum_fusion), channel_id=1, source_target_pairs={{0,10},{1,11},{16,26},{17,27},{32,42},{33,43},{48,58},{49,59},{64,... | collective-permute-start | bytes 786440 | tf_op jit(solution)/shard_map/ppermute | solution.py:60
  52.9 13.1 %collective-permute-start.16 = (bf16[512,256]{1,0:T(8,128)(2,1)S(1)}, bf16[512,256]{1,0:T(8,128)(2,1)S(1)}, u32[]{:S(2)}, u32[]{:S(2)}) collective-permute-start(bf16[512,256]{1,0:T(8,128)(2,1)S(1)} %add_add_fusion.2), channel_id=1, source_target_pairs={{0,1},{1,0},{2,3},{3,2},{4,5},{5,4},{6,7},{7,6},{8,9},{9,8},{10,11... | collective-permute-start | bytes 786440 | tf_op jit(solution)/shard_map/ppermute | solution.py:60
  54.9 14.3 %collective-permute-start.22 = (bf16[768,256]{1,0:T(8,128)(2,1)S(1)}, bf16[768,256]{1,0:T(8,128)(2,1)S(1)}, u32[]{:S(2)}, u32[]{:S(2)}) collective-permute-start(bf16[768,256]{1,0:T(8,128)(2,1)S(1)} %add_add_fusion.1), channel_id=1, source_target_pairs={{0,128},{16,144},{1,129},{17,145},{2,130},{18,146},{3,131},{19,147... | collective-permute-start | bytes 1179656 | tf_op jit(solution)/shard_map/ppermute | solution.py:60
  60.3 12.4 %collective-permute-start.21 = (bf16[768,256]{1,0:T(8,128)(2,1)S(1)}, bf16[768,256]{1,0:T(8,128)(2,1)S(1)}, u32[]{:S(2)}, u32[]{:S(2)}) collective-permute-start(bf16[768,256]{1,0:T(8,128)(2,1)S(1)} %add_add_fusion.1), channel_id=1, source_target_pairs={{0,32},{16,112},{1,33},{17,113},{2,34},{18,114},{3,35},{19,115},{4... | collective-permute-start | bytes 1179656 | tf_op jit(solution)/shard_map/ppermute | solution.py:60
  63.2 17.4 %collective-permute-start.20 = (bf16[768,256]{1,0:T(8,128)(2,1)S(1)}, bf16[768,256]{1,0:T(8,128)(2,1)S(1)}, u32[]{:S(2)}, u32[]{:S(2)}) collective-permute-start(bf16[768,256]{1,0:T(8,128)(2,1)S(1)} %add_add_fusion.1), channel_id=1, source_target_pairs={{0,416},{16,496},{1,417},{17,497},{2,418},{18,498},{3,419},{19,499... | collective-permute-start | bytes 1179656 | tf_op jit(solution)/shard_map/ppermute | solution.py:60
  64.7 21.9 %collective-permute-start.10 = (bf16[512,256]{1,0:T(8,128)(2,1)S(1)}, bf16[512,256]{1,0:T(8,128)(2,1)S(1)}, u32[]{:S(2)}, u32[]{:S(2)}) collective-permute-start(bf16[512,256]{1,0:T(8,128)(2,1)S(1)} %add_add_fusion.5), channel_id=1, source_target_pairs={{0,14},{1,15},{16,30},{17,31},{32,46},{33,47},{48,62},{49,63},{64,... | collective-permute-start | bytes 786440 | tf_op jit(solution)/shard_map/ppermute | solution.py:60
  66.0 20.6 %collective-permute-start.9 = (bf16[512,256]{1,0:T(8,128)(2,1)S(1)}, bf16[512,256]{1,0:T(8,128)(2,1)S(1)}, u32[]{:S(2)}, u32[]{:S(2)}) collective-permute-start(bf16[512,256]{1,0:T(8,128)(2,1)S(1)} %add_add_fusion.5), channel_id=1, source_target_pairs={{0,2},{1,3},{16,18},{17,19},{32,34},{33,35},{48,50},{49,51},{64,66... | collective-permute-start | bytes 786440 | tf_op jit(solution)/shard_map/ppermute | solution.py:60
  80.8 29.7 %collective-permute-start.24 = (bf16[384,256]{1,0:T(8,128)(2,1)S(1)}, bf16[384,256]{1,0:T(8,128)(2,1)S(1)}, u32[]{:S(2)}, u32[]{:S(2)}) collective-permute-start(bf16[384,256]{1,0:T(8,128)(2,1)S(1)} %get-tuple-element.22), channel_id=1, source_target_pairs={{16,0},{17,1},{18,2},{19,3},{20,4},{21,5},{22,6},{23,7},{24,8},{25... | collective-permute-start | bytes 589832 | tf_op jit(solution)/shard_map/ppermute | solution.py:60
  82.7 27.7 %collective-permute-start.23 = (bf16[384,256]{1,0:T(8,128)(2,1)S(1)}, bf16[384,256]{1,0:T(8,128)(2,1)S(1)}, u32[]{:S(2)}, u32[]{:S(2)}) collective-permute-start(bf16[384,256]{1,0:T(8,128)(2,1)S(1)} %get-tuple-element.23), channel_id=1, source_target_pairs={{0,16},{1,17},{2,18},{3,19},{4,20},{5,21},{6,22},{7,23},{8,24},{9,... | collective-permute-start | bytes 589832 | tf_op jit(solution)/shard_map/ppermute | solution.py:60
  86.7 24.7 %collective-permute-start.11 = (bf16[512,256]{1,0:T(8,128)(2,1)S(1)}, bf16[512,256]{1,0:T(8,128)(2,1)S(1)}, u32[]{:S(2)}, u32[]{:S(2)}) collective-permute-start(bf16[512,256]{1,0:T(8,128)(2,1)S(1)} %add_add_fusion.4), channel_id=1, source_target_pairs={{0,1},{1,0},{2,3},{3,2},{4,5},{5,4},{6,7},{7,6},{8,9},{9,8},{10,11... | collective-permute-start | bytes 786440 | tf_op jit(solution)/shard_map/ppermute | solution.py:60

commit v2 on v1

--- a/solution.py
+++ b/solution.py
@@ -5,6 +5,7 @@
 from jax.experimental.pallas import tpu as pltpu
 from jax.sharding import Mesh
 from jax.sharding import PartitionSpec as P
+
 
 BLK = 256
 X, Y, Z = 4, 8, 8
@@ -37,12 +38,14 @@
     ]
 
 
-HOLDERS = [(0, 0), (2, 0), (1, 4), (3, 4)]
-SPREAD_1 = [plane_pairs([((0, 0), h)]) for h in ((3, 4), (1, 4), (2, 0))]
-SPREAD_2 = [
-    plane_pairs([(h, (h[0] + dx, h[1] + dy)) for h in HOLDERS])
-    for dx, dy in ((-1, 2), (0, 2), (1, 0))
+HOLDERS = [(0, 0), (1, 6), (3, 2), (0, 6)]
+SPREAD_1 = [plane_pairs([((0, 0), h)]) for h in HOLDERS[1:]]
+TARGETS = [
+    [(2, 0), (1, 4), (2, 2), (2, 4)],
+    [(1, 2), (1, 0), (3, 4), (0, 4)],
+    [(3, 0), (2, 6), (0, 2), (3, 6)],
 ]
+SPREAD_2 = [plane_pairs(list(zip(HOLDERS, targets))) for targets in TARGETS]
 UP = [
     (device(x, y, z, c), device(x, y + 1, z, c))
     for x in range(X) for y in range(Y) for z in range(Z) for c in range(2)
@@ -74,7 +77,7 @@
     return slot_of, where, count
 
 
-def pack_kernel(here, row_pattern, col_pattern, matrix, first_out, rest_out, panel_out, sems):
+def pack_kernel(here, row_pattern, col_pattern, matrix, upper_out, panel_out, sems):
     prow, pcol = here[0], here[1]
     row_blocks, col_blocks = matrix.shape[0] // BLK, matrix.shape[1] // BLK
     k = (prow == 1).astype(jnp.int32)
@@ -83,7 +86,7 @@
     copies = []
     for s in range(COL_CAP):
         source = matrix.at[pl.ds(0, BLK), pl.ds(pl.multiple_of(col_at[s] * BLK, BLK), BLK)]
-        target = first_out if s == 0 else rest_out.at[pl.ds((s - 1) * BLK, BLK)]
+        target = upper_out.at[pl.ds(s * BLK, BLK)]
         copies.append(pltpu.make_async_copy(source, target, sems.at[s]))
     rows = [row_pattern[1, prow * row_blocks + i] > 0 for i in range(row_blocks)]
     _, row_at, count = slots(rows, ROW_CAP)
@@ -110,10 +113,9 @@
     return pl.pallas_call(
         pack_kernel,
         in_specs=[smem, smem, smem, pl.BlockSpec(memory_space=pl.ANY)],
-        out_specs=[vmem] * 3,
+        out_specs=[vmem] * 2,
         out_shape=[
-            jax.ShapeDtypeStruct((BLK, BLK), jnp.bfloat16),
-            jax.ShapeDtypeStruct(((COL_CAP - 1) * BLK, BLK), jnp.bfloat16),
+            jax.ShapeDtypeStruct((COL_CAP * BLK, BLK), jnp.bfloat16),
             jax.ShapeDtypeStruct((ROW_CAP * BLK, BLK), jnp.bfloat16),
         ],
         scratch_shapes=[pltpu.SemaphoreType.DMA((COL_CAP + ROW_CAP,))],
@@ -130,11 +132,7 @@
     return jnp.dot(a, b, preferred_element_type=jnp.float32)
 
 
-def panels_kernel(
-    here, row_pattern, pivot_0, upper_01, pivot_1, panel_0, panel_1, lower_0, lower_1
-):
-    prow = here[0]
-    row_blocks = row_pattern.shape[1] // (X * Y)
+def invert_kernel(pivot_0, pivot_1, *out):
     i = lax.broadcasted_iota(jnp.int32, (BLK, BLK), 0)
     j = lax.broadcasted_iota(jnp.int32, (BLK, BLK), 1)
     diagonal = i == j
@@ -157,42 +155,61 @@
                 )
             if step < 7:
                 powers[n] = dot(high, high) + (dot(high, low) + dot(low, high))
+    for n in range(2):
+        high, low = halves(sums[n] * scales[n])
+        out[2 * n][...] = high
+        out[2 * n + 1][...] = low
+
+
+def invert(pivot_0, pivot_1):
+    vmem = pl.BlockSpec(memory_space=pltpu.VMEM)
+    return pl.pallas_call(
+        invert_kernel,
+        in_specs=[vmem] * 2,
+        out_specs=[vmem] * 4,
+        out_shape=[jax.ShapeDtypeStruct((BLK, BLK), jnp.bfloat16)] * 4,
+        cost_estimate=pl.CostEstimate(
+            flops=96 * BLK**3, bytes_accessed=12 * BLK * BLK, transcendentals=0
+        ),
+        name="invert",
+    )(pivot_0, pivot_1)
+
+
+def lower_kernel(
+    here, row_pattern, high_0, low_0, high_1, low_1, upper_01, panel_0, panel_1, lower_0, lower_1
+):
+    prow = here[0]
+    row_blocks = row_pattern.shape[1] // (X * Y)
     rows = [row_pattern[1, prow * row_blocks + b] > 0 for b in range(row_blocks)]
     _, row_at, _ = slots(rows, ROW_CAP)
-    for n in range(2):
-        inverse = sums[n] * scales[n]
-        high, low = halves(inverse)
-        for s in range(ROW_CAP):
-            here_rows = pl.ds(s * BLK, BLK)
-            if n == 0:
-                source = panel_0[here_rows, :]
-                done = (prow == 0) & (row_at[s] == 0)
-            else:
-                source = (
-                    panel_1[here_rows, :].astype(jnp.float32)
-                    - dot(lower_0[here_rows, :], upper_01[...])
-                ).astype(jnp.bfloat16)
-                done = (prow <= 1) & (row_at[s] == 0)
-            lower = dot(source, high) + dot(source, low)
-            target = lower_0 if n == 0 else lower_1
-            target[here_rows, :] = jnp.where(done, 0.0, lower).astype(jnp.bfloat16)
-
-
-def panels(here, row_pattern, *blocks):
+    for s in range(ROW_CAP):
+        at = pl.ds(s * BLK, BLK)
+        lower = dot(panel_0[at, :], high_0[...]) + dot(panel_0[at, :], low_0[...])
+        done = (prow == 0) & (row_at[s] == 0)
+        lower = jnp.where(done, 0.0, lower).astype(jnp.bfloat16)
+        lower_0[at, :] = lower
+        rest = panel_1[at, :].astype(jnp.float32) - dot(lower, upper_01[...])
+        rest = rest.astype(jnp.bfloat16)
+        lower = dot(rest, high_1[...]) + dot(rest, low_1[...])
+        done = (prow <= 1) & (row_at[s] == 0)
+        lower_1[at, :] = jnp.where(done, 0.0, lower).astype(jnp.bfloat16)
+
+
+def lowers(here, row_pattern, *blocks):
     smem = pl.BlockSpec(memory_space=pltpu.SMEM)
     vmem = pl.BlockSpec(memory_space=pltpu.VMEM)
     shape = jax.ShapeDtypeStruct((ROW_CAP * BLK, BLK), jnp.bfloat16)
     return pl.pallas_call(
-        panels_kernel,
-        in_specs=[smem, smem] + [vmem] * 5,
+        lower_kernel,
+        in_specs=[smem, smem] + [vmem] * 7,
         out_specs=[vmem] * 2,
         out_shape=[shape, shape],
-        name="panels",
+        name="lowers",
     )(here, row_pattern, *blocks)
 
 
 def update_kernel(
-    here, row_pattern, col_pattern, source, lower_0, lower_1, first_0, rest_0, first_1, rest_1, out
+    here, row_pattern, col_pattern, source, lower_0, lower_1, upper_0, upper_1, out
 ):
     prow, pcol = here[0], here[1]
     i = pl.program_id(0)
@@ -208,7 +225,7 @@
     done = [first & (prow == 0), first & (prow <= 1)]
     rows = pl.ds(pl.multiple_of(slot * BLK, BLK), BLK)
     lower = [lower_0[rows, :], lower_1[rows, :]]
-    upper = [(first_0, rest_0), (first_1, rest_1)]
+    upper = [upper_0, upper_1]
     flags = [[col_pattern[k, pcol * col_blocks + j] > 0 for j in range(col_blocks)] for k in (0, 1)]
     col_slot = [slots(f, COL_CAP)[0] for f in flags]
     for j in range(col_blocks):
@@ -223,12 +240,8 @@
             used = stored[k] & jnp.logical_not(done[k]) & flags[k][j]
             if j == 0:
                 used = used & (pcol > k)
-            s = col_slot[k][j]
-            if j == 0:
-                block = upper[k][0][...]
-            else:
-                at = pl.ds(pl.multiple_of(jnp.maximum(s - 1, 0) * BLK, BLK), BLK)
-                block = jnp.where(s == 0, upper[k][0][...], upper[k][1][at, :])
+            at = pl.ds(pl.multiple_of(col_slot[k][j] * BLK, BLK), BLK)
+            block = upper[k][at, :]
             product = jnp.where(used, dot(lower[k], block), 0.0)
             value = (value - product).astype(jnp.bfloat16)
             if j == 0:
@@ -249,7 +262,7 @@
     return pl.pallas_call(
         update_kernel,
         grid=(row_blocks,),
-        in_specs=[smem] * 3 + [strip] + [vmem] * 6,
+        in_specs=[smem] * 3 + [strip] + [vmem] * 4,
         out_specs=strip,
         out_shape=jax.ShapeDtypeStruct(matrix.shape, matrix.dtype),
         name="update",
@@ -263,7 +276,7 @@
     here = jnp.where(jnp.arange(2) == 0, prow, pcol)
     even = y % 2 == 0
     core_0 = pcol % 2 == 0
-    first, rest, panel = pack(here, row_pattern, col_pattern, matrix)
+    upper, panel = pack(here, row_pattern, col_pattern, matrix)
     zero = jnp.zeros((), jnp.bfloat16)
 
     def only(flag, value):
@@ -285,31 +298,33 @@
         every = held
         for pairs in LINE_2:
             every = every + send(held, pairs)
-        return every, send(every, SWAP)
-
-    first_held = spread(first)
-    first_came = send(first_held, UP)
-    first_0 = jnp.where(even, first_held, first_came)
-    first_1 = jnp.where(even, first_came, first_held)
-    mine, other = along(panel)
-    panel_0 = jnp.where(core_0, mine, other)
-    panel_1 = jnp.where(core_0, other, mine)
-    mine, other = along(jnp.concatenate([first_0, first_1], axis=0))
-    pivot_0 = jnp.where(core_0, mine[:BLK], other[:BLK])
-    upper_01 = jnp.where(core_0, other[:BLK], mine[:BLK])
-    pivot_1 = jnp.where(core_0, other[BLK:], mine[BLK:])
-    rest_held = spread(rest)
-    half = rest.shape[0] // 2
-    rest_came = jnp.concatenate(
-        [send(rest_held[:half], UP), send(rest_held[half:], DOWN)],
+        return every
+
+    upper_held = spread(upper)
+    half = upper.shape[0] // 2
+    upper_came = jnp.concatenate(
+        [send(upper_held[:half], UP), send(upper_held[half:], DOWN)],
         axis=0,
     )
-    rest_0 = jnp.where(even, rest_held, rest_came)
-    rest_1 = jnp.where(even, rest_came, rest_held)
-    lower_0, lower_1 = panels(here, row_pattern, pivot_0, upper_01, pivot_1, panel_0, panel_1)
+    upper_0 = jnp.where(even, upper_held, upper_came)
+    upper_1 = jnp.where(even, upper_came, upper_held)
+    panel = along(panel)
+    pivot_held = spread(panel[:BLK])
+    pivot_came = send(pivot_held, UP)
+    mine = jnp.concatenate(
+        [jnp.where(even, pivot_held, pivot_came), jnp.where(even, pivot_came, pivot_held), panel],
+        axis=0,
+    )
+    other = send(mine, SWAP)
+    pivot_0 = jnp.where(core_0, mine[:BLK], other[:BLK])
+    pivot_1 = jnp.where(core_0, other[BLK : 2 * BLK], mine[BLK : 2 * BLK])
+    upper_01 = jnp.where(core_0, other[:BLK], mine[:BLK])
+    panel_0 = jnp.where(core_0, mine[2 * BLK :], other[2 * BLK :])
+    panel_1 = jnp.where(core_0, other[2 * BLK :], mine[2 * BLK :])
+    inverses = invert(pivot_0, pivot_1)
+    lower_0, lower_1 = lowers(here, row_pattern, *inverses, upper_01, panel_0, panel_1)
     return update(
-        here, row_pattern, col_pattern, matrix,
-        lower_0, lower_1, first_0, rest_0, first_1, rest_1,
+        here, row_pattern, col_pattern, matrix, lower_0, lower_1, upper_0, upper_1
     )
 
 

time: 124 us -> 121 us (0.976)
  the two profiles are of different devices: /device:TPU:4 before, /device:TPU:2 now
where the time goes in v2:
time: 121 us
  waiting for transfers between devices  64.4 us (53%)
  starting transfers between devices  35.3 us (29%)
  Pallas kernels  15.9 us (13%)
  other arithmetic  4.58 us (4%)
    ppermute x20, waiting for transfers between devices, send(): return lax.ppermute(value, AXES, pairs)  64.4 us
    ppermute x20, starting transfers between devices, send(): return lax.ppermute(value, AXES, pairs)  35.3 us
    pallas_call x1, Pallas kernels, update(): pl.pallas_call(update_kernel, grid=(row_blocks,), in_specs=[smem] * 3 + [...  5.14 us
    pallas_call x1, Pallas kernels, invert(): pl.pallas_call(invert_kernel, in_specs=[vmem] * 2, out_specs=[vmem] * 4,...  4.99 us
    pallas_call x1, Pallas kernels, pack(): pl.pallas_call(pack_kernel, in_specs=[smem, smem, smem, pl.BlockSpec(memo...  2.94 us
    pallas_call x1, Pallas kernels, lowers(): pl.pallas_call(lower_kernel, in_specs=[smem, smem] + [vmem] * 7, out_spec...  2.8 us
  transfers between devices with their start and end apart: 20, of which 7 were waited for; matrix products, arithmetic and copies ran while one was open for 2% of the time, Pallas kernels for 0%

profile of v2, /device:TPU:2, one launch (start us, length us, event | category | flops | bytes accessed | tf_op | source)
XLA Modules:
  0.0 120.7 jit_solution(588640934805761691)
XLA Ops:
  0.5 2.9 %pack.1 = (bf16[1024,256]{1,0:T(8,128)(2,1)}, bf16[512,256]{1,0:T(8,128)(2,1)}) custom-call(s32[2]{0:T(128)} %compare_select_fusion.here, s32[2,96]{1,0:T(2,128)} %row_pattern.5, s32[2,96]{1,0:T(2,128)} %col_pattern.3, bf16[768,1536]{1,0:T(8,128)(2,1)} %source.1), custom_call_target="tpu_custom_call" | custom-call | tf_op jit(solution)/shard_map/pack/pallas_call | solution.py:113
  3.5 11.1 %collective-permute-start.1 = (bf16[512,256]{1,0:T(8,128)(2,1)}, bf16[512,256]{1,0:T(8,128)(2,1)S(1)}, u32[]{:S(2)}, u32[]{:S(2)}) collective-permute-start(bf16[512,256]{1,0:T(8,128)(2,1)} %get-tuple-element.13), channel_id=1, source_target_pairs={{0,10},{1,11},{16,26},{17,27},{32,42},{33,43},{48,58},{49,59},{64,... | collective-permute-start | bytes 786440 | tf_op jit(solution)/shard_map/ppermute | solution.py:63
  14.6 1.3 %collective-permute-start = (bf16[512,256]{1,0:T(8,128)(2,1)}, bf16[512,256]{1,0:T(8,128)(2,1)S(1)}, u32[]{:S(2)}, u32[]{:S(2)}) collective-permute-start(bf16[512,256]{1,0:T(8,128)(2,1)} %get-tuple-element.13), channel_id=1, source_target_pairs={{0,6},{1,7},{16,22},{17,23},{32,38},{33,39},{48,54},{49,55},{64,70... | collective-permute-start | bytes 786440 | tf_op jit(solution)/shard_map/ppermute | solution.py:63
  15.9 0.7 collective-permute-start.14
  16.6 0.7 collective-permute-start.13
  17.3 0.7 collective-permute-start.12
  18.0 2.4 %collective-permute-done.1 = bf16[512,256]{1,0:T(8,128)(2,1)S(1)} collective-permute-done((bf16[512,256]{1,0:T(8,128)(2,1)}, bf16[512,256]{1,0:T(8,128)(2,1)S(1)}, u32[]{:S(2)}, u32[]{:S(2)}) %collective-permute-start.1) | collective-permute-done | bytes 262176 | tf_op jit(solution)/shard_map/ppermute | solution.py:63
  20.4 1.3 %collective-permute-done = bf16[512,256]{1,0:T(8,128)(2,1)S(1)} collective-permute-done((bf16[512,256]{1,0:T(8,128)(2,1)}, bf16[512,256]{1,0:T(8,128)(2,1)S(1)}, u32[]{:S(2)}, u32[]{:S(2)}) %collective-permute-start) | collective-permute-done | bytes 262176 | tf_op jit(solution)/shard_map/ppermute | solution.py:63
  21.7 1.0 add_add_fusion.3
  22.7 1.3 %collective-permute-start.3 = (bf16[512,256]{1,0:T(8,128)(2,1)S(1)}, bf16[512,256]{1,0:T(8,128)(2,1)S(1)}, u32[]{:S(2)}, u32[]{:S(2)}) collective-permute-start(bf16[512,256]{1,0:T(8,128)(2,1)S(1)} %add_add_fusion.3), channel_id=1, source_target_pairs={{0,14},{1,15},{16,30},{17,31},{32,46},{33,47},{48,62},{49,63},{64,... | collective-permute-start | bytes 786440 | tf_op jit(solution)/shard_map/ppermute | solution.py:63
  24.0 1.3 %collective-permute-start.2 = (bf16[512,256]{1,0:T(8,128)(2,1)S(1)}, bf16[512,256]{1,0:T(8,128)(2,1)S(1)}, u32[]{:S(2)}, u32[]{:S(2)}) collective-permute-start(bf16[512,256]{1,0:T(8,128)(2,1)S(1)} %add_add_fusion.3), channel_id=1, source_target_pairs={{0,2},{1,3},{16,18},{17,19},{32,34},{33,35},{48,50},{49,51},{64,66... | collective-permute-start | bytes 786440 | tf_op jit(solution)/shard_map/ppermute | solution.py:63
  25.3 3.6 %collective-permute-done.3 = bf16[512,256]{1,0:T(8,128)(2,1)S(1)} collective-permute-done((bf16[512,256]{1,0:T(8,128)(2,1)S(1)}, bf16[512,256]{1,0:T(8,128)(2,1)S(1)}, u32[]{:S(2)}, u32[]{:S(2)}) %collective-permute-start.3) | collective-permute-done | bytes 262176 | tf_op jit(solution)/shard_map/ppermute | solution.py:63
  28.9 1.3 %collective-permute-done.2 = bf16[512,256]{1,0:T(8,128)(2,1)S(1)} collective-permute-done((bf16[512,256]{1,0:T(8,128)(2,1)S(1)}, bf16[512,256]{1,0:T(8,128)(2,1)S(1)}, u32[]{:S(2)}, u32[]{:S(2)}) %collective-permute-start.2) | collective-permute-done | bytes 262176 | tf_op jit(solution)/shard_map/ppermute | solution.py:63
  30.3 0.7 collective-permute-start.5
  31.0 0.7 collective-permute-start.4
  32.5 0.7 collective-permute-start.17
  33.2 1.3 %collective-permute-start.16 = (bf16[1024,256]{1,0:T(8,128)(2,1)S(1)}, bf16[1024,256]{1,0:T(8,128)(2,1)S(1)}, u32[]{:S(2)}, u32[]{:S(2)}) collective-permute-start(bf16[1024,256]{1,0:T(8,128)(2,1)S(1)} %add_add_fusion.1), channel_id=1, source_target_pairs={{0,160},{16,240},{1,161},{17,241},{2,162},{18,242},{3,163},{19,243... | collective-permute-start | bytes 1572872 | tf_op jit(solution)/shard_map/ppermute | solution.py:63
  34.5 0.7 collective-permute-start.15
  35.9 1.3 %collective-permute-start.8 = (bf16[256,256]{1,0:T(8,128)(2,1)S(1)}, bf16[256,256]{1,0:T(8,128)(2,1)S(1)}, u32[]{:S(2)}, u32[]{:S(2)}) collective-permute-start(bf16[256,256]{1,0:T(8,128)(2,1)S(1)} %add_add_fusion.5), channel_id=1, source_target_pairs={{0,160},{16,240},{1,161},{17,241},{2,162},{18,242},{3,163},{19,243... | collective-permute-start | bytes 393224 | tf_op jit(solution)/shard_map/ppermute | solution.py:63
  37.3 0.7 collective-permute-start.7
  37.9 50.2 %collective-permute-done.8 = bf16[256,256]{1,0:T(8,128)(2,1)S(1)} collective-permute-done((bf16[256,256]{1,0:T(8,128)(2,1)S(1)}, bf16[256,256]{1,0:T(8,128)(2,1)S(1)}, u32[]{:S(2)}, u32[]{:S(2)}) %collective-permute-start.8) | collective-permute-done | bytes 131104 | tf_op jit(solution)/shard_map/ppermute | solution.py:63
  88.2 1.9 %collective-permute-start.10 = (bf16[256,256]{1,0:T(8,128)(2,1)S(1)}, bf16[256,256]{1,0:T(8,128)(2,1)S(1)}, u32[]{:S(2)}, u32[]{:S(2)}) collective-permute-start(bf16[256,256]{1,0:T(8,128)(2,1)S(1)} %add_add_fusion.4), channel_id=1, source_target_pairs={{0,16},{1,17},{2,18},{3,19},{4,20},{5,21},{6,22},{7,23},{8,24},{9,... | collective-permute-start | bytes 393224 | tf_op jit(solution)/shard_map/ppermute | solution.py:63
  90.3 5.1 %collective-permute-start.19 = (bf16[512,256]{1,0:T(8,128)(2,1)S(1)}, bf16[512,256]{1,0:T(8,128)(2,1)S(1)}, u32[]{:S(2)}, u32[]{:S(2)}) collective-permute-start(bf16[512,256]{1,0:T(8,128)(2,1)S(1)} %get-tuple-element.27), channel_id=1, source_target_pairs={{16,0},{17,1},{18,2},{19,3},{20,4},{21,5},{22,6},{23,7},{24,8},{25... | collective-permute-start | bytes 786440 | tf_op jit(solution)/shard_map/ppermute | solution.py:63
  95.5 1.9 %collective-permute-start.18 = (bf16[512,256]{1,0:T(8,128)(2,1)S(1)}, bf16[512,256]{1,0:T(8,128)(2,1)S(1)}, u32[]{:S(2)}, u32[]{:S(2)}) collective-permute-start(bf16[512,256]{1,0:T(8,128)(2,1)S(1)} %get-tuple-element.28), channel_id=1, source_target_pairs={{0,16},{1,17},{2,18},{3,19},{4,20},{5,21},{6,22},{7,23},{8,24},{9,... | collective-permute-start | bytes 786440 | tf_op jit(solution)/shard_map/ppermute | solution.py:63
  97.8 1.9 %collective-permute-start.11 = (bf16[1024,256]{1,0:T(8,128)(2,1)S(1)}, bf16[1024,256]{1,0:T(8,128)(2,1)S(1)}, u32[]{:S(2)}, u32[]{:S(2)}) collective-permute-start(bf16[1024,256]{1,0:T(8,128)(2,1)S(1)} %pad_maximum_fusion), channel_id=1, source_target_pairs={{0,1},{1,0},{2,3},{3,2},{4,5},{5,4},{6,7},{7,6},{8,9},{9,8},{10,11... | collective-permute-start | bytes 1572872 | tf_op jit(solution)/shard_map/ppermute | solution.py:63
  99.7 5.2 %collective-permute-done.18 = bf16[512,256]{1,0:T(8,128)(2,1)S(1)} collective-permute-done((bf16[512,256]{1,0:T(8,128)(2,1)S(1)}, bf16[512,256]{1,0:T(8,128)(2,1)S(1)}, u32[]{:S(2)}, u32[]{:S(2)}) %collective-permute-start.18) | collective-permute-done | bytes 262176 | tf_op jit(solution)/shard_map/ppermute | solution.py:63
  105.0 1.1 broadcast_select_fusion
  106.1 0.8 broadcast_select_fusion.6
  106.9 5.0 %invert.1 = (bf16[256,256]{1,0:T(8,128)(2,1)}, bf16[256,256]{1,0:T(8,128)(2,1)}, bf16[256,256]{1,0:T(8,128)(2,1)}, bf16[256,256]{1,0:T(8,128)(2,1)}) custom-call(bf16[256,256]{1,0:T(8,128)(2,1)} %get-tuple-element.26.pivot_0, bf16[256,256]{1,0:T(8,128)(2,1)} %get-tuple-element.29.pivot_1), custom_call_target="tpu_custom_call" | custom-call | flops 1610612736 | bytes 786432 | tf_op jit(solution)/shard_map/invert/pallas_call | solution.py:166
  111.9 0.9 broadcast_select_fusion.2
  112.7 2.8 %lowers.1 = (bf16[512,256]{1,0:T(8,128)(2,1)}, bf16[512,256]{1,0:T(8,128)(2,1)}) custom-call(s32[2]{0:T(128)} %compare_select_fusion.here, s32[2,96]{1,0:T(2,128)} %row_pattern.5, bf16[256,256]{1,0:T(8,128)(2,1)} %get-tuple-element.14.high_0, bf16[256,256]{1,0:T(8,128)(2,1)} %get-tuple-element.15.low_0, bf16[256,256]{1,0:T(8,128)(2,1)} %get-tuple-element.16.high_1, ...), custom_call_target="tpu_custom_call" | custom-call | tf_op jit(solution)/shard_map/lowers/pallas_call | solution.py:202
  115.5 5.1 %update.1 = bf16[768,1536]{1,0:T(8,128)(2,1)} custom-call(s32[2]{0:T(128)} %compare_select_fusion.here, s32[2,96]{1,0:T(2,128)} %row_pattern.5, s32[2,96]{1,0:T(2,128)} %col_pattern.3, bf16[768,1536]{1,0:T(8,128)(2,1)} %source.1, bf16[512,256]{1,0:T(8,128)(2,1)} %get-tuple-element.18.lower_0, bf16[512,256]{1,0:T(8,128)(2,1)} %get-tuple-element.19.lower_1, ...), custom_call_target="tpu_custom_call" | custom-call | tf_op jit(solution)/shard_map/update/pallas_call | solution.py:262
  (30 shorter events, 2.6 us)
Async XLA Ops:
  3.5 28.9 %copy-start = (bf16[1024,256]{1,0:T(8,128)(2,1)S(1)}, bf16[1024,256]{1,0:T(8,128)(2,1)}, u32[]{:S(2)}) copy-start(bf16[1024,256]{1,0:T(8,128)(2,1)} %get-tuple-element.20) | copy-start | bytes 1572868
  3.5 16.9 %collective-permute-start.1 = (bf16[512,256]{1,0:T(8,128)(2,1)}, bf16[512,256]{1,0:T(8,128)(2,1)S(1)}, u32[]{:S(2)}, u32[]{:S(2)}) collective-permute-start(bf16[512,256]{1,0:T(8,128)(2,1)} %get-tuple-element.13), channel_id=1, source_target_pairs={{0,10},{1,11},{16,26},{17,27},{32,42},{33,43},{48,58},{49,59},{64,... | collective-permute-start | bytes 786440 | tf_op jit(solution)/shard_map/ppermute | solution.py:63
  14.6 7.1 %collective-permute-start = (bf16[512,256]{1,0:T(8,128)(2,1)}, bf16[512,256]{1,0:T(8,128)(2,1)S(1)}, u32[]{:S(2)}, u32[]{:S(2)}) collective-permute-start(bf16[512,256]{1,0:T(8,128)(2,1)} %get-tuple-element.13), channel_id=1, source_target_pairs={{0,6},{1,7},{16,22},{17,23},{32,38},{33,39},{48,54},{49,55},{64,70... | collective-permute-start | bytes 786440 | tf_op jit(solution)/shard_map/ppermute | solution.py:63
  15.9 15.8 %collective-permute-start.14 = (bf16[1024,256]{1,0:T(8,128)(2,1)}, bf16[1024,256]{1,0:T(8,128)(2,1)S(1)}, u32[]{:S(2)}, u32[]{:S(2)}) collective-permute-start(bf16[1024,256]{1,0:T(8,128)(2,1)} %get-tuple-element.20), channel_id=1, source_target_pairs={{0,96},{16,48},{1,97},{17,49},{2,98},{18,50},{3,99},{19,51},{4,100... | collective-permute-start | bytes 1572872 | tf_op jit(solution)/shard_map/ppermute | solution.py:63
  16.6 15.8 %collective-permute-start.13 = (bf16[1024,256]{1,0:T(8,128)(2,1)}, bf16[1024,256]{1,0:T(8,128)(2,1)S(1)}, u32[]{:S(2)}, u32[]{:S(2)}) collective-permute-start(bf16[1024,256]{1,0:T(8,128)(2,1)} %get-tuple-element.20), channel_id=1, source_target_pairs={{0,416},{16,496},{1,417},{17,497},{2,418},{18,498},{3,419},{19,499... | collective-permute-start | bytes 1572872 | tf_op jit(solution)/shard_map/ppermute | solution.py:63
  17.3 15.1 %collective-permute-start.12 = (bf16[1024,256]{1,0:T(8,128)(2,1)}, bf16[1024,256]{1,0:T(8,128)(2,1)S(1)}, u32[]{:S(2)}, u32[]{:S(2)}) collective-permute-start(bf16[1024,256]{1,0:T(8,128)(2,1)} %get-tuple-element.20), channel_id=1, source_target_pairs={{0,224},{16,176},{1,225},{17,177},{2,226},{18,178},{3,227},{19,179... | collective-permute-start | bytes 1572872 | tf_op jit(solution)/shard_map/ppermute | solution.py:63
  22.7 6.2 %collective-permute-start.3 = (bf16[512,256]{1,0:T(8,128)(2,1)S(1)}, bf16[512,256]{1,0:T(8,128)(2,1)S(1)}, u32[]{:S(2)}, u32[]{:S(2)}) collective-permute-start(bf16[512,256]{1,0:T(8,128)(2,1)S(1)} %add_add_fusion.3), channel_id=1, source_target_pairs={{0,14},{1,15},{16,30},{17,31},{32,46},{33,47},{48,62},{49,63},{64,... | collective-permute-start | bytes 786440 | tf_op jit(solution)/shard_map/ppermute | solution.py:63
  24.0 6.2 %collective-permute-start.2 = (bf16[512,256]{1,0:T(8,128)(2,1)S(1)}, bf16[512,256]{1,0:T(8,128)(2,1)S(1)}, u32[]{:S(2)}, u32[]{:S(2)}) collective-permute-start(bf16[512,256]{1,0:T(8,128)(2,1)S(1)} %add_add_fusion.3), channel_id=1, source_target_pairs={{0,2},{1,3},{16,18},{17,19},{32,34},{33,35},{48,50},{49,51},{64,66... | collective-permute-start | bytes 786440 | tf_op jit(solution)/shard_map/ppermute | solution.py:63
  30.3 4.2 %collective-permute-start.5 = (bf16[256,256]{1,0:T(8,128)(2,1)S(1)}, bf16[256,256]{1,0:T(8,128)(2,1)S(1)}, u32[]{:S(2)}, u32[]{:S(2)}) collective-permute-start(bf16[256,256]{1,0:T(8,128)(2,1)S(1)} %slice.26), channel_id=1, source_target_pairs={{0,416},{16,496},{1,417},{17,497},{2,418},{18,498},{3,419},{19,499... | collective-permute-start | bytes 393224 | tf_op jit(solution)/shard_map/ppermute | solution.py:63
  31.0 4.2 %collective-permute-start.4 = (bf16[256,256]{1,0:T(8,128)(2,1)S(1)}, bf16[256,256]{1,0:T(8,128)(2,1)S(1)}, u32[]{:S(2)}, u32[]{:S(2)}) collective-permute-start(bf16[256,256]{1,0:T(8,128)(2,1)S(1)} %slice.26), channel_id=1, source_target_pairs={{0,224},{16,176},{1,225},{17,177},{2,226},{18,178},{3,227},{19,179... | collective-permute-start | bytes 393224 | tf_op jit(solution)/shard_map/ppermute | solution.py:63
  31.7 3.5 %collective-permute-start.6 = (bf16[256,256]{1,0:T(8,128)(2,1)S(1)}, bf16[256,256]{1,0:T(8,128)(2,1)S(1)}, u32[]{:S(2)}, u32[]{:S(2)}) collective-permute-start(bf16[256,256]{1,0:T(8,128)(2,1)S(1)} %slice.26), channel_id=1, source_target_pairs={{0,96},{16,48},{1,97},{17,49},{2,98},{18,50},{3,99},{19,51},{4,100... | collective-permute-start | bytes 393224 | tf_op jit(solution)/shard_map/ppermute | solution.py:63
  32.5 57.7 %collective-permute-start.17 = (bf16[1024,256]{1,0:T(8,128)(2,1)S(1)}, bf16[1024,256]{1,0:T(8,128)(2,1)S(1)}, u32[]{:S(2)}, u32[]{:S(2)}) collective-permute-start(bf16[1024,256]{1,0:T(8,128)(2,1)S(1)} %add_add_fusion.1), channel_id=1, source_target_pairs={{0,384},{16,400},{1,385},{17,401},{2,386},{18,402},{3,387},{19,403... | collective-permute-start | bytes 1572872 | tf_op jit(solution)/shard_map/ppermute | solution.py:63
  33.2 57.0 %collective-permute-start.16 = (bf16[1024,256]{1,0:T(8,128)(2,1)S(1)}, bf16[1024,256]{1,0:T(8,128)(2,1)S(1)}, u32[]{:S(2)}, u32[]{:S(2)}) collective-permute-start(bf16[1024,256]{1,0:T(8,128)(2,1)S(1)} %add_add_fusion.1), channel_id=1, source_target_pairs={{0,160},{16,240},{1,161},{17,241},{2,162},{18,242},{3,163},{19,243... | collective-permute-start | bytes 1572872 | tf_op jit(solution)/shard_map/ppermute | solution.py:63
  34.5 55.7 %collective-permute-start.15 = (bf16[1024,256]{1,0:T(8,128)(2,1)S(1)}, bf16[1024,256]{1,0:T(8,128)(2,1)S(1)}, u32[]{:S(2)}, u32[]{:S(2)}) collective-permute-start(bf16[1024,256]{1,0:T(8,128)(2,1)S(1)} %add_add_fusion.1), channel_id=1, source_target_pairs={{0,256},{16,272},{1,257},{17,273},{2,258},{18,274},{3,259},{19,275... | collective-permute-start | bytes 1572872 | tf_op jit(solution)/shard_map/ppermute | solution.py:63
  35.3 2.0 %collective-permute-start.9 = (bf16[256,256]{1,0:T(8,128)(2,1)S(1)}, bf16[256,256]{1,0:T(8,128)(2,1)S(1)}, u32[]{:S(2)}, u32[]{:S(2)}) collective-permute-start(bf16[256,256]{1,0:T(8,128)(2,1)S(1)} %add_add_fusion.5), channel_id=1, source_target_pairs={{0,384},{16,400},{1,385},{17,401},{2,386},{18,402},{3,387},{19,403... | collective-permute-start | bytes 393224 | tf_op jit(solution)/shard_map/ppermute | solution.py:63
  35.9 52.2 %collective-permute-start.8 = (bf16[256,256]{1,0:T(8,128)(2,1)S(1)}, bf16[256,256]{1,0:T(8,128)(2,1)S(1)}, u32[]{:S(2)}, u32[]{:S(2)}) collective-permute-start(bf16[256,256]{1,0:T(8,128)(2,1)S(1)} %add_add_fusion.5), channel_id=1, source_target_pairs={{0,160},{16,240},{1,161},{17,241},{2,162},{18,242},{3,163},{19,243... | collective-permute-start | bytes 393224 | tf_op jit(solution)/shard_map/ppermute | solution.py:63
  37.3 50.9 %collective-permute-start.7 = (bf16[256,256]{1,0:T(8,128)(2,1)S(1)}, bf16[256,256]{1,0:T(8,128)(2,1)S(1)}, u32[]{:S(2)}, u32[]{:S(2)}) collective-permute-start(bf16[256,256]{1,0:T(8,128)(2,1)S(1)} %add_add_fusion.5), channel_id=1, source_target_pairs={{0,256},{16,272},{1,257},{17,273},{2,258},{18,274},{3,259},{19,275... | collective-permute-start | bytes 393224 | tf_op jit(solution)/shard_map/ppermute | solution.py:63
  88.2 9.5 %collective-permute-start.10 = (bf16[256,256]{1,0:T(8,128)(2,1)S(1)}, bf16[256,256]{1,0:T(8,128)(2,1)S(1)}, u32[]{:S(2)}, u32[]{:S(2)}) collective-permute-start(bf16[256,256]{1,0:T(8,128)(2,1)S(1)} %add_add_fusion.4), channel_id=1, source_target_pairs={{0,16},{1,17},{2,18},{3,19},{4,20},{5,21},{6,22},{7,23},{8,24},{9,... | collective-permute-start | bytes 393224 | tf_op jit(solution)/shard_map/ppermute | solution.py:63
  90.3 14.6 %collective-permute-start.19 = (bf16[512,256]{1,0:T(8,128)(2,1)S(1)}, bf16[512,256]{1,0:T(8,128)(2,1)S(1)}, u32[]{:S(2)}, u32[]{:S(2)}) collective-permute-start(bf16[512,256]{1,0:T(8,128)(2,1)S(1)} %get-tuple-element.27), channel_id=1, source_target_pairs={{16,0},{17,1},{18,2},{19,3},{20,4},{21,5},{22,6},{23,7},{24,8},{25... | collective-permute-start | bytes 786440 | tf_op jit(solution)/shard_map/ppermute | solution.py:63
  95.5 9.5 %collective-permute-start.18 = (bf16[512,256]{1,0:T(8,128)(2,1)S(1)}, bf16[512,256]{1,0:T(8,128)(2,1)S(1)}, u32[]{:S(2)}, u32[]{:S(2)}) collective-permute-start(bf16[512,256]{1,0:T(8,128)(2,1)S(1)} %get-tuple-element.28), channel_id=1, source_target_pairs={{0,16},{1,17},{2,18},{3,19},{4,20},{5,21},{6,22},{7,23},{8,24},{9,... | collective-permute-start | bytes 786440 | tf_op jit(solution)/shard_map/ppermute | solution.py:63
  97.8 8.3 %collective-permute-start.11 = (bf16[1024,256]{1,0:T(8,128)(2,1)S(1)}, bf16[1024,256]{1,0:T(8,128)(2,1)S(1)}, u32[]{:S(2)}, u32[]{:S(2)}) collective-permute-start(bf16[1024,256]{1,0:T(8,128)(2,1)S(1)} %pad_maximum_fusion), channel_id=1, source_target_pairs={{0,1},{1,0},{2,3},{3,2},{4,5},{5,4},{6,7},{7,6},{8,9},{9,8},{10,11... | collective-permute-start | bytes 1572872 | tf_op jit(solution)/shard_map/ppermute | solution.py:63

commit v3 on v1

v3 whole, which is shorter than its diff:
```python
import jax
import jax.numpy as jnp
from jax import lax
from jax.experimental import pallas as pl
from jax.experimental.pallas import tpu as pltpu
from jax.sharding import Mesh
from jax.sharding import PartitionSpec as P


BLK = 256
X, Y, Z = 4, 8, 8
AXES = ("prow_0", "prow_1", "pcol")
PROW = ("prow_0", "prow_1")
ROW_CAP, COL_CAP = 2, 4


def device(x, y, z, core):
    return ((x % X) * Y + y % Y) * (2 * Z) + (z % Z) * 2 + core


def plane_pairs(pairs):
    out = []
    for (xs, ys), (xt, yt) in pairs:
        for z in range(Z):
            for core in range(2):
                out.append((device(xs, ys, z, core), device(xt, yt, z, core)))
                out.append((device(xs, 1 - ys, z, core), device(xt, 1 - yt, z, core)))
    return out


def line_pairs(pairs):
    return [
        (device(x, y, s, core), device(x, y, t, core))
        for s, t in pairs
        for x in range(X)
        for y in range(Y)
        for core in range(2)
    ]


SPREAD = [
    [plane_pairs([((0, 0), h)]) for h in ((2, 6), (1, 0), (3, 0))],
    [plane_pairs([((0, 0), (0, 6)), ((1, 0), (1, 6)), ((3, 0), (3, 6)), ((2, 6), (2, 0))])],
    [plane_pairs([((x, 0), (x, 2)) for x in range(X)] + [((x, 6), (x, 4)) for x in range(X)])],
]
UP = [
    (device(x, y, z, c), device(x, y + 1, z, c))
    for x in range(X) for y in range(Y) for z in range(Z) for c in range(2)
]
DOWN = [(t, s) for s, t in UP]
LINE_1 = [line_pairs([(0, 3)]), line_pairs([(0, 5)])]
LINE_2 = [line_pairs([(0, 1), (3, 4), (5, 6)]), line_pairs([(0, 7), (3, 2)])]
SWAP = [
    (device(x, y, z, c), device(x, y, z, 1 - c))
    for x in range(X) for y in range(Y) for z in range(Z) for c in range(2)
]


def send(value, pairs):
    return lax.ppermute(value, AXES, pairs)


def slots(flags, capacity):
    count = jnp.int32(0)
    slot_of = []
    where = [jnp.int32(0)] * capacity
    for position, flag in enumerate(flags):
        one = flag.astype(jnp.int32)
        slot_of.append(jnp.minimum(count, capacity - 1))
        where = [
            jnp.where(flag & (count == s), jnp.int32(position), w) for s, w in enumerate(where)
        ]
        count = count + one
    return slot_of, where, count


def pack_kernel(here, row_pattern, col_pattern, matrix, first_out, rest_out, panel_out, sems):
    prow, pcol = here[0], here[1]
    row_blocks, col_blocks = matrix.shape[0] // BLK, matrix.shape[1] // BLK
    k = (prow == 1).astype(jnp.int32)
    cols = [col_pattern[k, pcol * col_blocks + j] > 0 for j in range(col_blocks)]
    _, col_at, _ = slots(cols, COL_CAP)
    copies = []
    for s in range(COL_CAP):
        source = matrix.at[pl.ds(0, BLK), pl.ds(pl.multiple_of(col_at[s] * BLK, BLK), BLK)]
        target = first_out if s == 0 else rest_out.at[pl.ds((s - 1) * BLK, BLK)]
        copies.append(pltpu.make_async_copy(source, target, sems.at[s]))
    rows = [row_pattern[1, prow * row_blocks + i] > 0 for i in range(row_blocks)]
    _, row_at, count = slots(rows, ROW_CAP)
    for s in range(ROW_CAP):
        source = matrix.at[pl.ds(pl.multiple_of(row_at[s] * BLK, BLK), BLK), pl.ds(0, BLK)]
        target = panel_out.at[pl.ds(s * BLK, BLK)]
        copies.append(pltpu.make_async_copy(source, target, sems.at[COL_CAP + s]))
    for copy in copies:
        copy.start()
    for copy in copies:
        copy.wait()
    own = (pcol == 1).astype(jnp.int32)
    for s in range(ROW_CAP):
        stored = (count > s) & (row_pattern[own, prow * row_blocks + row_at[s]] > 0)

        @pl.when(jnp.logical_not(stored))
        def _(s=s):
            panel_out[pl.ds(s * BLK, BLK), :] = jnp.zeros((BLK, BLK), jnp.bfloat16)


def pack(here, row_pattern, col_pattern, matrix):
    smem = pl.BlockSpec(memory_space=pltpu.SMEM)
    vmem = pl.BlockSpec(memory_space=pltpu.VMEM)
    return pl.pallas_call(
        pack_kernel,
        in_specs=[smem, smem, smem, pl.BlockSpec(memory_space=pl.ANY)],
        out_specs=[vmem] * 3,
        out_shape=[
            vmem_shape(BLK, BLK),
            vmem_shape((COL_CAP - 1) * BLK, BLK),
            vmem_shape(ROW_CAP * BLK, BLK),
        ],
        scratch_shapes=[pltpu.SemaphoreType.DMA((COL_CAP + ROW_CAP,))],
        name="pack",
    )(here, row_pattern, col_pattern, matrix)


def in_vmem(*values):
    return [pltpu.with_memory_space_constraint(v, pltpu.VMEM) for v in values]


def vmem_shape(*shape):
    return pltpu.VMEM(shape, jnp.bfloat16)


def halves(value):
    high = value.astype(jnp.bfloat16)
    return high, (value - high.astype(jnp.float32)).astype(jnp.bfloat16)


def dot(a, b):
    return jnp.dot(a, b, preferred_element_type=jnp.float32)


def panels_kernel(here, row_pattern, mine, other, lower_0, lower_1):
    prow, core_0 = here[0], here[1] % 2 == 0
    row_blocks = row_pattern.shape[1] // (X * Y)

    def of_core(core, block):
        at = pl.ds(block * BLK, BLK)
        own = core_0 if core == 0 else jnp.logical_not(core_0)
        return jnp.where(own, mine[at, :], other[at, :])

    i = lax.broadcasted_iota(jnp.int32, (BLK, BLK), 0)
    j = lax.broadcasted_iota(jnp.int32, (BLK, BLK), 1)
    diagonal = i == j
    powers, sums, scales = [], [], []
    for n in range(2):
        p = of_core(n, n).astype(jnp.float32)
        d = jnp.where(diagonal, p, 0.0)
        by_row = jnp.sum(d, axis=1, keepdims=True)
        scales.append(1.0 / jnp.sum(d, axis=0, keepdims=True))
        r = jnp.where(diagonal, 0.0, -p / by_row)
        powers.append(r)
        sums.append(jnp.where(diagonal, 1.0, r))
    for step in range(8):
        for n in range(2):
            high, low = halves(powers[n])
            if step > 0:
                sum_high, sum_low = halves(sums[n])
                sums[n] = sums[n] + (
                    dot(high, sum_high) + (dot(high, sum_low) + dot(low, sum_high))
                )
            if step < 7:
                powers[n] = dot(high, high) + (dot(high, low) + dot(low, high))
    rows = [row_pattern[1, prow * row_blocks + b] > 0 for b in range(row_blocks)]
    _, row_at, _ = slots(rows, ROW_CAP)
    inverses = [halves(sums[n] * scales[n]) for n in range(2)]
    upper_01 = of_core(1, 0)
    for s in range(ROW_CAP):
        at = pl.ds(s * BLK, BLK)
        panel = of_core(0, 2 + s)
        high, low = inverses[0]
        lower = dot(panel, high) + dot(panel, low)
        done = (prow == 0) & (row_at[s] == 0)
        lower = jnp.where(done, 0.0, lower).astype(jnp.bfloat16)
        lower_0[at, :] = lower
        panel = of_core(1, 2 + s).astype(jnp.float32) - dot(lower, upper_01)
        panel = panel.astype(jnp.bfloat16)
        high, low = inverses[1]
        lower = dot(panel, high) + dot(panel, low)
        done = (prow <= 1) & (row_at[s] == 0)
        lower_1[at, :] = jnp.where(done, 0.0, lower).astype(jnp.bfloat16)


def panels(here, row_pattern, mine, other):
    smem = pl.BlockSpec(memory_space=pltpu.SMEM)
    vmem = pl.BlockSpec(memory_space=pltpu.VMEM)
    shape = vmem_shape(ROW_CAP * BLK, BLK)
    return pl.pallas_call(
        panels_kernel,
        in_specs=[smem, smem] + [vmem] * 2,
        out_specs=[vmem] * 2,
        out_shape=[shape, shape],
        cost_estimate=pl.CostEstimate(
            flops=120 * BLK**3, bytes_accessed=24 * BLK * BLK, transcendentals=0
        ),
        name="panels",
    )(here, row_pattern, *in_vmem(mine, other))


def update_kernel(
    here, row_pattern, col_pattern, source, lower_0, lower_1,
    first_held, first_came, rest_held, up_came, down_came, out, upper,
):
    prow, pcol = here[0], here[1]
    i = pl.program_id(0)
    row_blocks = pl.num_programs(0)
    col_blocks = source.shape[1] // BLK

    @pl.when(i == 0)
    def _():
        even = prow % 2 == 0
        for s in range(COL_CAP):
            rest = pl.ds((s - 1) * BLK, BLK)
            held = first_held[...] if s == 0 else rest_held[rest, :]
            came = (
                first_came[...]
                if s == 0
                else up_came[...]
                if s == COL_CAP - 1
                else down_came[rest, :]
            )
            upper[0, pl.ds(s * BLK, BLK), :] = jnp.where(even, held, came)
            upper[1, pl.ds(s * BLK, BLK), :] = jnp.where(even, came, held)

    row = prow * row_blocks + i
    slot = jnp.int32(0)
    for b in range(2):
        slot = slot + ((i > b) & (row_pattern[1, prow * row_blocks + b] > 0)).astype(jnp.int32)
    rows = pl.ds(pl.multiple_of(jnp.minimum(slot, ROW_CAP - 1) * BLK, BLK), BLK)
    stored = [row_pattern[k, row] > 0 for k in range(2)]
    first = i == 0
    done = [first & (prow == 0), first & (prow <= 1)]
    lower = [lower_0, lower_1]
    flags = [[col_pattern[k, pcol * col_blocks + j] > 0 for j in range(col_blocks)] for k in (0, 1)]
    col_slot = [slots(f, COL_CAP)[0] for f in flags]
    for j in range(col_blocks):
        columns = pl.ds(j * BLK, BLK)
        dropped = jnp.bool_(False)
        used = []
        for k in range(2):
            dropped = dropped | (first & (prow == k) & jnp.logical_not(flags[k][j]))
            use = stored[k] & jnp.logical_not(done[k]) & flags[k][j]
            if j == 0:
                dropped = dropped | ((pcol == k) & jnp.logical_not(stored[k]))
                use = use & (pcol > k)
            used.append(use)
        other = used[0] | used[1]

        def product(k, j=j):
            at = pl.ds(pl.multiple_of(col_slot[k][j] * BLK, BLK), BLK)
            return dot(lower[k][rows, :], upper[k, at, :])

        def kept(columns=columns, dropped=dropped):
            value = source[:, columns]
            return jnp.where(dropped, jnp.zeros_like(value), value)

        def reduced(value, k, j=j):
            return (value.astype(jnp.float32) - product(k, j)).astype(jnp.bfloat16)

        @pl.when(jnp.logical_not(other))
        def _(columns=columns, kept=kept):
            out[:, columns] = kept()

        @pl.when(used[0] & jnp.logical_not(used[1]))
        def _(columns=columns, kept=kept, reduced=reduced):
            out[:, columns] = reduced(kept(), 0)

        @pl.when(used[1] & jnp.logical_not(used[0]))
        def _(columns=columns, kept=kept, reduced=reduced):
            out[:, columns] = reduced(kept(), 1)

        @pl.when(used[0] & used[1])
        def _(columns=columns, kept=kept, reduced=reduced):
            out[:, columns] = reduced(reduced(kept(), 0), 1)

        if j == 0:
            for k in range(2):

                @pl.when((pcol == k) & jnp.logical_not(done[k]))
                def _(k=k, columns=columns):
                    value = lower[k][rows, :]
                    out[:, columns] = jnp.where(stored[k], value, jnp.zeros_like(value))


def update(here, row_pattern, col_pattern, matrix, *blocks):
    row_blocks = matrix.shape[0] // BLK
    breadth = matrix.shape[1]
    smem = pl.BlockSpec(memory_space=pltpu.SMEM)
    vmem = pl.BlockSpec(memory_space=pltpu.VMEM)
    strip = pl.BlockSpec((BLK, breadth), lambda i: (i, 0))
    return pl.pallas_call(
        update_kernel,
        grid=(row_blocks,),
        in_specs=[smem] * 3 + [strip] + [vmem] * 7,
        out_specs=strip,
        out_shape=jax.ShapeDtypeStruct(matrix.shape, matrix.dtype),
        scratch_shapes=[pltpu.VMEM((2, COL_CAP * BLK, BLK), jnp.bfloat16)],
        name="update",
    )(here, row_pattern, col_pattern, matrix, *in_vmem(*blocks))


def shards(matrix, row_pattern, col_pattern):
    prow = lax.axis_index(PROW).astype(jnp.int32)
    pcol = lax.axis_index("pcol").astype(jnp.int32)
    even = prow % 2 == 0
    here = jnp.where(jnp.arange(2) == 0, prow, pcol)
    first, rest, panel = pack(here, row_pattern, col_pattern, matrix)
    zero = jnp.zeros((), jnp.bfloat16)

    def tree(value, root, levels):
        held = jnp.where(root, value, zero)
        for level, letter in zip(levels, "abc"):
            source = value if letter == "a" else held
            for pairs in level:
                held = held + send(source, pairs)
        return held

    first_held = tree(first, prow <= 1, SPREAD)
    first_came = send(first_held, UP)
    rest_held = tree(rest, prow <= 1, SPREAD)
    down_came = send(rest_held[: 2 * BLK], DOWN)
    up_came = send(rest_held[2 * BLK :], UP)
    panel = tree(panel, pcol <= 1, [LINE_1, LINE_2])
    pivots = jnp.concatenate(
        [
            jnp.where(even, first_held, first_came),
            jnp.where(even, first_came, first_held),
        ],
        axis=0,
    )
    pivots = tree(pivots, pcol <= 1, [LINE_1, LINE_2])
    mine = jnp.concatenate([pivots, panel], axis=0)
    other = send(mine, SWAP)
    lower_0, lower_1 = panels(here, row_pattern, mine, other)
    return update(
        here, row_pattern, col_pattern, matrix, lower_0, lower_1,
        first_held, first_came, rest_held, up_came, down_came,
    )


def solution(mesh):
    torus = Mesh(mesh.devices.reshape(X, Y, mesh.shape["pcol"]), AXES)
    placed = (P(PROW, "pcol"), P(), P())
    return jax.shard_map(
        shards, mesh=torus, in_specs=placed, out_specs=P(PROW, "pcol"), check_vma=False
    )
```

time: 124 us -> 105 us (0.85)
  the two profiles are of different devices: /device:TPU:4 before, /device:TPU:24 now
where the time goes in v3:
time: 105 us; the launch traced here: 104 us
  starting transfers between devices  58.1 us (55%)
  waiting for transfers between devices  32.9 us (31%)
  Pallas kernels  11.7 us (11%)
  other arithmetic  1.22 us (1%)
    ppermute x22, starting transfers between devices, send(): return lax.ppermute(value, AXES, pairs)  58.1 us
    ppermute x22, waiting for transfers between devices, send(): return lax.ppermute(value, AXES, pairs)  32.9 us
    pallas_call x1, Pallas kernels, update(): pl.pallas_call(update_kernel, grid=(row_blocks,), in_specs=[smem] * 3 + [...  4.87 us
    pallas_call x1, Pallas kernels, panels(): pl.pallas_call(panels_kernel, in_specs=[smem, smem] + [vmem] * 2, out_spe...  4.67 us
    pallas_call x1, Pallas kernels, pack(): pl.pallas_call(pack_kernel, in_specs=[smem, smem, smem, pl.BlockSpec(memo...  2.2 us
  transfers between devices with their start and end apart: 22, of which 8 were waited for; matrix products, arithmetic and copies ran while one was open for 1% of the time, Pallas kernels for 4%

profile of v3, /device:TPU:24, one launch (start us, length us, event | category | flops | bytes accessed | tf_op | source)
XLA Modules:
  0.0 104.4 jit_solution(1778956067756948171)
XLA Ops:
  0.5 2.2 %pack.1 = (bf16[256,256]{1,0:T(8,128)(2,1)S(1)}, bf16[768,256]{1,0:T(8,128)(2,1)S(1)}, bf16[512,256]{1,0:T(8,128)(2,1)S(1)}) custom-call(s32[2]{0:T(128)} %compare_select_fusion.here, s32[2,96]{1,0:T(2,128)} %row_pattern.5, s32[2,96]{1,0:T(2,128)} %col_pattern.3, bf16[768,1536]{1,0:T(8,128)(2,1)} %source.1), custom_call_target="tpu_custom_call" | custom-call | tf_op jit(solution)/shard_map/pack/pallas_call | solution.py:110
  2.7 0.7 collective-permute-start.2
  4.1 0.7 collective-permute-start
  4.8 1.3 %collective-permute-start.3 = (bf16[256,256]{1,0:T(8,128)(2,1)S(1)}, bf16[256,256]{1,0:T(8,128)(2,1)S(1)}, u32[]{:S(2)}, u32[]{:S(2)}) collective-permute-start(bf16[256,256]{1,0:T(8,128)(2,1)S(1)} %add_add_fusion.5), channel_id=1, source_target_pairs={{0,96},{16,48},{1,97},{17,49},{2,98},{18,50},{3,99},{19,51},{4,100... | collective-permute-start | bytes 393224 | tf_op jit(solution)/shard_map/ppermute | solution.py:60
  6.1 12.1 %collective-permute-done.3 = bf16[256,256]{1,0:T(8,128)(2,1)S(1)} collective-permute-done((bf16[256,256]{1,0:T(8,128)(2,1)S(1)}, bf16[256,256]{1,0:T(8,128)(2,1)S(1)}, u32[]{:S(2)}, u32[]{:S(2)}) %collective-permute-start.3) | collective-permute-done | bytes 131104 | tf_op jit(solution)/shard_map/ppermute | solution.py:60
  18.2 1.3 %collective-permute-start.4 = (bf16[256,256]{1,0:T(8,128)(2,1)S(1)}, bf16[256,256]{1,0:T(8,128)(2,1)S(1)}, u32[]{:S(2)}, u32[]{:S(2)}) collective-permute-start(bf16[256,256]{1,0:T(8,128)(2,1)S(1)} %add.66), channel_id=1, source_target_pairs={{0,32},{16,112},{1,33},{17,113},{2,34},{18,114},{3,35},{19,115},{4... | collective-permute-start | bytes 393224 | tf_op jit(solution)/shard_map/ppermute | solution.py:60
  19.5 2.5 %collective-permute-done.4 = bf16[256,256]{1,0:T(8,128)(2,1)S(1)} collective-permute-done((bf16[256,256]{1,0:T(8,128)(2,1)S(1)}, bf16[256,256]{1,0:T(8,128)(2,1)S(1)}, u32[]{:S(2)}, u32[]{:S(2)}) %collective-permute-start.4) | collective-permute-done | bytes 131104 | tf_op jit(solution)/shard_map/ppermute | solution.py:60
  22.1 8.7 %collective-permute-start.5 = (bf16[256,256]{1,0:T(8,128)(2,1)S(1)}, bf16[256,256]{1,0:T(8,128)(2,1)S(1)}, u32[]{:S(2)}, u32[]{:S(2)}) collective-permute-start(bf16[256,256]{1,0:T(8,128)(2,1)S(1)} %add.67.first_held), channel_id=1, source_target_pairs={{0,16},{1,17},{2,18},{3,19},{4,20},{5,21},{6,22},{7,23},{8,24},{9,... | collective-permute-start | bytes 393224 | tf_op jit(solution)/shard_map/ppermute | solution.py:60
  30.7 10.8 %collective-permute-start.11 = (bf16[512,256]{1,0:T(8,128)(2,1)S(1)}, bf16[512,256]{1,0:T(8,128)(2,1)S(1)}, u32[]{:S(2)}, u32[]{:S(2)}) collective-permute-start(bf16[512,256]{1,0:T(8,128)(2,1)S(1)} %get-tuple-element.11), channel_id=1, source_target_pairs={{0,10},{1,11},{16,26},{17,27},{32,42},{33,43},{48,58},{49,59},{64,... | collective-permute-start | bytes 786440 | tf_op jit(solution)/shard_map/ppermute | solution.py:60
  41.6 1.3 %collective-permute-start.10 = (bf16[512,256]{1,0:T(8,128)(2,1)S(1)}, bf16[512,256]{1,0:T(8,128)(2,1)S(1)}, u32[]{:S(2)}, u32[]{:S(2)}) collective-permute-start(bf16[512,256]{1,0:T(8,128)(2,1)S(1)} %get-tuple-element.11), channel_id=1, source_target_pairs={{0,6},{1,7},{16,22},{17,23},{32,38},{33,39},{48,54},{49,55},{64,70... | collective-permute-start | bytes 786440 | tf_op jit(solution)/shard_map/ppermute | solution.py:60
  43.0 1.3 %collective-permute-start.6 = (bf16[512,256]{1,0:T(8,128)(2,1)S(1)}, bf16[512,256]{1,0:T(8,128)(2,1)S(1)}, u32[]{:S(2)}, u32[]{:S(2)}) collective-permute-start(bf16[512,256]{1,0:T(8,128)(2,1)S(1)} %pad_maximum_fusion.1), channel_id=1, source_target_pairs={{0,6},{1,7},{16,22},{17,23},{32,38},{33,39},{48,54},{49,55},{64,70... | collective-permute-start | bytes 786440 | tf_op jit(solution)/shard_map/ppermute | solution.py:60
  44.3 1.3 %collective-permute-start.7 = (bf16[512,256]{1,0:T(8,128)(2,1)S(1)}, bf16[512,256]{1,0:T(8,128)(2,1)S(1)}, u32[]{:S(2)}, u32[]{:S(2)}) collective-permute-start(bf16[512,256]{1,0:T(8,128)(2,1)S(1)} %pad_maximum_fusion.1), channel_id=1, source_target_pairs={{0,10},{1,11},{16,26},{17,27},{32,42},{33,43},{48,58},{49,59},{64,... | collective-permute-start | bytes 786440 | tf_op jit(solution)/shard_map/ppermute | solution.py:60
  45.6 0.7 collective-permute-start.17
  46.3 1.2 %collective-permute-done.11 = bf16[512,256]{1,0:T(8,128)(2,1)S(1)} collective-permute-done((bf16[512,256]{1,0:T(8,128)(2,1)S(1)}, bf16[512,256]{1,0:T(8,128)(2,1)S(1)}, u32[]{:S(2)}, u32[]{:S(2)}) %collective-permute-start.11) | collective-permute-done | bytes 262176 | tf_op jit(solution)/shard_map/ppermute | solution.py:60
  47.5 0.7 collective-permute-start.16
  48.2 0.7 collective-permute-start.15
  49.0 3.1 %collective-permute-done.6 = bf16[512,256]{1,0:T(8,128)(2,1)S(1)} collective-permute-done((bf16[512,256]{1,0:T(8,128)(2,1)S(1)}, bf16[512,256]{1,0:T(8,128)(2,1)S(1)}, u32[]{:S(2)}, u32[]{:S(2)}) %collective-permute-start.6) | collective-permute-done | bytes 262176 | tf_op jit(solution)/shard_map/ppermute | solution.py:60
  52.1 1.3 %collective-permute-start.13 = (bf16[512,256]{1,0:T(8,128)(2,1)S(1)}, bf16[512,256]{1,0:T(8,128)(2,1)S(1)}, u32[]{:S(2)}, u32[]{:S(2)}) collective-permute-start(bf16[512,256]{1,0:T(8,128)(2,1)S(1)} %add_add_fusion.2), channel_id=1, source_target_pairs={{0,14},{1,15},{16,30},{17,31},{32,46},{33,47},{48,62},{49,63},{64,... | collective-permute-start | bytes 786440 | tf_op jit(solution)/shard_map/ppermute | solution.py:60
  53.4 1.3 %collective-permute-start.12 = (bf16[512,256]{1,0:T(8,128)(2,1)S(1)}, bf16[512,256]{1,0:T(8,128)(2,1)S(1)}, u32[]{:S(2)}, u32[]{:S(2)}) collective-permute-start(bf16[512,256]{1,0:T(8,128)(2,1)S(1)} %add_add_fusion.2), channel_id=1, source_target_pairs={{0,2},{1,3},{16,18},{17,19},{32,34},{33,35},{48,50},{49,51},{64,66... | collective-permute-start | bytes 786440 | tf_op jit(solution)/shard_map/ppermute | solution.py:60
  54.8 1.3 %collective-permute-start.9 = (bf16[512,256]{1,0:T(8,128)(2,1)S(1)}, bf16[512,256]{1,0:T(8,128)(2,1)S(1)}, u32[]{:S(2)}, u32[]{:S(2)}) collective-permute-start(bf16[512,256]{1,0:T(8,128)(2,1)S(1)} %add_add_fusion.4), channel_id=1, source_target_pairs={{0,14},{1,15},{16,30},{17,31},{32,46},{33,47},{48,62},{49,63},{64,... | collective-permute-start | bytes 786440 | tf_op jit(solution)/shard_map/ppermute | solution.py:60
  56.2 1.3 %collective-permute-start.8 = (bf16[512,256]{1,0:T(8,128)(2,1)S(1)}, bf16[512,256]{1,0:T(8,128)(2,1)S(1)}, u32[]{:S(2)}, u32[]{:S(2)}) collective-permute-start(bf16[512,256]{1,0:T(8,128)(2,1)S(1)} %add_add_fusion.4), channel_id=1, source_target_pairs={{0,2},{1,3},{16,18},{17,19},{32,34},{33,35},{48,50},{49,51},{64,66... | collective-permute-start | bytes 786440 | tf_op jit(solution)/shard_map/ppermute | solution.py:60
  57.6 1.3 %collective-permute-start.18 = (bf16[768,256]{1,0:T(8,128)(2,1)S(1)}, bf16[768,256]{1,0:T(8,128)(2,1)S(1)}, u32[]{:S(2)}, u32[]{:S(2)}) collective-permute-start(bf16[768,256]{1,0:T(8,128)(2,1)S(1)} %add_add_fusion), channel_id=1, source_target_pairs={{0,96},{16,48},{1,97},{17,49},{2,98},{18,50},{3,99},{19,51},{4,100... | collective-permute-start | bytes 1179656 | tf_op jit(solution)/shard_map/ppermute | solution.py:60
  58.9 1.7 %collective-permute-done.9 = bf16[512,256]{1,0:T(8,128)(2,1)S(1)} collective-permute-done((bf16[512,256]{1,0:T(8,128)(2,1)S(1)}, bf16[512,256]{1,0:T(8,128)(2,1)S(1)}, u32[]{:S(2)}, u32[]{:S(2)}) %collective-permute-start.9) | collective-permute-done | bytes 262176 | tf_op jit(solution)/shard_map/ppermute | solution.py:60
  60.6 0.7 collective-permute-done.8
  61.5 1.9 %collective-permute-start.14 = (bf16[1024,256]{1,0:T(8,128)(2,1)S(1)}, bf16[1024,256]{1,0:T(8,128)(2,1)S(1)}, u32[]{:S(2)}, u32[]{:S(2)}) collective-permute-start(bf16[1024,256]{1,0:T(8,128)(2,1)S(1)} %pad_maximum_fusion.mine), channel_id=1, source_target_pairs={{0,1},{1,0},{2,3},{3,2},{4,5},{5,4},{6,7},{7,6},{8,9},{9,8},{10,11... | collective-permute-start | bytes 1572872 | tf_op jit(solution)/shard_map/ppermute | solution.py:60
  63.4 6.3 %collective-permute-done.18 = bf16[768,256]{1,0:T(8,128)(2,1)S(1)} collective-permute-done((bf16[768,256]{1,0:T(8,128)(2,1)S(1)}, bf16[768,256]{1,0:T(8,128)(2,1)S(1)}, u32[]{:S(2)}, u32[]{:S(2)}) %collective-permute-start.18) | collective-permute-done | bytes 393248 | tf_op jit(solution)/shard_map/ppermute | solution.py:60
  69.8 1.3 %collective-permute-start.19 = (bf16[768,256]{1,0:T(8,128)(2,1)S(1)}, bf16[768,256]{1,0:T(8,128)(2,1)S(1)}, u32[]{:S(2)}, u32[]{:S(2)}) collective-permute-start(bf16[768,256]{1,0:T(8,128)(2,1)S(1)} %add.79), channel_id=1, source_target_pairs={{0,32},{16,112},{1,33},{17,113},{2,34},{18,114},{3,35},{19,115},{4... | collective-permute-start | bytes 1179656 | tf_op jit(solution)/shard_map/ppermute | solution.py:60
  71.1 5.3 %collective-permute-done.19 = bf16[768,256]{1,0:T(8,128)(2,1)S(1)} collective-permute-done((bf16[768,256]{1,0:T(8,128)(2,1)S(1)}, bf16[768,256]{1,0:T(8,128)(2,1)S(1)}, u32[]{:S(2)}, u32[]{:S(2)}) %collective-permute-start.19) | collective-permute-done | bytes 393248 | tf_op jit(solution)/shard_map/ppermute | solution.py:60
  76.5 14.6 %collective-permute-start.21 = (bf16[512,256]{1,0:T(8,128)(2,1)S(1)}, bf16[512,256]{1,0:T(8,128)(2,1)S(1)}, u32[]{:S(2)}, u32[]{:S(2)}) collective-permute-start(bf16[512,256]{1,0:T(8,128)(2,1)S(1)} %slice.9), channel_id=1, source_target_pairs={{16,0},{17,1},{18,2},{19,3},{20,4},{21,5},{22,6},{23,7},{24,8},{25... | collective-permute-start | bytes 786440 | tf_op jit(solution)/shard_map/ppermute | solution.py:60
  91.1 3.7 %collective-permute-start.20 = (bf16[256,256]{1,0:T(8,128)(2,1)S(1)}, bf16[256,256]{1,0:T(8,128)(2,1)S(1)}, u32[]{:S(2)}, u32[]{:S(2)}) collective-permute-start(bf16[256,256]{1,0:T(8,128)(2,1)S(1)} %slice.8), channel_id=1, source_target_pairs={{0,16},{1,17},{2,18},{3,19},{4,20},{5,21},{6,22},{7,23},{8,24},{9,... | collective-permute-start | bytes 393224 | tf_op jit(solution)/shard_map/ppermute | solution.py:60
  94.9 4.7 %panels.1 = (bf16[512,256]{1,0:T(8,128)(2,1)S(1)}, bf16[512,256]{1,0:T(8,128)(2,1)S(1)}) custom-call(s32[2]{0:T(128)} %compare_select_fusion.here, s32[2,96]{1,0:T(2,128)} %row_pattern.5, bf16[1024,256]{1,0:T(8,128)(2,1)S(1)} %pad_maximum_fusion.mine, bf16[1024,256]{1,0:T(8,128)(2,1)S(1)} %collective-permute-done.14.other), custom_call_target="tpu_custom_call" | custom-call | flops 2013265920 | bytes 1572864 | tf_op jit(solution)/shard_map/panels/pallas_call | solution.py:196
  99.6 4.9 %update.1 = bf16[768,1536]{1,0:T(8,128)(2,1)} custom-call(s32[2]{0:T(128)} %compare_select_fusion.here, s32[2,96]{1,0:T(2,128)} %row_pattern.5, s32[2,96]{1,0:T(2,128)} %col_pattern.3, bf16[768,1536]{1,0:T(8,128)(2,1)} %source.1, bf16[512,256]{1,0:T(8,128)(2,1)S(1)} %get-tuple-element.12.lower_0, bf16[512,256]{1,0:T(8,128)(2,1)S(1)} %get-tuple-element.13.lower_1, ...), custom_call_target="tpu_custom_call" | custom-call | tf_op jit(solution)/shard_map/update/pallas_call | solution.py:299
  (31 shorter events, 2.0 us)
Async XLA Ops:
  2.7 2.0 %collective-permute-start.2 = (bf16[256,256]{1,0:T(8,128)(2,1)S(1)}, bf16[256,256]{1,0:T(8,128)(2,1)S(1)}, u32[]{:S(2)}, u32[]{:S(2)}) collective-permute-start(bf16[256,256]{1,0:T(8,128)(2,1)S(1)} %get-tuple-element.10), channel_id=1, source_target_pairs={{0,384},{16,400},{1,385},{17,401},{2,386},{18,402},{3,387},{19,403... | collective-permute-start | bytes 393224 | tf_op jit(solution)/shard_map/ppermute | solution.py:60
  3.4 1.4 %collective-permute-start.1 = (bf16[256,256]{1,0:T(8,128)(2,1)S(1)}, bf16[256,256]{1,0:T(8,128)(2,1)S(1)}, u32[]{:S(2)}, u32[]{:S(2)}) collective-permute-start(bf16[256,256]{1,0:T(8,128)(2,1)S(1)} %get-tuple-element.10), channel_id=1, source_target_pairs={{0,128},{16,144},{1,129},{17,145},{2,130},{18,146},{3,131},{19,147... | collective-permute-start | bytes 393224 | tf_op jit(solution)/shard_map/ppermute | solution.py:60
  4.1 0.7 collective-permute-start
  4.8 13.4 %collective-permute-start.3 = (bf16[256,256]{1,0:T(8,128)(2,1)S(1)}, bf16[256,256]{1,0:T(8,128)(2,1)S(1)}, u32[]{:S(2)}, u32[]{:S(2)}) collective-permute-start(bf16[256,256]{1,0:T(8,128)(2,1)S(1)} %add_add_fusion.5), channel_id=1, source_target_pairs={{0,96},{16,48},{1,97},{17,49},{2,98},{18,50},{3,99},{19,51},{4,100... | collective-permute-start | bytes 393224 | tf_op jit(solution)/shard_map/ppermute | solution.py:60
  18.2 3.8 %collective-permute-start.4 = (bf16[256,256]{1,0:T(8,128)(2,1)S(1)}, bf16[256,256]{1,0:T(8,128)(2,1)S(1)}, u32[]{:S(2)}, u32[]{:S(2)}) collective-permute-start(bf16[256,256]{1,0:T(8,128)(2,1)S(1)} %add.66), channel_id=1, source_target_pairs={{0,32},{16,112},{1,33},{17,113},{2,34},{18,114},{3,35},{19,115},{4... | collective-permute-start | bytes 393224 | tf_op jit(solution)/shard_map/ppermute | solution.py:60
  22.1 20.8 %collective-permute-start.5 = (bf16[256,256]{1,0:T(8,128)(2,1)S(1)}, bf16[256,256]{1,0:T(8,128)(2,1)S(1)}, u32[]{:S(2)}, u32[]{:S(2)}) collective-permute-start(bf16[256,256]{1,0:T(8,128)(2,1)S(1)} %add.67.first_held), channel_id=1, source_target_pairs={{0,16},{1,17},{2,18},{3,19},{4,20},{5,21},{6,22},{7,23},{8,24},{9,... | collective-permute-start | bytes 393224 | tf_op jit(solution)/shard_map/ppermute | solution.py:60
  30.7 16.8 %collective-permute-start.11 = (bf16[512,256]{1,0:T(8,128)(2,1)S(1)}, bf16[512,256]{1,0:T(8,128)(2,1)S(1)}, u32[]{:S(2)}, u32[]{:S(2)}) collective-permute-start(bf16[512,256]{1,0:T(8,128)(2,1)S(1)} %get-tuple-element.11), channel_id=1, source_target_pairs={{0,10},{1,11},{16,26},{17,27},{32,42},{33,43},{48,58},{49,59},{64,... | collective-permute-start | bytes 786440 | tf_op jit(solution)/shard_map/ppermute | solution.py:60
  41.6 6.7 %collective-permute-start.10 = (bf16[512,256]{1,0:T(8,128)(2,1)S(1)}, bf16[512,256]{1,0:T(8,128)(2,1)S(1)}, u32[]{:S(2)}, u32[]{:S(2)}) collective-permute-start(bf16[512,256]{1,0:T(8,128)(2,1)S(1)} %get-tuple-element.11), channel_id=1, source_target_pairs={{0,6},{1,7},{16,22},{17,23},{32,38},{33,39},{48,54},{49,55},{64,70... | collective-permute-start | bytes 786440 | tf_op jit(solution)/shard_map/ppermute | solution.py:60
  43.0 9.1 %collective-permute-start.6 = (bf16[512,256]{1,0:T(8,128)(2,1)S(1)}, bf16[512,256]{1,0:T(8,128)(2,1)S(1)}, u32[]{:S(2)}, u32[]{:S(2)}) collective-permute-start(bf16[512,256]{1,0:T(8,128)(2,1)S(1)} %pad_maximum_fusion.1), channel_id=1, source_target_pairs={{0,6},{1,7},{16,22},{17,23},{32,38},{33,39},{48,54},{49,55},{64,70... | collective-permute-start | bytes 786440 | tf_op jit(solution)/shard_map/ppermute | solution.py:60
  44.3 9.1 %collective-permute-start.7 = (bf16[512,256]{1,0:T(8,128)(2,1)S(1)}, bf16[512,256]{1,0:T(8,128)(2,1)S(1)}, u32[]{:S(2)}, u32[]{:S(2)}) collective-permute-start(bf16[512,256]{1,0:T(8,128)(2,1)S(1)} %pad_maximum_fusion.1), channel_id=1, source_target_pairs={{0,10},{1,11},{16,26},{17,27},{32,42},{33,43},{48,58},{49,59},{64,... | collective-permute-start | bytes 786440 | tf_op jit(solution)/shard_map/ppermute | solution.py:60
  45.6 9.3 %collective-permute-start.17 = (bf16[768,256]{1,0:T(8,128)(2,1)S(1)}, bf16[768,256]{1,0:T(8,128)(2,1)S(1)}, u32[]{:S(2)}, u32[]{:S(2)}) collective-permute-start(bf16[768,256]{1,0:T(8,128)(2,1)S(1)} %get-tuple-element.14), channel_id=1, source_target_pairs={{0,384},{16,400},{1,385},{17,401},{2,386},{18,402},{3,387},{19,403... | collective-permute-start | bytes 1179656 | tf_op jit(solution)/shard_map/ppermute | solution.py:60
  47.5 8.6 %collective-permute-start.16 = (bf16[768,256]{1,0:T(8,128)(2,1)S(1)}, bf16[768,256]{1,0:T(8,128)(2,1)S(1)}, u32[]{:S(2)}, u32[]{:S(2)}) collective-permute-start(bf16[768,256]{1,0:T(8,128)(2,1)S(1)} %get-tuple-element.14), channel_id=1, source_target_pairs={{0,128},{16,144},{1,129},{17,145},{2,130},{18,146},{3,131},{19,147... | collective-permute-start | bytes 1179656 | tf_op jit(solution)/shard_map/ppermute | solution.py:60
  48.2 9.3 %collective-permute-start.15 = (bf16[768,256]{1,0:T(8,128)(2,1)S(1)}, bf16[768,256]{1,0:T(8,128)(2,1)S(1)}, u32[]{:S(2)}, u32[]{:S(2)}) collective-permute-start(bf16[768,256]{1,0:T(8,128)(2,1)S(1)} %get-tuple-element.14), channel_id=1, source_target_pairs={{0,352},{16,304},{1,353},{17,305},{2,354},{18,306},{3,355},{19,307... | collective-permute-start | bytes 1179656 | tf_op jit(solution)/shard_map/ppermute | solution.py:60
  52.1 6.8 %collective-permute-start.13 = (bf16[512,256]{1,0:T(8,128)(2,1)S(1)}, bf16[512,256]{1,0:T(8,128)(2,1)S(1)}, u32[]{:S(2)}, u32[]{:S(2)}) collective-permute-start(bf16[512,256]{1,0:T(8,128)(2,1)S(1)} %add_add_fusion.2), channel_id=1, source_target_pairs={{0,14},{1,15},{16,30},{17,31},{32,46},{33,47},{48,62},{49,63},{64,... | collective-permute-start | bytes 786440 | tf_op jit(solution)/shard_map/ppermute | solution.py:60
  53.4 5.5 %collective-permute-start.12 = (bf16[512,256]{1,0:T(8,128)(2,1)S(1)}, bf16[512,256]{1,0:T(8,128)(2,1)S(1)}, u32[]{:S(2)}, u32[]{:S(2)}) collective-permute-start(bf16[512,256]{1,0:T(8,128)(2,1)S(1)} %add_add_fusion.2), channel_id=1, source_target_pairs={{0,2},{1,3},{16,18},{17,19},{32,34},{33,35},{48,50},{49,51},{64,66... | collective-permute-start | bytes 786440 | tf_op jit(solution)/shard_map/ppermute | solution.py:60
  54.8 5.8 %collective-permute-start.9 = (bf16[512,256]{1,0:T(8,128)(2,1)S(1)}, bf16[512,256]{1,0:T(8,128)(2,1)S(1)}, u32[]{:S(2)}, u32[]{:S(2)}) collective-permute-start(bf16[512,256]{1,0:T(8,128)(2,1)S(1)} %add_add_fusion.4), channel_id=1, source_target_pairs={{0,14},{1,15},{16,30},{17,31},{32,46},{33,47},{48,62},{49,63},{64,... | collective-permute-start | bytes 786440 | tf_op jit(solution)/shard_map/ppermute | solution.py:60
  56.2 5.2 %collective-permute-start.8 = (bf16[512,256]{1,0:T(8,128)(2,1)S(1)}, bf16[512,256]{1,0:T(8,128)(2,1)S(1)}, u32[]{:S(2)}, u32[]{:S(2)}) collective-permute-start(bf16[512,256]{1,0:T(8,128)(2,1)S(1)} %add_add_fusion.4), channel_id=1, source_target_pairs={{0,2},{1,3},{16,18},{17,19},{32,34},{33,35},{48,50},{49,51},{64,66... | collective-permute-start | bytes 786440 | tf_op jit(solution)/shard_map/ppermute | solution.py:60
  57.6 12.1 %collective-permute-start.18 = (bf16[768,256]{1,0:T(8,128)(2,1)S(1)}, bf16[768,256]{1,0:T(8,128)(2,1)S(1)}, u32[]{:S(2)}, u32[]{:S(2)}) collective-permute-start(bf16[768,256]{1,0:T(8,128)(2,1)S(1)} %add_add_fusion), channel_id=1, source_target_pairs={{0,96},{16,48},{1,97},{17,49},{2,98},{18,50},{3,99},{19,51},{4,100... | collective-permute-start | bytes 1179656 | tf_op jit(solution)/shard_map/ppermute | solution.py:60
  61.5 33.4 %collective-permute-start.14 = (bf16[1024,256]{1,0:T(8,128)(2,1)S(1)}, bf16[1024,256]{1,0:T(8,128)(2,1)S(1)}, u32[]{:S(2)}, u32[]{:S(2)}) collective-permute-start(bf16[1024,256]{1,0:T(8,128)(2,1)S(1)} %pad_maximum_fusion.mine), channel_id=1, source_target_pairs={{0,1},{1,0},{2,3},{3,2},{4,5},{5,4},{6,7},{7,6},{8,9},{9,8},{10,11... | collective-permute-start | bytes 1572872 | tf_op jit(solution)/shard_map/ppermute | solution.py:60
  69.8 6.6 %collective-permute-start.19 = (bf16[768,256]{1,0:T(8,128)(2,1)S(1)}, bf16[768,256]{1,0:T(8,128)(2,1)S(1)}, u32[]{:S(2)}, u32[]{:S(2)}) collective-permute-start(bf16[768,256]{1,0:T(8,128)(2,1)S(1)} %add.79), channel_id=1, source_target_pairs={{0,32},{16,112},{1,33},{17,113},{2,34},{18,114},{3,35},{19,115},{4... | collective-permute-start | bytes 1179656 | tf_op jit(solution)/shard_map/ppermute | solution.py:60
  76.5 23.1 %collective-permute-start.21 = (bf16[512,256]{1,0:T(8,128)(2,1)S(1)}, bf16[512,256]{1,0:T(8,128)(2,1)S(1)}, u32[]{:S(2)}, u32[]{:S(2)}) collective-permute-start(bf16[512,256]{1,0:T(8,128)(2,1)S(1)} %slice.9), channel_id=1, source_target_pairs={{16,0},{17,1},{18,2},{19,3},{20,4},{21,5},{22,6},{23,7},{24,8},{25... | collective-permute-start | bytes 786440 | tf_op jit(solution)/shard_map/ppermute | solution.py:60
  91.1 8.4 %collective-permute-start.20 = (bf16[256,256]{1,0:T(8,128)(2,1)S(1)}, bf16[256,256]{1,0:T(8,128)(2,1)S(1)}, u32[]{:S(2)}, u32[]{:S(2)}) collective-permute-start(bf16[256,256]{1,0:T(8,128)(2,1)S(1)} %slice.8), channel_id=1, source_target_pairs={{0,16},{1,17},{2,18},{3,19},{4,20},{5,21},{6,22},{7,23},{8,24},{9,... | collective-permute-start | bytes 393224 | tf_op jit(solution)/shard_map/ppermute | solution.py:60

commit v4 on v3

--- a/solution.py
+++ b/solution.py
@@ -161,6 +161,12 @@
         sums.append(jnp.where(diagonal, 1.0, r))
     for step in range(8):
         for n in range(2):
+            if step >= 5:
+                high = powers[n].astype(jnp.bfloat16)
+                sums[n] = sums[n] + dot(high, sums[n].astype(jnp.bfloat16))
+                if step < 7:
+                    powers[n] = dot(high, high)
+                continue
             high, low = halves(powers[n])
             if step > 0:
                 sum_high, sum_low = halves(sums[n])
@@ -207,7 +213,7 @@
 
 def update_kernel(
     here, row_pattern, col_pattern, source, lower_0, lower_1,
-    first_held, first_came, rest_held, up_came, down_came, out, upper,
+    first_held, rest_held, up_came, down_came, out, upper,
 ):
     prow, pcol = here[0], here[1]
     i = pl.program_id(0)
@@ -220,13 +226,12 @@
         for s in range(COL_CAP):
             rest = pl.ds((s - 1) * BLK, BLK)
             held = first_held[...] if s == 0 else rest_held[rest, :]
-            came = (
-                first_came[...]
-                if s == 0
-                else up_came[...]
-                if s == COL_CAP - 1
-                else down_came[rest, :]
-            )
+            if s == 0:
+                came = up_came[pl.ds(0, BLK), :]
+            elif s == COL_CAP - 1:
+                came = up_came[pl.ds(BLK, BLK), :]
+            else:
+                came = down_came[rest, :]
             upper[0, pl.ds(s * BLK, BLK), :] = jnp.where(even, held, came)
             upper[1, pl.ds(s * BLK, BLK), :] = jnp.where(even, came, held)
 
@@ -299,7 +304,7 @@
     return pl.pallas_call(
         update_kernel,
         grid=(row_blocks,),
-        in_specs=[smem] * 3 + [strip] + [vmem] * 7,
+        in_specs=[smem] * 3 + [strip] + [vmem] * 6,
         out_specs=strip,
         out_shape=jax.ShapeDtypeStruct(matrix.shape, matrix.dtype),
         scratch_shapes=[pltpu.VMEM((2, COL_CAP * BLK, BLK), jnp.bfloat16)],
@@ -324,25 +329,21 @@
         return held
 
     first_held = tree(first, prow <= 1, SPREAD)
-    first_came = send(first_held, UP)
     rest_held = tree(rest, prow <= 1, SPREAD)
     down_came = send(rest_held[: 2 * BLK], DOWN)
-    up_came = send(rest_held[2 * BLK :], UP)
+    up_came = send(jnp.concatenate([first_held, rest_held[2 * BLK :]], axis=0), UP)
     panel = tree(panel, pcol <= 1, [LINE_1, LINE_2])
-    pivots = jnp.concatenate(
-        [
-            jnp.where(even, first_held, first_came),
-            jnp.where(even, first_came, first_held),
-        ],
+    pivot_held = tree(first_held, pcol <= 1, [LINE_1, LINE_2])
+    pivot_came = send(pivot_held, UP)
+    mine = jnp.concatenate(
+        [jnp.where(even, pivot_held, pivot_came), jnp.where(even, pivot_came, pivot_held), panel],
         axis=0,
     )
-    pivots = tree(pivots, pcol <= 1, [LINE_1, LINE_2])
-    mine = jnp.concatenate([pivots, panel], axis=0)
     other = send(mine, SWAP)
     lower_0, lower_1 = panels(here, row_pattern, mine, other)
     return update(
         here, row_pattern, col_pattern, matrix, lower_0, lower_1,
-        first_held, first_came, rest_held, up_came, down_came,
+        first_held, rest_held, up_came, down_came,
     )
 
 

time: 105 us -> 90.4 us (0.86)
  the two profiles are of different devices: /device:TPU:24 before, /device:TPU:2 now
where the time goes in v4:
time: 90.4 us; the launch traced here: 89.7 us
  starting transfers between devices  56.2 us (62%)
  waiting for transfers between devices  20.8 us (23%)
  Pallas kernels  11.1 us (12%)
  other arithmetic  1.11 us (1%)
    ppermute x22, starting transfers between devices, send(): return lax.ppermute(value, AXES, pairs)  56.2 us
    ppermute x22, waiting for transfers between devices, send(): return lax.ppermute(value, AXES, pairs)  20.8 us
    pallas_call x1, Pallas kernels, update(): pl.pallas_call(update_kernel, grid=(row_blocks,), in_specs=[smem] * 3 + [...  4.84 us
    pallas_call x1, Pallas kernels, panels(): pl.pallas_call(panels_kernel, in_specs=[smem, smem] + [vmem] * 2, out_spe...  4.11 us
    pallas_call x1, Pallas kernels, pack(): pl.pallas_call(pack_kernel, in_specs=[smem, smem, smem, pl.BlockSpec(memo...  2.2 us
  transfers between devices with their start and end apart: 22, of which 9 were waited for; matrix products, arithmetic and copies ran while one was open for 1% of the time, Pallas kernels for 5%

profile of v4, /device:TPU:2, one launch (start us, length us, event | category | flops | bytes accessed | tf_op | source)
XLA Modules:
  0.0 89.7 jit_solution(16974639726420823350)
XLA Ops:
  0.0 0.5 compare_select_fusion.here
  0.5 2.2 %pack.1 = (bf16[256,256]{1,0:T(8,128)(2,1)S(1)}, bf16[768,256]{1,0:T(8,128)(2,1)S(1)}, bf16[512,256]{1,0:T(8,128)(2,1)S(1)}) custom-call(s32[2]{0:T(128)} %compare_select_fusion.here, s32[2,96]{1,0:T(2,128)} %row_pattern.5, s32[2,96]{1,0:T(2,128)} %col_pattern.3, bf16[768,1536]{1,0:T(8,128)(2,1)} %source.1), custom_call_target="tpu_custom_call" | custom-call | tf_op jit(solution)/shard_map/pack/pallas_call | solution.py:110
  2.7 0.7 collective-permute-start.2
  3.4 1.3 %collective-permute-start.1 = (bf16[256,256]{1,0:T(8,128)(2,1)S(1)}, bf16[256,256]{1,0:T(8,128)(2,1)S(1)}, u32[]{:S(2)}, u32[]{:S(2)}) collective-permute-start(bf16[256,256]{1,0:T(8,128)(2,1)S(1)} %get-tuple-element.10), channel_id=1, source_target_pairs={{0,128},{16,144},{1,129},{17,145},{2,130},{18,146},{3,131},{19,147... | collective-permute-start | bytes 393224 | tf_op jit(solution)/shard_map/ppermute | solution.py:60
  4.7 0.7 collective-permute-start
  5.4 8.7 %collective-permute-done.1 = bf16[256,256]{1,0:T(8,128)(2,1)S(1)} collective-permute-done((bf16[256,256]{1,0:T(8,128)(2,1)S(1)}, bf16[256,256]{1,0:T(8,128)(2,1)S(1)}, u32[]{:S(2)}, u32[]{:S(2)}) %collective-permute-start.1) | collective-permute-done | bytes 131104 | tf_op jit(solution)/shard_map/ppermute | solution.py:60
  14.2 1.3 %collective-permute-start.3 = (bf16[256,256]{1,0:T(8,128)(2,1)S(1)}, bf16[256,256]{1,0:T(8,128)(2,1)S(1)}, u32[]{:S(2)}, u32[]{:S(2)}) collective-permute-start(bf16[256,256]{1,0:T(8,128)(2,1)S(1)} %add_add_fusion.5), channel_id=1, source_target_pairs={{0,96},{16,48},{1,97},{17,49},{2,98},{18,50},{3,99},{19,51},{4,100... | collective-permute-start | bytes 393224 | tf_op jit(solution)/shard_map/ppermute | solution.py:60
  15.5 9.1 %collective-permute-start.11 = (bf16[512,256]{1,0:T(8,128)(2,1)S(1)}, bf16[512,256]{1,0:T(8,128)(2,1)S(1)}, u32[]{:S(2)}, u32[]{:S(2)}) collective-permute-start(bf16[512,256]{1,0:T(8,128)(2,1)S(1)} %get-tuple-element.11), channel_id=1, source_target_pairs={{0,10},{1,11},{16,26},{17,27},{32,42},{33,43},{48,58},{49,59},{64,... | collective-permute-start | bytes 786440 | tf_op jit(solution)/shard_map/ppermute | solution.py:60
  24.5 1.3 %collective-permute-start.10 = (bf16[512,256]{1,0:T(8,128)(2,1)S(1)}, bf16[512,256]{1,0:T(8,128)(2,1)S(1)}, u32[]{:S(2)}, u32[]{:S(2)}) collective-permute-start(bf16[512,256]{1,0:T(8,128)(2,1)S(1)} %get-tuple-element.11), channel_id=1, source_target_pairs={{0,6},{1,7},{16,22},{17,23},{32,38},{33,39},{48,54},{49,55},{64,70... | collective-permute-start | bytes 786440 | tf_op jit(solution)/shard_map/ppermute | solution.py:60
  25.9 1.3 %collective-permute-start.4 = (bf16[256,256]{1,0:T(8,128)(2,1)S(1)}, bf16[256,256]{1,0:T(8,128)(2,1)S(1)}, u32[]{:S(2)}, u32[]{:S(2)}) collective-permute-start(bf16[256,256]{1,0:T(8,128)(2,1)S(1)} %add.66), channel_id=1, source_target_pairs={{0,32},{16,112},{1,33},{17,113},{2,34},{18,114},{3,35},{19,115},{4... | collective-permute-start | bytes 393224 | tf_op jit(solution)/shard_map/ppermute | solution.py:60
  27.2 0.7 collective-permute-start.17
  27.9 1.3 %collective-permute-start.16 = (bf16[768,256]{1,0:T(8,128)(2,1)S(1)}, bf16[768,256]{1,0:T(8,128)(2,1)S(1)}, u32[]{:S(2)}, u32[]{:S(2)}) collective-permute-start(bf16[768,256]{1,0:T(8,128)(2,1)S(1)} %get-tuple-element.14), channel_id=1, source_target_pairs={{0,128},{16,144},{1,129},{17,145},{2,130},{18,146},{3,131},{19,147... | collective-permute-start | bytes 1179656 | tf_op jit(solution)/shard_map/ppermute | solution.py:60
  29.7 0.7 collective-permute-start.15
  30.4 6.1 %collective-permute-start.6 = (bf16[256,256]{1,0:T(8,128)(2,1)S(1)}, bf16[256,256]{1,0:T(8,128)(2,1)S(1)}, u32[]{:S(2)}, u32[]{:S(2)}) collective-permute-start(bf16[256,256]{1,0:T(8,128)(2,1)S(1)} %add.67.first_held), channel_id=1, source_target_pairs={{0,10},{1,11},{16,26},{17,27},{32,42},{33,43},{48,58},{49,59},{64,... | collective-permute-start | bytes 393224 | tf_op jit(solution)/shard_map/ppermute | solution.py:60
  36.6 1.3 %collective-permute-start.5 = (bf16[256,256]{1,0:T(8,128)(2,1)S(1)}, bf16[256,256]{1,0:T(8,128)(2,1)S(1)}, u32[]{:S(2)}, u32[]{:S(2)}) collective-permute-start(bf16[256,256]{1,0:T(8,128)(2,1)S(1)} %add.67.first_held), channel_id=1, source_target_pairs={{0,6},{1,7},{16,22},{17,23},{32,38},{33,39},{48,54},{49,55},{64,70... | collective-permute-start | bytes 393224 | tf_op jit(solution)/shard_map/ppermute | solution.py:60
  37.9 2.2 %collective-permute-done.6 = bf16[256,256]{1,0:T(8,128)(2,1)S(1)} collective-permute-done((bf16[256,256]{1,0:T(8,128)(2,1)S(1)}, bf16[256,256]{1,0:T(8,128)(2,1)S(1)}, u32[]{:S(2)}, u32[]{:S(2)}) %collective-permute-start.6) | collective-permute-done | bytes 131104 | tf_op jit(solution)/shard_map/ppermute | solution.py:60
  40.1 1.3 %collective-permute-start.13 = (bf16[512,256]{1,0:T(8,128)(2,1)S(1)}, bf16[512,256]{1,0:T(8,128)(2,1)S(1)}, u32[]{:S(2)}, u32[]{:S(2)}) collective-permute-start(bf16[512,256]{1,0:T(8,128)(2,1)S(1)} %add_add_fusion.2), channel_id=1, source_target_pairs={{0,14},{1,15},{16,30},{17,31},{32,46},{33,47},{48,62},{49,63},{64,... | collective-permute-start | bytes 786440 | tf_op jit(solution)/shard_map/ppermute | solution.py:60
  41.4 1.3 %collective-permute-start.12 = (bf16[512,256]{1,0:T(8,128)(2,1)S(1)}, bf16[512,256]{1,0:T(8,128)(2,1)S(1)}, u32[]{:S(2)}, u32[]{:S(2)}) collective-permute-start(bf16[512,256]{1,0:T(8,128)(2,1)S(1)} %add_add_fusion.2), channel_id=1, source_target_pairs={{0,2},{1,3},{16,18},{17,19},{32,34},{33,35},{48,50},{49,51},{64,66... | collective-permute-start | bytes 786440 | tf_op jit(solution)/shard_map/ppermute | solution.py:60
  42.8 1.3 %collective-permute-start.8 = (bf16[256,256]{1,0:T(8,128)(2,1)S(1)}, bf16[256,256]{1,0:T(8,128)(2,1)S(1)}, u32[]{:S(2)}, u32[]{:S(2)}) collective-permute-start(bf16[256,256]{1,0:T(8,128)(2,1)S(1)} %add_add_fusion.4), channel_id=1, source_target_pairs={{0,14},{1,15},{16,30},{17,31},{32,46},{33,47},{48,62},{49,63},{64,... | collective-permute-start | bytes 393224 | tf_op jit(solution)/shard_map/ppermute | solution.py:60
  44.1 1.3 %collective-permute-start.7 = (bf16[256,256]{1,0:T(8,128)(2,1)S(1)}, bf16[256,256]{1,0:T(8,128)(2,1)S(1)}, u32[]{:S(2)}, u32[]{:S(2)}) collective-permute-start(bf16[256,256]{1,0:T(8,128)(2,1)S(1)} %add_add_fusion.4), channel_id=1, source_target_pairs={{0,2},{1,3},{16,18},{17,19},{32,34},{33,35},{48,50},{49,51},{64,66... | collective-permute-start | bytes 393224 | tf_op jit(solution)/shard_map/ppermute | solution.py:60
  45.5 1.8 %collective-permute-start.18 = (bf16[768,256]{1,0:T(8,128)(2,1)S(1)}, bf16[768,256]{1,0:T(8,128)(2,1)S(1)}, u32[]{:S(2)}, u32[]{:S(2)}) collective-permute-start(bf16[768,256]{1,0:T(8,128)(2,1)S(1)} %add_add_fusion), channel_id=1, source_target_pairs={{0,96},{16,48},{1,97},{17,49},{2,98},{18,50},{3,99},{19,51},{4,100... | collective-permute-start | bytes 1179656 | tf_op jit(solution)/shard_map/ppermute | solution.py:60
  47.5 1.3 %collective-permute-done.7 = bf16[256,256]{1,0:T(8,128)(2,1)S(1)} collective-permute-done((bf16[256,256]{1,0:T(8,128)(2,1)S(1)}, bf16[256,256]{1,0:T(8,128)(2,1)S(1)}, u32[]{:S(2)}, u32[]{:S(2)}) %collective-permute-start.7) | collective-permute-done | bytes 131104 | tf_op jit(solution)/shard_map/ppermute | solution.py:60
  48.8 3.4 %collective-permute-start.9 = (bf16[256,256]{1,0:T(8,128)(2,1)S(1)}, bf16[256,256]{1,0:T(8,128)(2,1)S(1)}, u32[]{:S(2)}, u32[]{:S(2)}) collective-permute-start(bf16[256,256]{1,0:T(8,128)(2,1)S(1)} %add_add_fusion.3), channel_id=1, source_target_pairs={{0,16},{1,17},{2,18},{3,19},{4,20},{5,21},{6,22},{7,23},{8,24},{9,... | collective-permute-start | bytes 393224 | tf_op jit(solution)/shard_map/ppermute | solution.py:60
  52.7 1.3 %collective-permute-start.19 = (bf16[768,256]{1,0:T(8,128)(2,1)S(1)}, bf16[768,256]{1,0:T(8,128)(2,1)S(1)}, u32[]{:S(2)}, u32[]{:S(2)}) collective-permute-start(bf16[768,256]{1,0:T(8,128)(2,1)S(1)} %add.79), channel_id=1, source_target_pairs={{0,32},{16,112},{1,33},{17,113},{2,34},{18,114},{3,35},{19,115},{4... | collective-permute-start | bytes 1179656 | tf_op jit(solution)/shard_map/ppermute | solution.py:60
  54.0 2.9 %collective-permute-done.9 = bf16[256,256]{1,0:T(8,128)(2,1)S(1)} collective-permute-done((bf16[256,256]{1,0:T(8,128)(2,1)S(1)}, bf16[256,256]{1,0:T(8,128)(2,1)S(1)}, u32[]{:S(2)}, u32[]{:S(2)}) %collective-permute-start.9) | collective-permute-done | bytes 131104 | tf_op jit(solution)/shard_map/ppermute | solution.py:60
  57.0 1.9 %collective-permute-start.14 = (bf16[1024,256]{1,0:T(8,128)(2,1)S(1)}, bf16[1024,256]{1,0:T(8,128)(2,1)S(1)}, u32[]{:S(2)}, u32[]{:S(2)}) collective-permute-start(bf16[1024,256]{1,0:T(8,128)(2,1)S(1)} %pad_maximum_fusion.mine), channel_id=1, source_target_pairs={{0,1},{1,0},{2,3},{3,2},{4,5},{5,4},{6,7},{7,6},{8,9},{9,8},{10,11... | collective-permute-start | bytes 1572872 | tf_op jit(solution)/shard_map/ppermute | solution.py:60
  58.9 1.3 %collective-permute-done.19 = bf16[768,256]{1,0:T(8,128)(2,1)S(1)} collective-permute-done((bf16[768,256]{1,0:T(8,128)(2,1)S(1)}, bf16[768,256]{1,0:T(8,128)(2,1)S(1)}, u32[]{:S(2)}, u32[]{:S(2)}) %collective-permute-start.19) | collective-permute-done | bytes 393248 | tf_op jit(solution)/shard_map/ppermute | solution.py:60
  60.4 15.0 %collective-permute-start.21 = (bf16[512,256]{1,0:T(8,128)(2,1)S(1)}, bf16[512,256]{1,0:T(8,128)(2,1)S(1)}, u32[]{:S(2)}, u32[]{:S(2)}) collective-permute-start(bf16[512,256]{1,0:T(8,128)(2,1)S(1)} %slice.9), channel_id=1, source_target_pairs={{16,0},{17,1},{18,2},{19,3},{20,4},{21,5},{22,6},{23,7},{24,8},{25... | collective-permute-start | bytes 786440 | tf_op jit(solution)/shard_map/ppermute | solution.py:60
  75.4 1.9 %collective-permute-start.20 = (bf16[512,256]{1,0:T(8,128)(2,1)S(1)}, bf16[512,256]{1,0:T(8,128)(2,1)S(1)}, u32[]{:S(2)}, u32[]{:S(2)}) collective-permute-start(bf16[512,256]{1,0:T(8,128)(2,1)S(1)} %pad_maximum_fusion.1), channel_id=1, source_target_pairs={{0,16},{1,17},{2,18},{3,19},{4,20},{5,21},{6,22},{7,23},{8,24},{9,... | collective-permute-start | bytes 786440 | tf_op jit(solution)/shard_map/ppermute | solution.py:60
  77.3 4.1 %panels.1 = (bf16[512,256]{1,0:T(8,128)(2,1)S(1)}, bf16[512,256]{1,0:T(8,128)(2,1)S(1)}) custom-call(s32[2]{0:T(128)} %compare_select_fusion.here, s32[2,96]{1,0:T(2,128)} %row_pattern.5, bf16[1024,256]{1,0:T(8,128)(2,1)S(1)} %pad_maximum_fusion.mine, bf16[1024,256]{1,0:T(8,128)(2,1)S(1)} %collective-permute-done.14.other), custom_call_target="tpu_custom_call" | custom-call | flops 2013265920 | bytes 1572864 | tf_op jit(solution)/shard_map/panels/pallas_call | solution.py:202
  81.5 3.4 %collective-permute-done.20.up_came = bf16[512,256]{1,0:T(8,128)(2,1)S(1)} collective-permute-done((bf16[512,256]{1,0:T(8,128)(2,1)S(1)}, bf16[512,256]{1,0:T(8,128)(2,1)S(1)}, u32[]{:S(2)}, u32[]{:S(2)}) %collective-permute-start.20) | collective-permute-done | bytes 262176 | tf_op jit(solution)/shard_map/ppermute | solution.py:60
  84.9 4.8 %update.1 = bf16[768,1536]{1,0:T(8,128)(2,1)} custom-call(s32[2]{0:T(128)} %compare_select_fusion.here, s32[2,96]{1,0:T(2,128)} %row_pattern.5, s32[2,96]{1,0:T(2,128)} %col_pattern.3, bf16[768,1536]{1,0:T(8,128)(2,1)} %source.1, bf16[512,256]{1,0:T(8,128)(2,1)S(1)} %get-tuple-element.12.lower_0, bf16[512,256]{1,0:T(8,128)(2,1)S(1)} %get-tuple-element.13.lower_1, ...), custom_call_target="tpu_custom_call" | custom-call | tf_op jit(solution)/shard_map/update/pallas_call | solution.py:304
  (31 shorter events, 1.6 us)
Async XLA Ops:
  2.7 2.7 %collective-permute-start.2 = (bf16[256,256]{1,0:T(8,128)(2,1)S(1)}, bf16[256,256]{1,0:T(8,128)(2,1)S(1)}, u32[]{:S(2)}, u32[]{:S(2)}) collective-permute-start(bf16[256,256]{1,0:T(8,128)(2,1)S(1)} %get-tuple-element.10), channel_id=1, source_target_pairs={{0,384},{16,400},{1,385},{17,401},{2,386},{18,402},{3,387},{19,403... | collective-permute-start | bytes 393224 | tf_op jit(solution)/shard_map/ppermute | solution.py:60
  3.4 10.7 %collective-permute-start.1 = (bf16[256,256]{1,0:T(8,128)(2,1)S(1)}, bf16[256,256]{1,0:T(8,128)(2,1)S(1)}, u32[]{:S(2)}, u32[]{:S(2)}) collective-permute-start(bf16[256,256]{1,0:T(8,128)(2,1)S(1)} %get-tuple-element.10), channel_id=1, source_target_pairs={{0,128},{16,144},{1,129},{17,145},{2,130},{18,146},{3,131},{19,147... | collective-permute-start | bytes 393224 | tf_op jit(solution)/shard_map/ppermute | solution.py:60
  4.7 9.4 %collective-permute-start = (bf16[256,256]{1,0:T(8,128)(2,1)S(1)}, bf16[256,256]{1,0:T(8,128)(2,1)S(1)}, u32[]{:S(2)}, u32[]{:S(2)}) collective-permute-start(bf16[256,256]{1,0:T(8,128)(2,1)S(1)} %get-tuple-element.10), channel_id=1, source_target_pairs={{0,352},{16,304},{1,353},{17,305},{2,354},{18,306},{3,355},{19,307... | collective-permute-start | bytes 393224 | tf_op jit(solution)/shard_map/ppermute | solution.py:60
  14.2 11.7 %collective-permute-start.3 = (bf16[256,256]{1,0:T(8,128)(2,1)S(1)}, bf16[256,256]{1,0:T(8,128)(2,1)S(1)}, u32[]{:S(2)}, u32[]{:S(2)}) collective-permute-start(bf16[256,256]{1,0:T(8,128)(2,1)S(1)} %add_add_fusion.5), channel_id=1, source_target_pairs={{0,96},{16,48},{1,97},{17,49},{2,98},{18,50},{3,99},{19,51},{4,100... | collective-permute-start | bytes 393224 | tf_op jit(solution)/shard_map/ppermute | solution.py:60
  15.5 15.0 %collective-permute-start.11 = (bf16[512,256]{1,0:T(8,128)(2,1)S(1)}, bf16[512,256]{1,0:T(8,128)(2,1)S(1)}, u32[]{:S(2)}, u32[]{:S(2)}) collective-permute-start(bf16[512,256]{1,0:T(8,128)(2,1)S(1)} %get-tuple-element.11), channel_id=1, source_target_pairs={{0,10},{1,11},{16,26},{17,27},{32,42},{33,43},{48,58},{49,59},{64,... | collective-permute-start | bytes 786440 | tf_op jit(solution)/shard_map/ppermute | solution.py:60
  24.5 12.0 %collective-permute-start.10 = (bf16[512,256]{1,0:T(8,128)(2,1)S(1)}, bf16[512,256]{1,0:T(8,128)(2,1)S(1)}, u32[]{:S(2)}, u32[]{:S(2)}) collective-permute-start(bf16[512,256]{1,0:T(8,128)(2,1)S(1)} %get-tuple-element.11), channel_id=1, source_target_pairs={{0,6},{1,7},{16,22},{17,23},{32,38},{33,39},{48,54},{49,55},{64,70... | collective-permute-start | bytes 786440 | tf_op jit(solution)/shard_map/ppermute | solution.py:60
  25.9 3.8 %collective-permute-start.4 = (bf16[256,256]{1,0:T(8,128)(2,1)S(1)}, bf16[256,256]{1,0:T(8,128)(2,1)S(1)}, u32[]{:S(2)}, u32[]{:S(2)}) collective-permute-start(bf16[256,256]{1,0:T(8,128)(2,1)S(1)} %add.66), channel_id=1, source_target_pairs={{0,32},{16,112},{1,33},{17,113},{2,34},{18,114},{3,35},{19,115},{4... | collective-permute-start | bytes 393224 | tf_op jit(solution)/shard_map/ppermute | solution.py:60
  27.2 15.6 %collective-permute-start.17 = (bf16[768,256]{1,0:T(8,128)(2,1)S(1)}, bf16[768,256]{1,0:T(8,128)(2,1)S(1)}, u32[]{:S(2)}, u32[]{:S(2)}) collective-permute-start(bf16[768,256]{1,0:T(8,128)(2,1)S(1)} %get-tuple-element.14), channel_id=1, source_target_pairs={{0,384},{16,400},{1,385},{17,401},{2,386},{18,402},{3,387},{19,403... | collective-permute-start | bytes 1179656 | tf_op jit(solution)/shard_map/ppermute | solution.py:60
  27.9 16.2 %collective-permute-start.16 = (bf16[768,256]{1,0:T(8,128)(2,1)S(1)}, bf16[768,256]{1,0:T(8,128)(2,1)S(1)}, u32[]{:S(2)}, u32[]{:S(2)}) collective-permute-start(bf16[768,256]{1,0:T(8,128)(2,1)S(1)} %get-tuple-element.14), channel_id=1, source_target_pairs={{0,128},{16,144},{1,129},{17,145},{2,130},{18,146},{3,131},{19,147... | collective-permute-start | bytes 1179656 | tf_op jit(solution)/shard_map/ppermute | solution.py:60
  29.7 15.7 %collective-permute-start.15 = (bf16[768,256]{1,0:T(8,128)(2,1)S(1)}, bf16[768,256]{1,0:T(8,128)(2,1)S(1)}, u32[]{:S(2)}, u32[]{:S(2)}) collective-permute-start(bf16[768,256]{1,0:T(8,128)(2,1)S(1)} %get-tuple-element.14), channel_id=1, source_target_pairs={{0,352},{16,304},{1,353},{17,305},{2,354},{18,306},{3,355},{19,307... | collective-permute-start | bytes 1179656 | tf_op jit(solution)/shard_map/ppermute | solution.py:60
  30.4 9.7 %collective-permute-start.6 = (bf16[256,256]{1,0:T(8,128)(2,1)S(1)}, bf16[256,256]{1,0:T(8,128)(2,1)S(1)}, u32[]{:S(2)}, u32[]{:S(2)}) collective-permute-start(bf16[256,256]{1,0:T(8,128)(2,1)S(1)} %add.67.first_held), channel_id=1, source_target_pairs={{0,10},{1,11},{16,26},{17,27},{32,42},{33,43},{48,58},{49,59},{64,... | collective-permute-start | bytes 393224 | tf_op jit(solution)/shard_map/ppermute | solution.py:60
  36.6 4.8 %collective-permute-start.5 = (bf16[256,256]{1,0:T(8,128)(2,1)S(1)}, bf16[256,256]{1,0:T(8,128)(2,1)S(1)}, u32[]{:S(2)}, u32[]{:S(2)}) collective-permute-start(bf16[256,256]{1,0:T(8,128)(2,1)S(1)} %add.67.first_held), channel_id=1, source_target_pairs={{0,6},{1,7},{16,22},{17,23},{32,38},{33,39},{48,54},{49,55},{64,70... | collective-permute-start | bytes 393224 | tf_op jit(solution)/shard_map/ppermute | solution.py:60
  40.1 12.1 %collective-permute-start.13 = (bf16[512,256]{1,0:T(8,128)(2,1)S(1)}, bf16[512,256]{1,0:T(8,128)(2,1)S(1)}, u32[]{:S(2)}, u32[]{:S(2)}) collective-permute-start(bf16[512,256]{1,0:T(8,128)(2,1)S(1)} %add_add_fusion.2), channel_id=1, source_target_pairs={{0,14},{1,15},{16,30},{17,31},{32,46},{33,47},{48,62},{49,63},{64,... | collective-permute-start | bytes 786440 | tf_op jit(solution)/shard_map/ppermute | solution.py:60
  41.4 10.8 %collective-permute-start.12 = (bf16[512,256]{1,0:T(8,128)(2,1)S(1)}, bf16[512,256]{1,0:T(8,128)(2,1)S(1)}, u32[]{:S(2)}, u32[]{:S(2)}) collective-permute-start(bf16[512,256]{1,0:T(8,128)(2,1)S(1)} %add_add_fusion.2), channel_id=1, source_target_pairs={{0,2},{1,3},{16,18},{17,19},{32,34},{33,35},{48,50},{49,51},{64,66... | collective-permute-start | bytes 786440 | tf_op jit(solution)/shard_map/ppermute | solution.py:60
  42.8 4.7 %collective-permute-start.8 = (bf16[256,256]{1,0:T(8,128)(2,1)S(1)}, bf16[256,256]{1,0:T(8,128)(2,1)S(1)}, u32[]{:S(2)}, u32[]{:S(2)}) collective-permute-start(bf16[256,256]{1,0:T(8,128)(2,1)S(1)} %add_add_fusion.4), channel_id=1, source_target_pairs={{0,14},{1,15},{16,30},{17,31},{32,46},{33,47},{48,62},{49,63},{64,... | collective-permute-start | bytes 393224 | tf_op jit(solution)/shard_map/ppermute | solution.py:60
  44.1 4.7 %collective-permute-start.7 = (bf16[256,256]{1,0:T(8,128)(2,1)S(1)}, bf16[256,256]{1,0:T(8,128)(2,1)S(1)}, u32[]{:S(2)}, u32[]{:S(2)}) collective-permute-start(bf16[256,256]{1,0:T(8,128)(2,1)S(1)} %add_add_fusion.4), channel_id=1, source_target_pairs={{0,2},{1,3},{16,18},{17,19},{32,34},{33,35},{48,50},{49,51},{64,66... | collective-permute-start | bytes 393224 | tf_op jit(solution)/shard_map/ppermute | solution.py:60
  45.5 7.1 %collective-permute-start.18 = (bf16[768,256]{1,0:T(8,128)(2,1)S(1)}, bf16[768,256]{1,0:T(8,128)(2,1)S(1)}, u32[]{:S(2)}, u32[]{:S(2)}) collective-permute-start(bf16[768,256]{1,0:T(8,128)(2,1)S(1)} %add_add_fusion), channel_id=1, source_target_pairs={{0,96},{16,48},{1,97},{17,49},{2,98},{18,50},{3,99},{19,51},{4,100... | collective-permute-start | bytes 1179656 | tf_op jit(solution)/shard_map/ppermute | solution.py:60
  48.8 8.1 %collective-permute-start.9 = (bf16[256,256]{1,0:T(8,128)(2,1)S(1)}, bf16[256,256]{1,0:T(8,128)(2,1)S(1)}, u32[]{:S(2)}, u32[]{:S(2)}) collective-permute-start(bf16[256,256]{1,0:T(8,128)(2,1)S(1)} %add_add_fusion.3), channel_id=1, source_target_pairs={{0,16},{1,17},{2,18},{3,19},{4,20},{5,21},{6,22},{7,23},{8,24},{9,... | collective-permute-start | bytes 393224 | tf_op jit(solution)/shard_map/ppermute | solution.py:60
  52.7 7.5 %collective-permute-start.19 = (bf16[768,256]{1,0:T(8,128)(2,1)S(1)}, bf16[768,256]{1,0:T(8,128)(2,1)S(1)}, u32[]{:S(2)}, u32[]{:S(2)}) collective-permute-start(bf16[768,256]{1,0:T(8,128)(2,1)S(1)} %add.79), channel_id=1, source_target_pairs={{0,32},{16,112},{1,33},{17,113},{2,34},{18,114},{3,35},{19,115},{4... | collective-permute-start | bytes 1179656 | tf_op jit(solution)/shard_map/ppermute | solution.py:60
  57.0 20.4 %collective-permute-start.14 = (bf16[1024,256]{1,0:T(8,128)(2,1)S(1)}, bf16[1024,256]{1,0:T(8,128)(2,1)S(1)}, u32[]{:S(2)}, u32[]{:S(2)}) collective-permute-start(bf16[1024,256]{1,0:T(8,128)(2,1)S(1)} %pad_maximum_fusion.mine), channel_id=1, source_target_pairs={{0,1},{1,0},{2,3},{3,2},{4,5},{5,4},{6,7},{7,6},{8,9},{9,8},{10,11... | collective-permute-start | bytes 1572872 | tf_op jit(solution)/shard_map/ppermute | solution.py:60
  60.4 21.1 %collective-permute-start.21 = (bf16[512,256]{1,0:T(8,128)(2,1)S(1)}, bf16[512,256]{1,0:T(8,128)(2,1)S(1)}, u32[]{:S(2)}, u32[]{:S(2)}) collective-permute-start(bf16[512,256]{1,0:T(8,128)(2,1)S(1)} %slice.9), channel_id=1, source_target_pairs={{16,0},{17,1},{18,2},{19,3},{20,4},{21,5},{22,6},{23,7},{24,8},{25... | collective-permute-start | bytes 786440 | tf_op jit(solution)/shard_map/ppermute | solution.py:60
  75.4 9.5 %collective-permute-start.20 = (bf16[512,256]{1,0:T(8,128)(2,1)S(1)}, bf16[512,256]{1,0:T(8,128)(2,1)S(1)}, u32[]{:S(2)}, u32[]{:S(2)}) collective-permute-start(bf16[512,256]{1,0:T(8,128)(2,1)S(1)} %pad_maximum_fusion.1), channel_id=1, source_target_pairs={{0,16},{1,17},{2,18},{3,19},{4,20},{5,21},{6,22},{7,23},{8,24},{9,... | collective-permute-start | bytes 786440 | tf_op jit(solution)/shard_map/ppermute | solution.py:60

commit v5 on v4

--- a/solution.py
+++ b/solution.py
@@ -42,6 +42,11 @@
     [plane_pairs([((0, 0), h)]) for h in ((2, 6), (1, 0), (3, 0))],
     [plane_pairs([((0, 0), (0, 6)), ((1, 0), (1, 6)), ((3, 0), (3, 6)), ((2, 6), (2, 0))])],
     [plane_pairs([((x, 0), (x, 2)) for x in range(X)] + [((x, 6), (x, 4)) for x in range(X)])],
+]
+SPREAD_REST = [
+    [plane_pairs([((0, 0), (x, 0))]) for x in (2, 1, 3)],
+    [plane_pairs([((x, 0), (x, 6)) for x in range(X)])],
+    SPREAD[2],
 ]
 UP = [
     (device(x, y, z, c), device(x, y + 1, z, c))
@@ -325,11 +330,12 @@
         for level, letter in zip(levels, "abc"):
             source = value if letter == "a" else held
             for pairs in level:
-                held = held + send(source, pairs)
+                came = send(source, pairs)
+                held = held + came
         return held
 
     first_held = tree(first, prow <= 1, SPREAD)
-    rest_held = tree(rest, prow <= 1, SPREAD)
+    rest_held = tree(rest, prow <= 1, SPREAD_REST)
     down_came = send(rest_held[: 2 * BLK], DOWN)
     up_came = send(jnp.concatenate([first_held, rest_held[2 * BLK :]], axis=0), UP)
     panel = tree(panel, pcol <= 1, [LINE_1, LINE_2])

time: 90.4 us -> 94.5 us (1.045)
  the two profiles are of different devices: /device:TPU:2 before, /device:TPU:44 now
where the time goes in v5:
time: 94.5 us; the launch traced here: 93.9 us
  starting transfers between devices  49.7 us (53%)
  waiting for transfers between devices  31.5 us (33%)
  Pallas kernels  11.2 us (12%)
  other arithmetic  1.11 us (1%)
    ppermute x22, starting transfers between devices, send(): return lax.ppermute(value, AXES, pairs)  49.7 us
    ppermute x22, waiting for transfers between devices, send(): return lax.ppermute(value, AXES, pairs)  31.5 us
    pallas_call x1, Pallas kernels, update(): pl.pallas_call(update_kernel, grid=(row_blocks,), in_specs=[smem] * 3 + [...  5.01 us
    pallas_call x1, Pallas kernels, panels(): pl.pallas_call(panels_kernel, in_specs=[smem, smem] + [vmem] * 2, out_spe...  4.11 us
    pallas_call x1, Pallas kernels, pack(): pl.pallas_call(pack_kernel, in_specs=[smem, smem, smem, pl.BlockSpec(memo...  2.06 us
  transfers between devices with their start and end apart: 22, of which 7 were waited for; matrix products, arithmetic and copies ran while one was open for 1% of the time, Pallas kernels for 4%

profile of v5, /device:TPU:44, one launch (start us, length us, event | category | flops | bytes accessed | tf_op | source)
XLA Modules:
  0.0 93.9 jit_solution(3003004399606122176)
XLA Ops:
  0.5 2.1 %pack.1 = (bf16[256,256]{1,0:T(8,128)(2,1)S(1)}, bf16[768,256]{1,0:T(8,128)(2,1)S(1)}, bf16[512,256]{1,0:T(8,128)(2,1)S(1)}) custom-call(s32[2]{0:T(128)} %compare_select_fusion.here, s32[2,96]{1,0:T(2,128)} %row_pattern.5, s32[2,96]{1,0:T(2,128)} %col_pattern.3, bf16[768,1536]{1,0:T(8,128)(2,1)} %source.1), custom_call_target="tpu_custom_call" | custom-call | tf_op jit(solution)/shard_map/pack/pallas_call | solution.py:115
  2.6 0.7 collective-permute-start.2
  3.3 0.7 collective-permute-start.1
  3.9 0.7 collective-permute-start
  4.7 0.7 collective-permute-start.3
  5.4 10.9 %collective-permute-start.11 = (bf16[512,256]{1,0:T(8,128)(2,1)S(1)}, bf16[512,256]{1,0:T(8,128)(2,1)S(1)}, u32[]{:S(2)}, u32[]{:S(2)}) collective-permute-start(bf16[512,256]{1,0:T(8,128)(2,1)S(1)} %get-tuple-element.11), channel_id=1, source_target_pairs={{0,10},{1,11},{16,26},{17,27},{32,42},{33,43},{48,58},{49,59},{64,... | collective-permute-start | bytes 786440 | tf_op jit(solution)/shard_map/ppermute | solution.py:65
  16.3 1.3 %collective-permute-start.10 = (bf16[512,256]{1,0:T(8,128)(2,1)S(1)}, bf16[512,256]{1,0:T(8,128)(2,1)S(1)}, u32[]{:S(2)}, u32[]{:S(2)}) collective-permute-start(bf16[512,256]{1,0:T(8,128)(2,1)S(1)} %get-tuple-element.11), channel_id=1, source_target_pairs={{0,6},{1,7},{16,22},{17,23},{32,38},{33,39},{48,54},{49,55},{64,70... | collective-permute-start | bytes 786440 | tf_op jit(solution)/shard_map/ppermute | solution.py:65
  17.7 1.3 %collective-permute-start.4 = (bf16[256,256]{1,0:T(8,128)(2,1)S(1)}, bf16[256,256]{1,0:T(8,128)(2,1)S(1)}, u32[]{:S(2)}, u32[]{:S(2)}) collective-permute-start(bf16[256,256]{1,0:T(8,128)(2,1)S(1)} %add.66), channel_id=1, source_target_pairs={{0,32},{16,112},{1,33},{17,113},{2,34},{18,114},{3,35},{19,115},{4... | collective-permute-start | bytes 393224 | tf_op jit(solution)/shard_map/ppermute | solution.py:65
  19.0 0.7 collective-permute-start.17
  19.7 0.7 collective-permute-start.16
  20.4 13.0 %collective-permute-done.4 = bf16[256,256]{1,0:T(8,128)(2,1)S(1)} collective-permute-done((bf16[256,256]{1,0:T(8,128)(2,1)S(1)}, bf16[256,256]{1,0:T(8,128)(2,1)S(1)}, u32[]{:S(2)}, u32[]{:S(2)}) %collective-permute-start.4) | collective-permute-done | bytes 131104 | tf_op jit(solution)/shard_map/ppermute | solution.py:65
  33.4 0.7 collective-permute-start.15
  34.2 1.3 %collective-permute-start.6 = (bf16[256,256]{1,0:T(8,128)(2,1)S(1)}, bf16[256,256]{1,0:T(8,128)(2,1)S(1)}, u32[]{:S(2)}, u32[]{:S(2)}) collective-permute-start(bf16[256,256]{1,0:T(8,128)(2,1)S(1)} %add.67.first_held), channel_id=1, source_target_pairs={{0,10},{1,11},{16,26},{17,27},{32,42},{33,43},{48,58},{49,59},{64,... | collective-permute-start | bytes 393224 | tf_op jit(solution)/shard_map/ppermute | solution.py:65
  35.5 1.3 %collective-permute-start.5 = (bf16[256,256]{1,0:T(8,128)(2,1)S(1)}, bf16[256,256]{1,0:T(8,128)(2,1)S(1)}, u32[]{:S(2)}, u32[]{:S(2)}) collective-permute-start(bf16[256,256]{1,0:T(8,128)(2,1)S(1)} %add.67.first_held), channel_id=1, source_target_pairs={{0,6},{1,7},{16,22},{17,23},{32,38},{33,39},{48,54},{49,55},{64,70... | collective-permute-start | bytes 393224 | tf_op jit(solution)/shard_map/ppermute | solution.py:65
  36.9 2.2 %collective-permute-done.6 = bf16[256,256]{1,0:T(8,128)(2,1)S(1)} collective-permute-done((bf16[256,256]{1,0:T(8,128)(2,1)S(1)}, bf16[256,256]{1,0:T(8,128)(2,1)S(1)}, u32[]{:S(2)}, u32[]{:S(2)}) %collective-permute-start.6) | collective-permute-done | bytes 131104 | tf_op jit(solution)/shard_map/ppermute | solution.py:65
  39.0 1.3 %collective-permute-start.13 = (bf16[512,256]{1,0:T(8,128)(2,1)S(1)}, bf16[512,256]{1,0:T(8,128)(2,1)S(1)}, u32[]{:S(2)}, u32[]{:S(2)}) collective-permute-start(bf16[512,256]{1,0:T(8,128)(2,1)S(1)} %add_add_fusion.2), channel_id=1, source_target_pairs={{0,14},{1,15},{16,30},{17,31},{32,46},{33,47},{48,62},{49,63},{64,... | collective-permute-start | bytes 786440 | tf_op jit(solution)/shard_map/ppermute | solution.py:65
  40.3 1.3 %collective-permute-start.12 = (bf16[512,256]{1,0:T(8,128)(2,1)S(1)}, bf16[512,256]{1,0:T(8,128)(2,1)S(1)}, u32[]{:S(2)}, u32[]{:S(2)}) collective-permute-start(bf16[512,256]{1,0:T(8,128)(2,1)S(1)} %add_add_fusion.2), channel_id=1, source_target_pairs={{0,2},{1,3},{16,18},{17,19},{32,34},{33,35},{48,50},{49,51},{64,66... | collective-permute-start | bytes 786440 | tf_op jit(solution)/shard_map/ppermute | solution.py:65
  41.7 1.3 %collective-permute-start.8 = (bf16[256,256]{1,0:T(8,128)(2,1)S(1)}, bf16[256,256]{1,0:T(8,128)(2,1)S(1)}, u32[]{:S(2)}, u32[]{:S(2)}) collective-permute-start(bf16[256,256]{1,0:T(8,128)(2,1)S(1)} %add_add_fusion.4), channel_id=1, source_target_pairs={{0,14},{1,15},{16,30},{17,31},{32,46},{33,47},{48,62},{49,63},{64,... | collective-permute-start | bytes 393224 | tf_op jit(solution)/shard_map/ppermute | solution.py:65
  43.0 1.3 %collective-permute-start.7 = (bf16[256,256]{1,0:T(8,128)(2,1)S(1)}, bf16[256,256]{1,0:T(8,128)(2,1)S(1)}, u32[]{:S(2)}, u32[]{:S(2)}) collective-permute-start(bf16[256,256]{1,0:T(8,128)(2,1)S(1)} %add_add_fusion.4), channel_id=1, source_target_pairs={{0,2},{1,3},{16,18},{17,19},{32,34},{33,35},{48,50},{49,51},{64,66... | collective-permute-start | bytes 393224 | tf_op jit(solution)/shard_map/ppermute | solution.py:65
  44.4 0.7 collective-permute-start.18
  45.1 1.3 %collective-permute-done.8 = bf16[256,256]{1,0:T(8,128)(2,1)S(1)} collective-permute-done((bf16[256,256]{1,0:T(8,128)(2,1)S(1)}, bf16[256,256]{1,0:T(8,128)(2,1)S(1)}, u32[]{:S(2)}, u32[]{:S(2)}) %collective-permute-start.8) | collective-permute-done | bytes 131104 | tf_op jit(solution)/shard_map/ppermute | solution.py:65
  46.4 1.3 %collective-permute-done.7 = bf16[256,256]{1,0:T(8,128)(2,1)S(1)} collective-permute-done((bf16[256,256]{1,0:T(8,128)(2,1)S(1)}, bf16[256,256]{1,0:T(8,128)(2,1)S(1)}, u32[]{:S(2)}, u32[]{:S(2)}) %collective-permute-start.7) | collective-permute-done | bytes 131104 | tf_op jit(solution)/shard_map/ppermute | solution.py:65
  47.7 6.8 %collective-permute-start.9 = (bf16[256,256]{1,0:T(8,128)(2,1)S(1)}, bf16[256,256]{1,0:T(8,128)(2,1)S(1)}, u32[]{:S(2)}, u32[]{:S(2)}) collective-permute-start(bf16[256,256]{1,0:T(8,128)(2,1)S(1)} %add_add_fusion.3), channel_id=1, source_target_pairs={{0,16},{1,17},{2,18},{3,19},{4,20},{5,21},{6,22},{7,23},{8,24},{9,... | collective-permute-start | bytes 393224 | tf_op jit(solution)/shard_map/ppermute | solution.py:65
  54.8 1.3 %collective-permute-start.19 = (bf16[768,256]{1,0:T(8,128)(2,1)S(1)}, bf16[768,256]{1,0:T(8,128)(2,1)S(1)}, u32[]{:S(2)}, u32[]{:S(2)}) collective-permute-start(bf16[768,256]{1,0:T(8,128)(2,1)S(1)} %add.79), channel_id=1, source_target_pairs={{0,32},{16,112},{1,33},{17,113},{2,34},{18,114},{3,35},{19,115},{4... | collective-permute-start | bytes 1179656 | tf_op jit(solution)/shard_map/ppermute | solution.py:65
  56.1 1.0 %collective-permute-done.9 = bf16[256,256]{1,0:T(8,128)(2,1)S(1)} collective-permute-done((bf16[256,256]{1,0:T(8,128)(2,1)S(1)}, bf16[256,256]{1,0:T(8,128)(2,1)S(1)}, u32[]{:S(2)}, u32[]{:S(2)}) %collective-permute-start.9) | collective-permute-done | bytes 131104 | tf_op jit(solution)/shard_map/ppermute | solution.py:65
  57.1 1.9 %collective-permute-start.14 = (bf16[1024,256]{1,0:T(8,128)(2,1)S(1)}, bf16[1024,256]{1,0:T(8,128)(2,1)S(1)}, u32[]{:S(2)}, u32[]{:S(2)}) collective-permute-start(bf16[1024,256]{1,0:T(8,128)(2,1)S(1)} %pad_maximum_fusion.mine), channel_id=1, source_target_pairs={{0,1},{1,0},{2,3},{3,2},{4,5},{5,4},{6,7},{7,6},{8,9},{9,8},{10,11... | collective-permute-start | bytes 1572872 | tf_op jit(solution)/shard_map/ppermute | solution.py:65
  59.1 10.4 %collective-permute-done.19 = bf16[768,256]{1,0:T(8,128)(2,1)S(1)} collective-permute-done((bf16[768,256]{1,0:T(8,128)(2,1)S(1)}, bf16[768,256]{1,0:T(8,128)(2,1)S(1)}, u32[]{:S(2)}, u32[]{:S(2)}) %collective-permute-start.19) | collective-permute-done | bytes 393248 | tf_op jit(solution)/shard_map/ppermute | solution.py:65
  69.7 10.9 %collective-permute-start.21 = (bf16[512,256]{1,0:T(8,128)(2,1)S(1)}, bf16[512,256]{1,0:T(8,128)(2,1)S(1)}, u32[]{:S(2)}, u32[]{:S(2)}) collective-permute-start(bf16[512,256]{1,0:T(8,128)(2,1)S(1)} %slice.9), channel_id=1, source_target_pairs={{16,0},{17,1},{18,2},{19,3},{20,4},{21,5},{22,6},{23,7},{24,8},{25... | collective-permute-start | bytes 786440 | tf_op jit(solution)/shard_map/ppermute | solution.py:65
  80.6 1.9 %collective-permute-start.20 = (bf16[512,256]{1,0:T(8,128)(2,1)S(1)}, bf16[512,256]{1,0:T(8,128)(2,1)S(1)}, u32[]{:S(2)}, u32[]{:S(2)}) collective-permute-start(bf16[512,256]{1,0:T(8,128)(2,1)S(1)} %pad_maximum_fusion.1), channel_id=1, source_target_pairs={{0,16},{1,17},{2,18},{3,19},{4,20},{5,21},{6,22},{7,23},{8,24},{9,... | collective-permute-start | bytes 786440 | tf_op jit(solution)/shard_map/ppermute | solution.py:65
  82.5 4.1 %panels.1 = (bf16[512,256]{1,0:T(8,128)(2,1)S(1)}, bf16[512,256]{1,0:T(8,128)(2,1)S(1)}) custom-call(s32[2]{0:T(128)} %compare_select_fusion.here, s32[2,96]{1,0:T(2,128)} %row_pattern.5, bf16[1024,256]{1,0:T(8,128)(2,1)S(1)} %pad_maximum_fusion.mine, bf16[1024,256]{1,0:T(8,128)(2,1)S(1)} %collective-permute-done.14.other), custom_call_target="tpu_custom_call" | custom-call | flops 2013265920 | bytes 1572864 | tf_op jit(solution)/shard_map/panels/pallas_call | solution.py:207
  86.7 2.2 %collective-permute-done.20.up_came = bf16[512,256]{1,0:T(8,128)(2,1)S(1)} collective-permute-done((bf16[512,256]{1,0:T(8,128)(2,1)S(1)}, bf16[512,256]{1,0:T(8,128)(2,1)S(1)}, u32[]{:S(2)}, u32[]{:S(2)}) %collective-permute-start.20) | collective-permute-done | bytes 262176 | tf_op jit(solution)/shard_map/ppermute | solution.py:65
  88.9 5.0 %update.1 = bf16[768,1536]{1,0:T(8,128)(2,1)} custom-call(s32[2]{0:T(128)} %compare_select_fusion.here, s32[2,96]{1,0:T(2,128)} %row_pattern.5, s32[2,96]{1,0:T(2,128)} %col_pattern.3, bf16[768,1536]{1,0:T(8,128)(2,1)} %source.1, bf16[512,256]{1,0:T(8,128)(2,1)S(1)} %get-tuple-element.12.lower_0, bf16[512,256]{1,0:T(8,128)(2,1)S(1)} %get-tuple-element.13.lower_1, ...), custom_call_target="tpu_custom_call" | custom-call | tf_op jit(solution)/shard_map/update/pallas_call | solution.py:309
  (31 shorter events, 1.2 us)
Async XLA Ops:
  2.6 2.0 %collective-permute-start.2 = (bf16[256,256]{1,0:T(8,128)(2,1)S(1)}, bf16[256,256]{1,0:T(8,128)(2,1)S(1)}, u32[]{:S(2)}, u32[]{:S(2)}) collective-permute-start(bf16[256,256]{1,0:T(8,128)(2,1)S(1)} %get-tuple-element.10), channel_id=1, source_target_pairs={{0,384},{16,400},{1,385},{17,401},{2,386},{18,402},{3,387},{19,403... | collective-permute-start | bytes 393224 | tf_op jit(solution)/shard_map/ppermute | solution.py:65
  3.3 1.4 %collective-permute-start.1 = (bf16[256,256]{1,0:T(8,128)(2,1)S(1)}, bf16[256,256]{1,0:T(8,128)(2,1)S(1)}, u32[]{:S(2)}, u32[]{:S(2)}) collective-permute-start(bf16[256,256]{1,0:T(8,128)(2,1)S(1)} %get-tuple-element.10), channel_id=1, source_target_pairs={{0,128},{16,144},{1,129},{17,145},{2,130},{18,146},{3,131},{19,147... | collective-permute-start | bytes 393224 | tf_op jit(solution)/shard_map/ppermute | solution.py:65
  3.9 0.7 collective-permute-start
  4.7 12.9 %collective-permute-start.3 = (bf16[256,256]{1,0:T(8,128)(2,1)S(1)}, bf16[256,256]{1,0:T(8,128)(2,1)S(1)}, u32[]{:S(2)}, u32[]{:S(2)}) collective-permute-start(bf16[256,256]{1,0:T(8,128)(2,1)S(1)} %add_add_fusion.5), channel_id=1, source_target_pairs={{0,96},{16,48},{1,97},{17,49},{2,98},{18,50},{3,99},{19,51},{4,100... | collective-permute-start | bytes 393224 | tf_op jit(solution)/shard_map/ppermute | solution.py:65
  5.4 28.8 %collective-permute-start.11 = (bf16[512,256]{1,0:T(8,128)(2,1)S(1)}, bf16[512,256]{1,0:T(8,128)(2,1)S(1)}, u32[]{:S(2)}, u32[]{:S(2)}) collective-permute-start(bf16[512,256]{1,0:T(8,128)(2,1)S(1)} %get-tuple-element.11), channel_id=1, source_target_pairs={{0,10},{1,11},{16,26},{17,27},{32,42},{33,43},{48,58},{49,59},{64,... | collective-permute-start | bytes 786440 | tf_op jit(solution)/shard_map/ppermute | solution.py:65
  16.3 19.2 %collective-permute-start.10 = (bf16[512,256]{1,0:T(8,128)(2,1)S(1)}, bf16[512,256]{1,0:T(8,128)(2,1)S(1)}, u32[]{:S(2)}, u32[]{:S(2)}) collective-permute-start(bf16[512,256]{1,0:T(8,128)(2,1)S(1)} %get-tuple-element.11), channel_id=1, source_target_pairs={{0,6},{1,7},{16,22},{17,23},{32,38},{33,39},{48,54},{49,55},{64,70... | collective-permute-start | bytes 786440 | tf_op jit(solution)/shard_map/ppermute | solution.py:65
  17.7 15.8 %collective-permute-start.4 = (bf16[256,256]{1,0:T(8,128)(2,1)S(1)}, bf16[256,256]{1,0:T(8,128)(2,1)S(1)}, u32[]{:S(2)}, u32[]{:S(2)}) collective-permute-start(bf16[256,256]{1,0:T(8,128)(2,1)S(1)} %add.66), channel_id=1, source_target_pairs={{0,32},{16,112},{1,33},{17,113},{2,34},{18,114},{3,35},{19,115},{4... | collective-permute-start | bytes 393224 | tf_op jit(solution)/shard_map/ppermute | solution.py:65
  19.0 22.7 %collective-permute-start.17 = (bf16[768,256]{1,0:T(8,128)(2,1)S(1)}, bf16[768,256]{1,0:T(8,128)(2,1)S(1)}, u32[]{:S(2)}, u32[]{:S(2)}) collective-permute-start(bf16[768,256]{1,0:T(8,128)(2,1)S(1)} %get-tuple-element.14), channel_id=1, source_target_pairs={{0,384},{16,400},{1,385},{17,401},{2,386},{18,402},{3,387},{19,403... | collective-permute-start | bytes 1179656 | tf_op jit(solution)/shard_map/ppermute | solution.py:65
  19.7 23.3 %collective-permute-start.16 = (bf16[768,256]{1,0:T(8,128)(2,1)S(1)}, bf16[768,256]{1,0:T(8,128)(2,1)S(1)}, u32[]{:S(2)}, u32[]{:S(2)}) collective-permute-start(bf16[768,256]{1,0:T(8,128)(2,1)S(1)} %get-tuple-element.14), channel_id=1, source_target_pairs={{0,128},{16,144},{1,129},{17,145},{2,130},{18,146},{3,131},{19,147... | collective-permute-start | bytes 1179656 | tf_op jit(solution)/shard_map/ppermute | solution.py:65
  33.4 10.9 %collective-permute-start.15 = (bf16[768,256]{1,0:T(8,128)(2,1)S(1)}, bf16[768,256]{1,0:T(8,128)(2,1)S(1)}, u32[]{:S(2)}, u32[]{:S(2)}) collective-permute-start(bf16[768,256]{1,0:T(8,128)(2,1)S(1)} %get-tuple-element.14), channel_id=1, source_target_pairs={{0,256},{16,272},{1,257},{17,273},{2,258},{18,274},{3,259},{19,275... | collective-permute-start | bytes 1179656 | tf_op jit(solution)/shard_map/ppermute | solution.py:65
  34.2 4.8 %collective-permute-start.6 = (bf16[256,256]{1,0:T(8,128)(2,1)S(1)}, bf16[256,256]{1,0:T(8,128)(2,1)S(1)}, u32[]{:S(2)}, u32[]{:S(2)}) collective-permute-start(bf16[256,256]{1,0:T(8,128)(2,1)S(1)} %add.67.first_held), channel_id=1, source_target_pairs={{0,10},{1,11},{16,26},{17,27},{32,42},{33,43},{48,58},{49,59},{64,... | collective-permute-start | bytes 393224 | tf_op jit(solution)/shard_map/ppermute | solution.py:65
  35.5 4.8 %collective-permute-start.5 = (bf16[256,256]{1,0:T(8,128)(2,1)S(1)}, bf16[256,256]{1,0:T(8,128)(2,1)S(1)}, u32[]{:S(2)}, u32[]{:S(2)}) collective-permute-start(bf16[256,256]{1,0:T(8,128)(2,1)S(1)} %add.67.first_held), channel_id=1, source_target_pairs={{0,6},{1,7},{16,22},{17,23},{32,38},{33,39},{48,54},{49,55},{64,70... | collective-permute-start | bytes 393224 | tf_op jit(solution)/shard_map/ppermute | solution.py:65
  39.0 15.5 %collective-permute-start.13 = (bf16[512,256]{1,0:T(8,128)(2,1)S(1)}, bf16[512,256]{1,0:T(8,128)(2,1)S(1)}, u32[]{:S(2)}, u32[]{:S(2)}) collective-permute-start(bf16[512,256]{1,0:T(8,128)(2,1)S(1)} %add_add_fusion.2), channel_id=1, source_target_pairs={{0,14},{1,15},{16,30},{17,31},{32,46},{33,47},{48,62},{49,63},{64,... | collective-permute-start | bytes 786440 | tf_op jit(solution)/shard_map/ppermute | solution.py:65
  40.3 14.2 %collective-permute-start.12 = (bf16[512,256]{1,0:T(8,128)(2,1)S(1)}, bf16[512,256]{1,0:T(8,128)(2,1)S(1)}, u32[]{:S(2)}, u32[]{:S(2)}) collective-permute-start(bf16[512,256]{1,0:T(8,128)(2,1)S(1)} %add_add_fusion.2), channel_id=1, source_target_pairs={{0,2},{1,3},{16,18},{17,19},{32,34},{33,35},{48,50},{49,51},{64,66... | collective-permute-start | bytes 786440 | tf_op jit(solution)/shard_map/ppermute | solution.py:65
  41.7 4.7 %collective-permute-start.8 = (bf16[256,256]{1,0:T(8,128)(2,1)S(1)}, bf16[256,256]{1,0:T(8,128)(2,1)S(1)}, u32[]{:S(2)}, u32[]{:S(2)}) collective-permute-start(bf16[256,256]{1,0:T(8,128)(2,1)S(1)} %add_add_fusion.4), channel_id=1, source_target_pairs={{0,14},{1,15},{16,30},{17,31},{32,46},{33,47},{48,62},{49,63},{64,... | collective-permute-start | bytes 393224 | tf_op jit(solution)/shard_map/ppermute | solution.py:65
  43.0 4.7 %collective-permute-start.7 = (bf16[256,256]{1,0:T(8,128)(2,1)S(1)}, bf16[256,256]{1,0:T(8,128)(2,1)S(1)}, u32[]{:S(2)}, u32[]{:S(2)}) collective-permute-start(bf16[256,256]{1,0:T(8,128)(2,1)S(1)} %add_add_fusion.4), channel_id=1, source_target_pairs={{0,2},{1,3},{16,18},{17,19},{32,34},{33,35},{48,50},{49,51},{64,66... | collective-permute-start | bytes 393224 | tf_op jit(solution)/shard_map/ppermute | solution.py:65
  44.4 10.2 %collective-permute-start.18 = (bf16[768,256]{1,0:T(8,128)(2,1)S(1)}, bf16[768,256]{1,0:T(8,128)(2,1)S(1)}, u32[]{:S(2)}, u32[]{:S(2)}) collective-permute-start(bf16[768,256]{1,0:T(8,128)(2,1)S(1)} %add_add_fusion), channel_id=1, source_target_pairs={{0,96},{16,48},{1,97},{17,49},{2,98},{18,50},{3,99},{19,51},{4,100... | collective-permute-start | bytes 1179656 | tf_op jit(solution)/shard_map/ppermute | solution.py:65
  47.7 9.4 %collective-permute-start.9 = (bf16[256,256]{1,0:T(8,128)(2,1)S(1)}, bf16[256,256]{1,0:T(8,128)(2,1)S(1)}, u32[]{:S(2)}, u32[]{:S(2)}) collective-permute-start(bf16[256,256]{1,0:T(8,128)(2,1)S(1)} %add_add_fusion.3), channel_id=1, source_target_pairs={{0,16},{1,17},{2,18},{3,19},{4,20},{5,21},{6,22},{7,23},{8,24},{9,... | collective-permute-start | bytes 393224 | tf_op jit(solution)/shard_map/ppermute | solution.py:65
  54.8 14.7 %collective-permute-start.19 = (bf16[768,256]{1,0:T(8,128)(2,1)S(1)}, bf16[768,256]{1,0:T(8,128)(2,1)S(1)}, u32[]{:S(2)}, u32[]{:S(2)}) collective-permute-start(bf16[768,256]{1,0:T(8,128)(2,1)S(1)} %add.79), channel_id=1, source_target_pairs={{0,32},{16,112},{1,33},{17,113},{2,34},{18,114},{3,35},{19,115},{4... | collective-permute-start | bytes 1179656 | tf_op jit(solution)/shard_map/ppermute | solution.py:65
  57.1 25.4 %collective-permute-start.14 = (bf16[1024,256]{1,0:T(8,128)(2,1)S(1)}, bf16[1024,256]{1,0:T(8,128)(2,1)S(1)}, u32[]{:S(2)}, u32[]{:S(2)}) collective-permute-start(bf16[1024,256]{1,0:T(8,128)(2,1)S(1)} %pad_maximum_fusion.mine), channel_id=1, source_target_pairs={{0,1},{1,0},{2,3},{3,2},{4,5},{5,4},{6,7},{7,6},{8,9},{9,8},{10,11... | collective-permute-start | bytes 1572872 | tf_op jit(solution)/shard_map/ppermute | solution.py:65
  69.7 17.0 %collective-permute-start.21 = (bf16[512,256]{1,0:T(8,128)(2,1)S(1)}, bf16[512,256]{1,0:T(8,128)(2,1)S(1)}, u32[]{:S(2)}, u32[]{:S(2)}) collective-permute-start(bf16[512,256]{1,0:T(8,128)(2,1)S(1)} %slice.9), channel_id=1, source_target_pairs={{16,0},{17,1},{18,2},{19,3},{20,4},{21,5},{22,6},{23,7},{24,8},{25... | collective-permute-start | bytes 786440 | tf_op jit(solution)/shard_map/ppermute | solution.py:65
  80.6 8.3 %collective-permute-start.20 = (bf16[512,256]{1,0:T(8,128)(2,1)S(1)}, bf16[512,256]{1,0:T(8,128)(2,1)S(1)}, u32[]{:S(2)}, u32[]{:S(2)}) collective-permute-start(bf16[512,256]{1,0:T(8,128)(2,1)S(1)} %pad_maximum_fusion.1), channel_id=1, source_target_pairs={{0,16},{1,17},{2,18},{3,19},{4,20},{5,21},{6,22},{7,23},{8,24},{9,... | collective-permute-start | bytes 786440 | tf_op jit(solution)/shard_map/ppermute | solution.py:65
